TPU v7x, 32 devices: a whole 2x2x4 slice. The times are simulated.
32 devices in a mesh: doc: 8 (over y, x, core), seq: 4 (over z).
Axes of the slice: x: 2, y: 2, z: 4, core: 2. Of those that a mesh axis runs over, the one named last changes fastest.
Arguments:
- tokens: bfloat16 [8, 2048, 1024], P('doc', 'seq'), may hold values from -6 to 6
- w_query: bfloat16 [1024, 1024], P(('doc', 'seq')), may hold values from -0.1875 to 0.1875
- w_key: bfloat16 [1024, 1024], P(('doc', 'seq')), may hold values from -0.1875 to 0.1875
- w_value: bfloat16 [1024, 1024], P(('doc', 'seq')), may hold values from -0.1875 to 0.1875
- w_out: bfloat16 [1024, 1024], P(('doc', 'seq')), may hold values from -2 to 2
- w_gate: bfloat16 [1024, 2816], P(('doc', 'seq')), may hold values from -0.1875 to 0.1875
- w_up: bfloat16 [1024, 2816], P(('doc', 'seq')), may hold values from -0.1875 to 0.1875
- w_down: bfloat16 [2816, 1024], P(('doc', 'seq')), may hold values from -0.109375 to 0.109375
- gain_attn: bfloat16 [1024], P(('doc', 'seq')), may hold values from 0.5 to 1.5
- gain_ffn: bfloat16 [1024], P(('doc', 'seq')), may hold values from 0.5 to 1.5
- cache_keys: bfloat16 [8, 512, 1024], P('doc', 'seq'), may hold values from -6 to 6
- cache_values: bfloat16 [8, 512, 1024], P('doc', 'seq'), may hold values from -6 to 6
- memory_flags: int32 [8], P('doc'), may hold values 0 or 1
- memory_source: int32 [8], P('doc'), may hold values from 0 to 7
- positions: int32 [8, 2048], P('doc', 'seq'), may hold values from 0 to 5118, as said below
- out_grad: bfloat16 [8, 2048, 1024], P('doc', 'seq'), may hold values from -6 to 6
Outputs:
- layer_out: bfloat16 [8, 2048, 1024], P('doc', 'seq')
- grad_tokens: float32 [8, 2048, 1024], P('doc', 'seq')
- grad_query: float32 [1024, 1024], P(('doc', 'seq'))
- grad_key: float32 [1024, 1024], P(('doc', 'seq'))
- grad_value: float32 [1024, 1024], P(('doc', 'seq'))
- grad_out: float32 [1024, 1024], P(('doc', 'seq'))
- grad_gate: float32 [1024, 2816], P(('doc', 'seq'))
- grad_up: float32 [1024, 2816], P(('doc', 'seq'))
- grad_down: float32 [2816, 1024], P(('doc', 'seq'))
- grad_gain_attn: float32 [1024], P(('doc', 'seq'))
- grad_gain_ffn: float32 [1024], P(('doc', 'seq'))
Inputs may be any that keep to these rules, and one draw needn't show every extreme that they name: `positions`: within a segment each position is 1 or 2 more than the one before.
All inputs are finite; a program needn't handle non-finite values. No bound on the sum of `memory_flags` on one device may be relied on, other than what follows from the above.
Results may differ from a plain program's by a relative error of at most 0.04.
Values may be sent and summed in bfloat16 or wider, within the bound.
No kernel may reach another device: no remote copies, remote signals or barrier semaphores. Data moves between devices by JAX's collectives and lax.ppermute only.
A program may use at most 256 MiB of HBM per device.

v0:
```python
import math

import jax
import jax.numpy as jnp
from jax import lax
from jax.sharding import PartitionSpec as P

HEADS = 8
HEAD_DIM = 128


EPS_NORM = 1e-05
NEG_FILL = -1e30


def rms_factor(values):
    return lax.rsqrt(jnp.mean(values * values, -1, keepdims=True) + EPS_NORM)


def rotary_tables(token_pos):
    half_dim = HEAD_DIM // 2
    frequency = jnp.exp(
        jnp.arange(half_dim, dtype=jnp.float32) * (-2.0 * math.log(10000.0) / HEAD_DIM)
    )
    angles = token_pos.astype(jnp.float32)[..., None] * frequency
    return (jnp.cos(angles), jnp.sin(angles))


def rotate(values, cos_vals, sin_vals):
    half_dim = values.shape[-1] // 2
    first_half = values[..., :half_dim]
    second_half = values[..., half_dim:]
    cos_b = cos_vals[..., None, :]
    sin_b = sin_vals[..., None, :]
    return jnp.concatenate(
        [first_half * cos_b - second_half * sin_b, second_half * cos_b + first_half * sin_b], -1
    )


def rotate_back(grads, cos_vals, sin_vals):
    half_dim = grads.shape[-1] // 2
    first_half = grads[..., :half_dim]
    second_half = grads[..., half_dim:]
    cos_b = cos_vals[..., None, :]
    sin_b = sin_vals[..., None, :]
    return jnp.concatenate(
        [first_half * cos_b + second_half * sin_b, second_half * cos_b - first_half * sin_b], -1
    )


def online_step(fold_state, scores, allowed, value_heads):
    row_max, row_sum, weighted = fold_state
    masked = jnp.where(allowed, scores, NEG_FILL)
    new_max = jnp.maximum(row_max, jnp.max(masked, -1))
    weights_p = jnp.where(allowed, jnp.exp(scores - new_max[..., None]), 0.0)
    rescale = jnp.exp(row_max - new_max)
    row_sum = row_sum * rescale + jnp.sum(weights_p, -1)
    weighted = weighted * jnp.transpose(rescale, (0, 2, 1))[..., None] + jnp.einsum(
        "shqk,skhd->sqhd",
        weights_p.astype(jnp.bfloat16),
        value_heads,
        preferred_element_type=jnp.float32,
    )
    return (new_max, row_sum, weighted)


def norm_back(d_normed, normed, factor):
    return factor * (d_normed - normed * jnp.mean(d_normed * normed, -1, keepdims=True))


def on_device(
    tokens,
    w_query,
    w_key,
    w_value,
    w_out,
    w_gate,
    w_up,
    w_down,
    gain_attn,
    gain_ffn,
    cache_keys,
    cache_values,
    memory_flags,
    memory_source,
    positions,
    out_grad,
):
    fwd_weights = (
        lax.all_gather(w_query, ("doc", "seq"), axis=0, tiled=True),
        lax.all_gather(w_key, ("doc", "seq"), axis=0, tiled=True),
        lax.all_gather(w_value, ("doc", "seq"), axis=0, tiled=True),
        lax.all_gather(w_out, ("doc", "seq"), axis=0, tiled=True),
        lax.all_gather(w_gate, ("doc", "seq"), axis=0, tiled=True),
        lax.all_gather(w_up, ("doc", "seq"), axis=0, tiled=True),
        lax.all_gather(w_down, ("doc", "seq"), axis=0, tiled=True),
        lax.all_gather(gain_attn, ("doc", "seq"), axis=0, tiled=True),
        lax.all_gather(gain_ffn, ("doc", "seq"), axis=0, tiled=True),
    )
    seg_count, tok_local, model_width = tokens.shape
    ff_width = w_gate.shape[1]
    flat_rows = seg_count * tok_local
    score_scale = 1.0 / math.sqrt(HEAD_DIM)
    total_len = tok_local * lax.axis_size("seq")
    state_shape = (seg_count, HEADS, tok_local)
    head_shape = (seg_count, tok_local, HEADS, HEAD_DIM)
    inputs = tokens.astype(jnp.float32)
    factor_one = rms_factor(inputs)
    normed_one = inputs * factor_one
    attn_in = (normed_one * fwd_weights[7].astype(jnp.float32)).astype(jnp.bfloat16)
    query_f = jnp.dot(attn_in, fwd_weights[0], preferred_element_type=jnp.float32)
    keys_f = jnp.dot(attn_in, fwd_weights[1], preferred_element_type=jnp.float32)
    v_low = jnp.dot(attn_in, fwd_weights[2], preferred_element_type=jnp.float32).astype(
        jnp.bfloat16
    )
    cos_vals, sin_vals = rotary_tables(positions)
    q_heads = query_f.reshape(head_shape)
    q_rot = rotate(q_heads, cos_vals, sin_vals).astype(jnp.bfloat16)
    q_mem = q_heads.astype(jnp.bfloat16)
    k_rot = (
        rotate(keys_f.reshape(head_shape), cos_vals, sin_vals)
        .astype(jnp.bfloat16)
        .reshape(seg_count, tok_local, model_width)
    )
    query_rows = lax.axis_index("seq") * tok_local + jnp.arange(tok_local, dtype=jnp.int32)
    initial = (
        jnp.full(state_shape, NEG_FILL, jnp.float32),
        jnp.zeros(state_shape, jnp.float32),
        jnp.zeros(head_shape, jnp.float32),
    )
    key_part = lax.all_gather(k_rot, "seq", axis=1, tiled=True)
    value_part = lax.all_gather(v_low, "seq", axis=1, tiled=True)
    key_span = key_part.shape[1]
    key_heads = key_part.reshape(seg_count, key_span, HEADS, HEAD_DIM)
    scores = (
        jnp.einsum("sqhd,skhd->shqk", q_rot, key_heads, preferred_element_type=jnp.float32)
        * score_scale
    )
    key_cols = jnp.arange(key_span, dtype=jnp.int32)
    allowed = (key_cols[None, :] <= query_rows[:, None])[None, None]
    fold_state = online_step(
        initial, scores, allowed, value_part.reshape(seg_count, key_span, HEADS, HEAD_DIM)
    )
    every_keys, every_values = (
        lax.all_gather(cache_keys, "doc", axis=0, tiled=True),
        lax.all_gather(cache_values, "doc", axis=0, tiled=True),
    )
    mem_keys = jnp.concatenate([cache_keys, jnp.take(every_keys, memory_source, axis=0)], 1)
    mem_values = jnp.concatenate([cache_values, jnp.take(every_values, memory_source, axis=0)], 1)
    flag_on = (memory_flags > 0)[:, None, None, None]
    key_part = lax.all_gather(mem_keys, "seq", axis=1, tiled=True)
    value_part = lax.all_gather(mem_values, "seq", axis=1, tiled=True)
    key_span = key_part.shape[1]
    key_heads = key_part.reshape(seg_count, key_span, HEADS, HEAD_DIM)
    scores = (
        jnp.einsum("sqhd,skhd->shqk", q_mem, key_heads, preferred_element_type=jnp.float32)
        * score_scale
    )
    row_max, row_sum, weighted = online_step(
        fold_state, scores, flag_on, value_part.reshape(seg_count, key_span, HEADS, HEAD_DIM)
    )
    log_total = row_max + jnp.log(row_sum)
    attended = weighted / jnp.transpose(row_sum, (0, 2, 1))[..., None]
    attn_low = attended.reshape(flat_rows, model_width).astype(jnp.bfloat16)
    resid_mid = inputs.reshape(flat_rows, model_width) + jnp.dot(
        attn_low, fwd_weights[3], preferred_element_type=jnp.float32
    )
    factor_two = rms_factor(resid_mid)
    normed_two = resid_mid * factor_two
    ffn_in = (normed_two * fwd_weights[8].astype(jnp.float32)).astype(jnp.bfloat16)
    gate_act = jnp.dot(ffn_in, fwd_weights[4], preferred_element_type=jnp.float32)
    up_act = jnp.dot(ffn_in, fwd_weights[5], preferred_element_type=jnp.float32)
    sig_gate = jax.nn.sigmoid(gate_act)
    silu_gate = jax.nn.silu(gate_act)
    hidden = (silu_gate * up_act).astype(jnp.bfloat16)
    result = (
        resid_mid + jnp.dot(hidden, fwd_weights[6], preferred_element_type=jnp.float32)
    ).astype(jnp.bfloat16)
    back_weights = (
        lax.all_gather(w_query, ("doc", "seq"), axis=0, tiled=True),
        lax.all_gather(w_key, ("doc", "seq"), axis=0, tiled=True),
        lax.all_gather(w_value, ("doc", "seq"), axis=0, tiled=True),
        lax.all_gather(w_out, ("doc", "seq"), axis=0, tiled=True),
        lax.all_gather(w_gate, ("doc", "seq"), axis=0, tiled=True),
        lax.all_gather(w_up, ("doc", "seq"), axis=0, tiled=True),
        lax.all_gather(w_down, ("doc", "seq"), axis=0, tiled=True),
        lax.all_gather(gain_attn, ("doc", "seq"), axis=0, tiled=True),
        lax.all_gather(gain_ffn, ("doc", "seq"), axis=0, tiled=True),
    )
    grad_y = out_grad.reshape(flat_rows, model_width)
    d_hidden = jnp.einsum("td,fd->tf", grad_y, back_weights[6], preferred_element_type=jnp.float32)
    d_gate = (d_hidden * up_act * (sig_gate * (1.0 + gate_act * (1.0 - sig_gate)))).astype(
        jnp.bfloat16
    )
    d_up = (d_hidden * silu_gate).astype(jnp.bfloat16)
    d_ffn_in = jnp.einsum(
        "tf,df->td", d_gate, back_weights[4], preferred_element_type=jnp.float32
    ) + jnp.einsum("tf,df->td", d_up, back_weights[5], preferred_element_type=jnp.float32)
    g_gain_ffn = jnp.sum(d_ffn_in * normed_two, 0)
    d_mid = grad_y.astype(jnp.float32) + norm_back(
        d_ffn_in * back_weights[8].astype(jnp.float32), normed_two, factor_two
    )
    d_branch = d_mid.astype(jnp.bfloat16)
    d_att = (
        jnp.einsum("te,de->td", d_branch, back_weights[3], preferred_element_type=jnp.float32)
        .astype(jnp.bfloat16)
        .reshape(head_shape)
    )
    delta_rows = jnp.transpose(jnp.sum(d_att.astype(jnp.float32) * attended, -1), (0, 2, 1))
    gathered_keys, gathered_values = (
        lax.all_gather(k_rot, "seq", axis=1, tiled=True),
        lax.all_gather(v_low, "seq", axis=1, tiled=True),
    )
    block_len = min(512, total_len)
    n_blocks = total_len // block_len
    key_blocks = jnp.transpose(
        gathered_keys.reshape(seg_count, n_blocks, block_len, HEADS, HEAD_DIM), (1, 0, 2, 3, 4)
    )
    value_blocks = jnp.transpose(
        gathered_values.reshape(seg_count, n_blocks, block_len, HEADS, HEAD_DIM), (1, 0, 2, 3, 4)
    )

    def block_grads(key_heads, value_heads, block_num):
        scores = (
            jnp.einsum("sqhd,skhd->shqk", q_rot, key_heads, preferred_element_type=jnp.float32)
            * score_scale
        )
        key_cols = block_num * block_len + jnp.arange(block_len, dtype=jnp.int32)
        allowed = (key_cols[None, :] <= query_rows[:, None])[None, None]
        probabilities = jnp.where(allowed, jnp.exp(scores - log_total[..., None]), 0.0)
        d_probs = jnp.einsum(
            "sqhd,skhd->shqk", d_att, value_heads, preferred_element_type=jnp.float32
        )
        d_scores = (probabilities * (d_probs - delta_rows[..., None])).astype(jnp.bfloat16)
        return (probabilities, d_scores)

    def query_step(d_query_acc, block_inputs):
        key_heads, value_heads, block_num = block_inputs
        probabilities, d_scores = block_grads(key_heads, value_heads, block_num)
        return (
            d_query_acc
            + jnp.einsum(
                "shqk,skhd->sqhd", d_scores, key_heads, preferred_element_type=jnp.float32
            ),
            None,
        )

    d_qrot, unused_out = lax.scan(
        query_step,
        jnp.zeros(head_shape, jnp.float32),
        (key_blocks, value_blocks, jnp.arange(n_blocks, dtype=jnp.int32)),
    )
    own_keys = k_rot.reshape(head_shape)
    own_values = v_low.reshape(head_shape)
    lse_rows = jnp.transpose(log_total, (0, 2, 1))
    delta_tok = jnp.transpose(delta_rows, (0, 2, 1))
    q_part = lax.all_gather(q_rot, "seq", axis=1, tiled=True)
    datt_part = lax.all_gather(d_att, "seq", axis=1, tiled=True)
    lse_part = lax.all_gather(lse_rows.astype(jnp.bfloat16), "seq", axis=1, tiled=True).astype(
        jnp.float32
    )
    delta_part = lax.all_gather(delta_tok.astype(jnp.bfloat16), "seq", axis=1, tiled=True).astype(
        jnp.float32
    )
    row_span = q_part.shape[1]
    scores = (
        jnp.einsum("sqhd,skhd->shqk", q_part, own_keys, preferred_element_type=jnp.float32)
        * score_scale
    )
    visit_rows = jnp.arange(row_span, dtype=jnp.int32)
    allowed = (query_rows[None, :] <= visit_rows[:, None])[None, None]
    lse_heads = jnp.transpose(lse_part, (0, 2, 1))
    delta_heads = jnp.transpose(delta_part, (0, 2, 1))
    probabilities = jnp.where(allowed, jnp.exp(scores - lse_heads[..., None]), 0.0)
    d_probs = jnp.einsum(
        "sqhd,skhd->shqk", datt_part, own_values, preferred_element_type=jnp.float32
    )
    d_scores = (probabilities * (d_probs - delta_heads[..., None])).astype(jnp.bfloat16)
    key_acc = jnp.einsum("shqk,sqhd->skhd", d_scores, q_part, preferred_element_type=jnp.float32)
    value_acc = jnp.einsum(
        "shqk,sqhd->skhd",
        probabilities.astype(jnp.bfloat16),
        datt_part,
        preferred_element_type=jnp.float32,
    )
    key_acc, value_acc = (key_acc, value_acc)
    key_sum = key_acc.reshape(seg_count, tok_local, model_width)
    value_sum = value_acc.reshape(seg_count, tok_local, model_width)
    key_part = lax.all_gather(mem_keys, "seq", axis=1, tiled=True)
    value_part = lax.all_gather(mem_values, "seq", axis=1, tiled=True)
    key_span = key_part.shape[1]
    key_heads = key_part.reshape(seg_count, key_span, HEADS, HEAD_DIM)
    value_heads = value_part.reshape(seg_count, key_span, HEADS, HEAD_DIM)
    scores = (
        jnp.einsum("sqhd,skhd->shqk", q_mem, key_heads, preferred_element_type=jnp.float32)
        * score_scale
    )
    probabilities = jnp.where(flag_on, jnp.exp(scores - log_total[..., None]), 0.0)
    d_probs = jnp.einsum("sqhd,skhd->shqk", d_att, value_heads, preferred_element_type=jnp.float32)
    d_scores = (probabilities * (d_probs - delta_rows[..., None])).astype(jnp.bfloat16)
    d_qmem = jnp.einsum("shqk,skhd->sqhd", d_scores, key_heads, preferred_element_type=jnp.float32)
    d_query = (
        ((rotate_back(d_qrot, cos_vals, sin_vals) + d_qmem) * score_scale)
        .astype(jnp.bfloat16)
        .reshape(flat_rows, model_width)
    )
    d_key = (
        (rotate_back(key_sum.reshape(head_shape), cos_vals, sin_vals) * score_scale)
        .astype(jnp.bfloat16)
        .reshape(flat_rows, model_width)
    )
    d_value = value_sum.astype(jnp.bfloat16).reshape(flat_rows, model_width)
    attn_in_flat = attn_in.reshape(flat_rows, model_width)
    d_attn_in = jnp.einsum(
        "te,de->td", d_query, back_weights[0], preferred_element_type=jnp.float32
    )
    d_attn_in = d_attn_in + jnp.einsum(
        "te,de->td", d_key, back_weights[1], preferred_element_type=jnp.float32
    )
    d_attn_in = d_attn_in + jnp.einsum(
        "te,de->td", d_value, back_weights[2], preferred_element_type=jnp.float32
    )
    normed_flat = normed_one.reshape(flat_rows, model_width)
    g_gain_attn = jnp.sum(d_attn_in * normed_flat, 0)
    grad_in = d_mid + norm_back(
        d_attn_in * back_weights[7].astype(jnp.float32),
        normed_flat,
        factor_one.reshape(flat_rows, 1),
    )
    grad_tokens = grad_in.reshape(seg_count, tok_local, model_width)
    gate_part = jnp.einsum("td,tf->df", ffn_in, d_gate, preferred_element_type=jnp.float32)
    up_part = jnp.einsum("td,tf->df", ffn_in, d_up, preferred_element_type=jnp.float32)
    both_parts = lax.psum_scatter(
        jnp.concatenate([gate_part, up_part], 1), ("doc", "seq"), scatter_dimension=0, tiled=True
    )
    down_part = lax.psum_scatter(
        jnp.einsum("tf,td->fd", hidden, grad_y, preferred_element_type=jnp.float32),
        ("doc", "seq"),
        scatter_dimension=0,
        tiled=True,
    )
    query_part = jnp.einsum("td,te->de", attn_in_flat, d_query, preferred_element_type=jnp.float32)
    key_part = jnp.einsum("td,te->de", attn_in_flat, d_key, preferred_element_type=jnp.float32)
    value_part = jnp.einsum("td,te->de", attn_in_flat, d_value, preferred_element_type=jnp.float32)
    out_part = jnp.einsum("td,te->de", attn_low, d_branch, preferred_element_type=jnp.float32)
    attn_sums = lax.psum_scatter(
        jnp.concatenate([query_part, key_part, value_part, out_part], 1),
        ("doc", "seq"),
        scatter_dimension=0,
        tiled=True,
    )
    gain_attn_sum, gain_ffn_sum = (
        lax.psum_scatter(g_gain_attn, ("doc", "seq"), scatter_dimension=0, tiled=True),
        lax.psum_scatter(g_gain_ffn, ("doc", "seq"), scatter_dimension=0, tiled=True),
    )
    layer_out = result.reshape(seg_count, tok_local, model_width)
    return (
        layer_out,
        grad_tokens,
        attn_sums[:, :model_width],
        attn_sums[:, model_width : 2 * model_width],
        attn_sums[:, 2 * model_width : 3 * model_width],
        attn_sums[:, 3 * model_width :],
        both_parts[:, :ff_width],
        both_parts[:, ff_width:],
        down_part,
        gain_attn_sum,
        gain_ffn_sum,
    )


def solution(mesh):
    in_specs = (
        P("doc", "seq", None),
        P(("doc", "seq"), None),
        P(("doc", "seq"), None),
        P(("doc", "seq"), None),
        P(("doc", "seq"), None),
        P(("doc", "seq"), None),
        P(("doc", "seq"), None),
        P(("doc", "seq"), None),
        P(("doc", "seq")),
        P(("doc", "seq")),
        P("doc", "seq", None),
        P("doc", "seq", None),
        P("doc"),
        P("doc"),
        P("doc", "seq"),
        P("doc", "seq", None),
    )
    out_specs = (
        P("doc", "seq", None),
        P("doc", "seq", None),
        P(("doc", "seq"), None),
        P(("doc", "seq"), None),
        P(("doc", "seq"), None),
        P(("doc", "seq"), None),
        P(("doc", "seq"), None),
        P(("doc", "seq"), None),
        P(("doc", "seq"), None),
        P(("doc", "seq")),
        P(("doc", "seq")),
    )
    return jax.shard_map(
        on_device, mesh=mesh, in_specs=in_specs, out_specs=out_specs, check_vma=False
    )
```

profile of v0, /device:TPU:0, one launch (start us, length us, event | category | flops | bytes accessed | tf_op | source)
XLA Modules:
  0.0 2177.2 jit_solution(11208984185066202139)
XLA Ops:
  12.5 28.0 %all-gather.25.cloned.1.call-done = bf16[8,128,1024]{2,1,0:T(8,128)(2,1)} async-done(((bf16[1,128,1024]{2,1,0:T(8,128)(2,1)}), bf16[8,128,1024]{2,1,0:T(8,128)(2,1)}) %all-gather.25.cloned.1.call-update) | async-done | bytes 2097168 | tf_op jit(solution)/shard_map/all_gather | solution.py:145
  42.7 27.7 %all-gather.29.cloned.1.call-done = bf16[8,128,1024]{2,1,0:T(8,128)(2,1)} async-done(((bf16[1,128,1024]{2,1,0:T(8,128)(2,1)}), bf16[8,128,1024]{2,1,0:T(8,128)(2,1)}) %all-gather.29.cloned.1.call-update) | async-done | bytes 2097168 | tf_op jit(solution)/shard_map/all_gather | solution.py:146
  72.8 39.4 %all-reduce.5 = (bf16[1024]{0:T(1024)(128)(2,1)S(1)}, bf16[1024]{0:T(1024)(128)(2,1)S(1)}) all-reduce(bf16[1024]{0:T(1024)(128)(2,1)S(1)} %dynamic-update-slice.1, bf16[1024]{0:T(1024)(128)(2,1)S(1)} %dynamic-update-slice.2), channel_id=1, replica_groups=mesh['doc'=8,'seq'=4] {'doc','seq'}, use_global_device_ids=true, to_apply=%add | all-reduce | flops 2048 | bytes 8192
  113.1 16.8 all-gather.17.cloned.1.call-done
  136.0 52.0 %all-gather.19.cloned.1.call-done = bf16[1024,1024]{1,0:T(8,128)(2,1)} async-done(((bf16[32,1024]{1,0:T(8,128)(2,1)}), bf16[1024,1024]{1,0:T(8,128)(2,1)}) %all-gather.19.cloned.1.call-update) | async-done | bytes 2097168 | tf_op jit(solution)/shard_map/all_gather | solution.py:91
  198.5 47.6 %all-gather.23.cloned.1.call-done = bf16[1024,1024]{1,0:T(8,128)(2,1)} async-done(((bf16[32,1024]{1,0:T(8,128)(2,1)}), bf16[1024,1024]{1,0:T(8,128)(2,1)}) %all-gather.23.cloned.1.call-update) | async-done | bytes 2097168 | tf_op jit(solution)/shard_map/all_gather | solution.py:92
  258.5 34.2 %all-gather.27.cloned.1.call-done = bf16[1,1024,1024]{1,2,0:T(8,128)(2,1)} async-done(((bf16[1,256,1024]{1,2,0:T(8,128)(2,1)}), bf16[1,1024,1024]{1,2,0:T(8,128)(2,1)}) %all-gather.27.cloned.1.call-update) | async-done | bytes 2097168 | tf_op jit(solution)/shard_map/all_gather | solution.py:151
  303.8 34.7 %all-gather.31.cloned.1.call-done = bf16[1,1024,1024]{2,1,0:T(8,128)(2,1)} async-done(((bf16[1,256,1024]{2,1,0:T(8,128)(2,1)}), bf16[1,1024,1024]{2,1,0:T(8,128)(2,1)}) %all-gather.31.cloned.1.call-update) | async-done | bytes 2097168 | tf_op jit(solution)/shard_map/all_gather | solution.py:152
  342.4 77.7 %all-gather.21.cloned.1.call-done = bf16[1,2048,1024]{1,2,0:T(8,128)(2,1)} async-done(((bf16[1,512,1024]{1,2,0:T(8,128)(2,1)}), bf16[1,2048,1024]{1,2,0:T(8,128)(2,1)}) %all-gather.21.cloned.1.call-update) | async-done | bytes 4194320 | tf_op jit(solution)/shard_map/all_gather | solution.py:131
  435.9 65.1 %all-gather.45.cloned.1.call-done = bf16[2048,1024]{1,0:T(8,128)(2,1)} async-done(((bf16[512,1024]{1,0:T(8,128)(2,1)}), bf16[2048,1024]{1,0:T(8,128)(2,1)}) %all-gather.45.cloned.1.call-update) | async-done | bytes 4194320 | tf_op jit(solution)/shard_map/all_gather | solution.py:132
  521.1 15.2 fusion.22
  564.9 18.2 fusion.27
  598.4 41.7 %all-gather.41.cloned.1.call-done = bf16[1,2048,8,128]{1,3,2,0:T(8,128)(2,1)} async-done(((bf16[1,512,8,128]{1,3,2,0:T(8,128)(2,1)}), bf16[1,2048,8,128]{1,3,2,0:T(8,128)(2,1)}) %all-gather.41.cloned.1.call-update) | async-done | bytes 4194320 | tf_op jit(solution)/shard_map/all_gather | solution.py:257
  640.0 15.7 fusion.43
  655.8 52.8 %all-gather.35.cloned.1.call-done = bf16[1024,2816]{1,0:T(8,128)(2,1)} async-done(((bf16[32,2816]{1,0:T(8,128)(2,1)}), bf16[1024,2816]{1,0:T(8,128)(2,1)}) %all-gather.35.cloned.1.call-update) | async-done | bytes 5767184 | tf_op jit(solution)/shard_map/all_gather | solution.py:94
  717.2 60.6 %all-gather.37.cloned.1.call-done = bf16[1024,2816]{1,0:T(8,128)(2,1)} async-done(((bf16[32,2816]{1,0:T(8,128)(2,1)}), bf16[1024,2816]{1,0:T(8,128)(2,1)}) %all-gather.37.cloned.1.call-update) | async-done | bytes 5767184 | tf_op jit(solution)/shard_map/all_gather | solution.py:95
  785.5 61.3 %all-gather.39.cloned.1.call-done = bf16[2816,1024]{1,0:T(8,128)(2,1)} async-done(((bf16[88,1024]{1,0:T(8,128)(2,1)}), bf16[2816,1024]{1,0:T(8,128)(2,1)}) %all-gather.39.cloned.1.call-update) | async-done | bytes 5767184 | tf_op jit(solution)/shard_map/all_gather | solution.py:96
  895.7 74.0 %while.12 = (s32[]{:T(128)}, f32[1,512,8,128]{1,3,2,0:T(8,128)}, bf16[4,1,512,8,128]{4,2,3,1,0:T(8,128)(2,1)}, s32[4]{0:T(128)}, bf16[1,512,8,128]{3,1,2,0:T(8,1...) while((s32[]{:T(128)}, f32[1,512,8,128]{1,3,2,0:T(8,128)}, ...), condition=%wide.region_9.11_spmd.clone, body=%wide.region_8.10_spmd.clone.sunk | while | flops 1624507392 | bytes 28877996 | solution.py:248
  969.8 21.5 fusion.65
  1040.8 17.5 copy.109
  1101.6 43.8 %all-reduce.4 = (f32[1024]{0:T(1024)S(1)}, f32[1024]{0:T(1024)S(1)}) all-reduce(f32[1024]{0:T(1024)S(1)} %get-tuple-element.177, f32[1024]{0:T(1024)S(1)} %copy-done.48), channel_id=6, replica_groups=mesh['doc'=8,'seq'=4] {'doc','seq'}, use_global_device_ids=true, to_apply=%region_15.17.clone | all-reduce | flops 2048 | bytes 16384
  1150.1 273.1 %reduce-scatter.10.cloned.1.call-done = f32[32,4096]{1,0:T(8,128)} async-done(((f32[1024,4096]{1,0:T(8,128)}), f32[32,4096]{1,0:T(8,128)}) %reduce-scatter.10.cloned.1.call-update) | async-done | bytes 524304
  1425.1 492.6 %reduce-scatter.6.cloned.1.call-done = f32[32,5632]{1,0:T(8,128)} async-done(((f32[1024,5632]{1,0:T(8,128)}), f32[32,5632]{1,0:T(8,128)}) %reduce-scatter.6.cloned.1.call-update) | async-done | bytes 720912 | tf_op jit(solution)/shard_map/reduce_scatter | solution.py:333
  1919.7 250.4 %reduce-scatter.8.cloned.1.call-done = f32[88,1024]{1,0:T(8,128)} async-done(((f32[2816,1024]{1,0:T(8,128)}), f32[88,1024]{1,0:T(8,128)}) %reduce-scatter.8.cloned.1.call-update) | async-done | bytes 360464 | tf_op jit(solution)/shard_map/reduce_scatter | solution.py:336
  (266 shorter events, 370.0 us)
Async XLA Ops:
  7.2 33.4 %all-gather.25.cloned.1.call-start = ((), (), s32[]{:S(2)}) async-start(), calls=%async_computation.7 | async-start | bytes 2359296 | tf_op jit(solution)/shard_map/all_gather | solution.py:145
  7.9 62.4 %all-gather.29.cloned.1.call-start = ((), (), s32[]{:S(2)}) async-start(), calls=%async_computation.9 | async-start | bytes 2359296 | tf_op jit(solution)/shard_map/all_gather | solution.py:146
  8.7 121.2 %all-gather.17.cloned.1.call-start = ((), (), s32[]{:S(2)}) async-start(), calls=%async_computation.3 | async-start | bytes 2162688 | tf_op jit(solution)/shard_map/all_gather | solution.py:90
  9.4 178.6 %all-gather.19.cloned.1.call-start = ((), (), s32[]{:S(2)}) async-start(), calls=%async_computation.4 | async-start | bytes 2162688 | tf_op jit(solution)/shard_map/all_gather | solution.py:91
  10.0 236.1 %all-gather.23.cloned.1.call-start = ((), (), s32[]{:S(2)}) async-start(), calls=%async_computation.6 | async-start | bytes 2162688 | tf_op jit(solution)/shard_map/all_gather | solution.py:92
  10.6 101.6 %copy-start.49 = (s32[1,512]{1,0:T(1,128)S(1)}, s32[1,512]{1,0:T(1,128)}, u32[]{:S(2)}) copy-start(s32[1,512]{1,0:T(1,128)} %param.34) | copy-start | bytes 6148
  10.6 101.6 %copy-start.10 = (bf16[1,512,1024]{2,1,0:T(8,128)(2,1)S(1)}, bf16[1,512,1024]{2,1,0:T(8,128)(2,1)}, u32[]{:S(2)}) copy-start(bf16[1,512,1024]{2,1,0:T(8,128)(2,1)} %param.20) | copy-start | bytes 3145732
  10.6 282.0 %all-gather.27.cloned.1.call-start = ((), (), s32[]{:S(2)}) async-start(), calls=%async_computation.8 | async-start | bytes 2621440 | tf_op jit(solution)/shard_map/all_gather | solution.py:151
  42.6 295.8 %all-gather.31.cloned.1.call-start = ((), (), s32[]{:S(2)}) async-start(), calls=%async_computation.10 | async-start | bytes 2621440 | tf_op jit(solution)/shard_map/all_gather | solution.py:152
  72.2 347.9 %all-gather.21.cloned.1.call-start = ((), (), s32[]{:S(2)}) async-start(), calls=%async_computation.5 | async-start | bytes 5242880 | tf_op jit(solution)/shard_map/all_gather | solution.py:131
  112.2 134.0 %copy-start.43 = (f32[1024]{0:T(1024)}, f32[1024]{0:T(1024)S(1)}, u32[]{:S(2)}) copy-start(f32[1024]{0:T(1024)S(1)} %convert_element_type.184) | copy-start | bytes 12292
  112.5 133.6 %copy-start.45 = (f32[512]{0:T(512)}, f32[512]{0:T(512)S(1)}, u32[]{:S(2)}) copy-start(f32[512]{0:T(512)S(1)} %add_rsqrt_fusion.1) | copy-start | bytes 6148
  198.5 302.5 %all-gather.45.cloned.1.call-start = ((), (), s32[]{:S(2)}) async-start(), calls=%async_computation.19 | async-start | bytes 5242880 | tf_op jit(solution)/shard_map/all_gather | solution.py:132
  250.1 343.1 %all-gather.33.cloned.1.call-start = ((), (), s32[]{:S(2)}) async-start(), calls=%async_computation.11 | async-start | bytes 2162688 | tf_op jit(solution)/shard_map/all_gather | solution.py:93
  250.6 389.4 %all-gather.41.cloned.1.call-start = ((), (), s32[]{:S(2)}) async-start(), calls=%async_computation.15 | async-start | bytes 5242880 | tf_op jit(solution)/shard_map/all_gather | solution.py:257
  251.9 456.8 %all-gather.35.cloned.1.call-start = ((), (), s32[]{:S(2)}) async-start(), calls=%async_computation.12 | async-start | bytes 5947392 | tf_op jit(solution)/shard_map/all_gather | solution.py:94
  252.4 525.3 %all-gather.37.cloned.1.call-start = ((), (), s32[]{:S(2)}) async-start(), calls=%async_computation.13 | async-start | bytes 5947392 | tf_op jit(solution)/shard_map/all_gather | solution.py:95
  253.2 593.6 %all-gather.39.cloned.1.call-start = ((), (), s32[]{:S(2)}) async-start(), calls=%async_computation.14 | async-start | bytes 5947392 | tf_op jit(solution)/shard_map/all_gather | solution.py:96
  253.8 716.0 %all-gather.43.cloned.1.call-start = ((), (), s32[]{:S(2)}) async-start(), calls=%async_computation.16 | async-start | bytes 5242880 | tf_op jit(solution)/shard_map/all_gather | solution.py:258
  596.4 272.9 %copy-start.3 = (f32[512,1024]{1,0:T(8,128)}, f32[512,1024]{1,0:T(8,128)S(1)}, u32[]{:S(2)}) copy-start(f32[512,1024]{1,0:T(8,128)S(1)} %get-tuple-element.242) | copy-start | bytes 6291460
  655.8 122.0 %copy-start.36 = (bf16[512,1024]{1,0:T(8,128)(2,1)S(1)}, bf16[512,1024]{1,0:T(8,128)(2,1)}, u32[]{:S(2)}) copy-start(bf16[512,1024]{1,0:T(8,128)(2,1)} %multiply_convert_fusion.5) | copy-start | bytes 3145732
  876.6 546.6 %reduce-scatter.10.cloned.1.call-start = ((), (), s32[]{:S(2)}) async-start(), calls=%async_computation.20 | async-start | bytes 17301504
  1058.4 859.4 %reduce-scatter.6.cloned.1.call-start = ((), (), s32[]{:S(2)}) async-start(), calls=%async_computation.17 | async-start | bytes 23789568 | tf_op jit(solution)/shard_map/reduce_scatter | solution.py:333
  1076.3 1093.9 %reduce-scatter.8.cloned.1.call-start = ((), (), s32[]{:S(2)}) async-start(), calls=%async_computation.18 | async-start | bytes 11894784 | tf_op jit(solution)/shard_map/reduce_scatter | solution.py:336
  (53 other events, 875.2 us)
Sparse Core Ops, SparseCore 0:
  9.9 30.5 all-gather.24
  42.4 27.8 all-gather.28
  73.3 56.4 all-gather.16
  132.6 55.3 all-gather.18
  190.7 55.3 all-gather.22
  247.5 45.0 all-gather.26
  294.2 44.1 all-gather.30
  340.6 79.4 all-gather.20
  421.7 79.2 all-gather.44
  503.8 54.9 all-gather.32
  560.4 79.6 all-gather.40
  642.7 65.8 all-gather.34
  711.5 66.2 all-gather.36
  780.5 66.2 all-gather.38
  876.7 80.0 all-gather.42
  1058.5 364.6 reduce-scatter.9
  1425.4 492.3 reduce-scatter.5
  1920.5 249.6 reduce-scatter.7
where the time goes:
time: 2190 us; the launch traced here: 2180 us
  waiting for transfers between devices  1620 us (74%)
  matrix products  275 us (13%)
  blocking collectives  110 us (5%)
  local copies, waits for them, and re-layouts  89 us (4%)
  other arithmetic  60.5 us (3%)
    reduce_scatter x1, waiting for transfers between devices, on_device(): lax.psum_scatter(jnp.concatenate([gate_part, up_part], 1), ('doc', 'seq')...  493 us
    unnamed x19, waiting for transfers between devices  279 us
    reduce_scatter x1, waiting for transfers between devices, on_device(): lax.psum_scatter(jnp.einsum('tf,td->fd', hidden, grad_y, preferred_elemen...  250 us
    unnamed x2, blocking collectives  83.2 us
    all_gather x1, waiting for transfers between devices, on_device(): key_part = lax.all_gather(k_rot, 'seq', axis=1, tiled=True)  77.7 us
    all_gather x1, waiting for transfers between devices, on_device(): value_part = lax.all_gather(v_low, 'seq', axis=1, tiled=True)  65.1 us
    all_gather x1, waiting for transfers between devices, on_device(): lax.all_gather(w_down, ('doc', 'seq'), axis=0, tiled=True)  61.3 us
    all_gather x1, waiting for transfers between devices, on_device(): lax.all_gather(w_up, ('doc', 'seq'), axis=0, tiled=True)  60.6 us
  transfers between devices with their start and end apart: 18, of which 16 were waited for; matrix products, arithmetic and copies ran while one was open for 14% of the time, Pallas kernels for 0%

commit v1 on v0

--- a/solution.py
+++ b/solution.py
@@ -1,8 +1,11 @@
+import functools
 import math
 
 import jax
 import jax.numpy as jnp
 from jax import lax
+from jax.experimental import pallas as pl
+from jax.experimental.pallas import tpu as pltpu
 from jax.sharding import PartitionSpec as P
 
 HEADS = 8
@@ -369,6 +372,533 @@
     )
 
 
+LINE = ("doc", "seq")
+MXU = dict(preferred_element_type=jnp.float32)
+LOG2E = 1.4426950408889634
+
+
+def dot_nt(left, right):
+    return lax.dot_general(left, right, (((1,), (1,)), ((), ())), **MXU)
+
+
+def dot_tn(left, right):
+    return lax.dot_general(left, right, (((0,), (0,)), ((), ())), **MXU)
+
+
+def dot_nn(left, right):
+    return jnp.dot(left, right, **MXU)
+
+
+def whole(count):
+    return [pl.BlockSpec(memory_space=pltpu.VMEM)] * count
+
+
+def hbm(count):
+    return [pl.BlockSpec(memory_space=pl.ANY)] * count
+
+
+def smem():
+    return pl.BlockSpec(memory_space=pltpu.SMEM)
+
+
+def attend_kernel(
+    place, b0, b1, b2, b3, mem_own, mem_src, cos_ref, sin_ref,
+    qr_ref, qm_ref, kr_ref, v_ref, att_ref, lse_ref, o0, o1, o2, o3,
+    max_s, sum_s, acc_s,
+):
+    quarter, flag = place[0], place[1]
+    rows_q = b0.shape[0]
+    width = o0.shape[1]
+    heads = width // HEAD_DIM
+    tiles = qr_ref.shape[0] // rows_q
+    scale2 = LOG2E / math.sqrt(HEAD_DIM)
+    half = HEAD_DIM // 2
+
+    for rel, block in enumerate((b0, b1, b2, b3)):
+        rows = pl.ds(pl.multiple_of((quarter ^ rel) * rows_q, rows_q), rows_q)
+        cos_t, sin_t = cos_ref[rows, :], sin_ref[rows, :]
+        for head in range(heads):
+            cols = slice(head * HEAD_DIM, (head + 1) * HEAD_DIM)
+            query = block[:, head * HEAD_DIM : (head + 1) * HEAD_DIM]
+            qm_ref[rows, cols] = query
+            wide = query.astype(jnp.float32)
+            qr_ref[rows, cols] = (wide * cos_t + pltpu.roll(wide, half, 1) * sin_t).astype(
+                jnp.bfloat16
+            )
+            wide = block[:, width + head * HEAD_DIM : width + (head + 1) * HEAD_DIM].astype(
+                jnp.float32
+            )
+            kr_ref[rows, cols] = (wide * cos_t + pltpu.roll(wide, half, 1) * sin_t).astype(
+                jnp.bfloat16
+            )
+            v_ref[rows, cols] = block[
+                :, 2 * width + head * HEAD_DIM : 2 * width + (head + 1) * HEAD_DIM
+            ]
+
+    for head in range(heads):
+        cols = slice(head * HEAD_DIM, (head + 1) * HEAD_DIM)
+        vcols = slice(width + head * HEAD_DIM, width + (head + 1) * HEAD_DIM)
+
+        def fold(scores, values):
+            old_max = max_s[...]
+            new_max = jnp.maximum(old_max, jnp.max(scores, 1, keepdims=True))
+            spread = jnp.concatenate([new_max] * (scores.shape[1] // HEAD_DIM), 1)
+            weights = jnp.exp2((scores - spread) * scale2)
+            shrink = jnp.exp2((old_max - new_max) * scale2)
+            sum_s[...] = sum_s[...] * shrink + jnp.sum(weights, 1, keepdims=True)
+            acc_s[...] = acc_s[...] * shrink + dot_nn(weights.astype(jnp.bfloat16), values)
+            max_s[...] = new_max
+
+        def tile(index, carry):
+            rows = pl.ds(pl.multiple_of(index * rows_q, rows_q), rows_q)
+            query = qr_ref[rows, cols]
+            max_s[...] = jnp.full_like(max_s, NEG_FILL)
+            sum_s[...] = jnp.zeros_like(sum_s)
+            acc_s[...] = jnp.zeros_like(acc_s)
+
+            def earlier(block, inner):
+                keys = pl.ds(pl.multiple_of(block * rows_q, rows_q), rows_q)
+                fold(dot_nt(query, kr_ref[keys, cols]), v_ref[keys, cols])
+                return inner
+
+            lax.fori_loop(0, index, earlier, 0)
+            scores = dot_nt(query, kr_ref[rows, cols])
+            row_i = lax.broadcasted_iota(jnp.int32, scores.shape, 0)
+            col_i = lax.broadcasted_iota(jnp.int32, scores.shape, 1)
+            fold(jnp.where(col_i <= row_i, scores, NEG_FILL), v_ref[rows, cols])
+
+            @pl.when(flag > 0)
+            def _():
+                plain = qm_ref[rows, cols]
+                for mem in (mem_own, mem_src):
+                    fold(dot_nt(plain, mem[:, cols]), mem[:, vcols])
+
+            total = sum_s[...]
+            att_ref[rows, cols] = (acc_s[...] / total).astype(jnp.bfloat16)
+            lse = max_s[...] * scale2 + jnp.log(total) * LOG2E
+            lse_ref[head, :, rows] = jnp.transpose(lse)[:8]
+            return carry
+
+        lax.fori_loop(0, tiles, tile, 0)
+
+    for rel, out in enumerate((o0, o1, o2, o3)):
+        rows = pl.ds(pl.multiple_of((quarter ^ rel) * rows_q, rows_q), rows_q)
+        out[...] = att_ref[rows, :]
+
+
+def attend(place, blocks, mem_own, mem_src, cos_t, sin_t):
+    rows_q, three = blocks[0].shape
+    width = three // 3
+    length = cos_t.shape[0]
+    low = jnp.bfloat16
+    full = jax.ShapeDtypeStruct((length, width), low)
+    part = jax.ShapeDtypeStruct((rows_q, width), low)
+    return pl.pallas_call(
+        attend_kernel,
+        out_shape=[full] * 5
+        + [jax.ShapeDtypeStruct((width // HEAD_DIM, 8, length), jnp.float32)]
+        + [part] * 4,
+        in_specs=[smem()] + whole(8),
+        out_specs=whole(10),
+        scratch_shapes=[pltpu.VMEM((rows_q, HEAD_DIM), jnp.float32)] * 3,
+        compiler_params=pltpu.CompilerParams(vmem_limit_bytes=40 << 20),
+        cost_estimate=pl.CostEstimate(
+            flops=length * length * width * 4, bytes_accessed=14 << 20, transcendentals=length * length * 4
+        ),
+        name="attend",
+    )(place, *blocks, mem_own, mem_src, cos_t, sin_t)
+
+
+def attend_back_kernel(
+    place, qr_ref, qm_ref, kr_ref, v_ref, att_ref, lse_ref, d0, d1, d2, d3, mem_own, mem_src,
+    cos_ref, sin_ref, g0, g1, g2, g3, datt, dkey, dval, dqr, dqm, grads,
+):
+    quarter, flag = place[0], place[1]
+    rows_q, width = d0.shape
+    heads = width // HEAD_DIM
+    tiles = qr_ref.shape[0] // rows_q
+    scale = 1.0 / math.sqrt(HEAD_DIM)
+    scale2 = LOG2E * scale
+    half = HEAD_DIM // 2
+    low = jnp.bfloat16
+
+    def unrotate(grad, rows):
+        return grad * cos_ref[rows, :] - pltpu.roll(grad, half, 1) * sin_ref[rows, :]
+
+    for rel, block in enumerate((d0, d1, d2, d3)):
+        rows = pl.ds(pl.multiple_of((quarter ^ rel) * rows_q, rows_q), rows_q)
+        datt[rows, :] = block[...]
+
+    for head in range(heads):
+        cols = slice(head * HEAD_DIM, (head + 1) * HEAD_DIM)
+        vcols = slice(width + head * HEAD_DIM, width + (head + 1) * HEAD_DIM)
+        dkey[...] = jnp.zeros_like(dkey)
+        dval[...] = jnp.zeros_like(dval)
+
+        def tile(index, carry):
+            rows = pl.ds(pl.multiple_of(index * rows_q, rows_q), rows_q)
+            query = qr_ref[rows, cols]
+            d_out = datt[rows, cols]
+            delta = jnp.sum(
+                jnp.transpose(d_out.astype(jnp.float32) * att_ref[rows, cols].astype(jnp.float32)),
+                0,
+                keepdims=True,
+            )
+            lse = lse_ref[head, 0:1, rows]
+            dqr[...] = jnp.zeros_like(dqr)
+            dqm[...] = jnp.zeros_like(dqm)
+
+            def block_grads(keys, values, queries, masked):
+                power = dot_nt(keys, queries) * scale2 - lse
+                if masked:
+                    key_i = lax.broadcasted_iota(jnp.int32, power.shape, 0)
+                    query_i = lax.broadcasted_iota(jnp.int32, power.shape, 1)
+                    power = jnp.where(key_i <= query_i, power, NEG_FILL)
+                probs = jnp.exp2(power)
+                d_scores = probs * (dot_nt(values, d_out) - delta)
+                return probs.astype(low), d_scores.astype(low)
+
+            def local(keys_at, masked):
+                keys = kr_ref[keys_at, cols]
+                probs, d_scores = block_grads(keys, v_ref[keys_at, cols], query, masked)
+                dval[keys_at, :] += dot_nn(probs, d_out)
+                dkey[keys_at, :] += dot_nn(d_scores, query)
+                dqr[...] += dot_tn(d_scores, keys)
+
+            def earlier(block, inner):
+                local(pl.ds(pl.multiple_of(block * rows_q, rows_q), rows_q), False)
+                return inner
+
+            lax.fori_loop(0, index, earlier, 0)
+            local(rows, True)
+
+            @pl.when(flag > 0)
+            def _():
+                plain = qm_ref[rows, cols]
+                for mem in (mem_own, mem_src):
+                    keys = mem[:, cols]
+                    probs, d_scores = block_grads(keys, mem[:, vcols], plain, False)
+                    dqm[...] += dot_tn(d_scores, keys)
+
+            grads[rows, cols] = ((unrotate(dqr[...], rows) + dqm[...]) * scale).astype(low)
+            return carry
+
+        lax.fori_loop(0, tiles, tile, 0)
+        for index in range(tiles):
+            rows = pl.ds(index * rows_q, rows_q)
+            grads[rows, vcols] = (unrotate(dkey[rows, :], rows) * scale).astype(low)
+            grads[rows, 2 * width + head * HEAD_DIM : 2 * width + (head + 1) * HEAD_DIM] = dval[
+                rows, :
+            ].astype(low)
+
+    for rel, out in enumerate((g0, g1, g2, g3)):
+        rows = pl.ds(pl.multiple_of((quarter ^ rel) * rows_q, rows_q), rows_q)
+        out[...] = grads[rows, :]
+
+
+def attend_back(place, saved, d_blocks, mem_own, mem_src, cos_t, sin_t):
+    rows_q, width = d_blocks[0].shape
+    length = cos_t.shape[0]
+    low = jnp.bfloat16
+    return pl.pallas_call(
+        attend_back_kernel,
+        out_shape=[jax.ShapeDtypeStruct((rows_q, 3 * width), low)] * 4,
+        in_specs=[smem()] + whole(14),
+        out_specs=whole(4),
+        scratch_shapes=[
+            pltpu.VMEM((length, width), low),
+            pltpu.VMEM((length, HEAD_DIM), jnp.float32),
+            pltpu.VMEM((length, HEAD_DIM), jnp.float32),
+            pltpu.VMEM((rows_q, HEAD_DIM), jnp.float32),
+            pltpu.VMEM((rows_q, HEAD_DIM), jnp.float32),
+            pltpu.VMEM((length, 3 * width), low),
+        ],
+        compiler_params=pltpu.CompilerParams(vmem_limit_bytes=48 << 20),
+        cost_estimate=pl.CostEstimate(
+            flops=length * length * width * 10, bytes_accessed=14 << 20, transcendentals=length * length * 4
+        ),
+        name="attend_back",
+    )(place, *saved, *d_blocks, mem_own, mem_src, cos_t, sin_t)
+
+
+def settle_kernel(plan, widths, rows, n_pieces, *refs):
+    where = refs[0]
+    pieces = refs[1 : 1 + n_pieces]
+    outs = refs[1 + n_pieces : 1 + n_pieces + len(widths)]
+    sems = refs[-1]
+    copies = []
+    for piece, (rel, first, count) in zip(pieces, plan):
+        start = pl.multiple_of((where[0] ^ rel) * rows + first, 16)
+        left = 0
+        for out, width in zip(outs, widths):
+            copy = pltpu.make_async_copy(
+                piece.at[:, pl.ds(left, width)],
+                out.at[pl.ds(start, count), :],
+                sems.at[len(copies)],
+            )
+            copy.start()
+            copies.append(copy)
+            left += width
+    for copy in copies:
+        copy.wait()
+
+
+def settle(where, plan, pieces, widths, rows, n_doc):
+    low = jnp.bfloat16
+    return pl.pallas_call(
+        functools.partial(settle_kernel, plan, widths, rows, len(pieces)),
+        out_shape=[jax.ShapeDtypeStruct((n_doc * rows, width), low) for width in widths],
+        in_specs=[smem()] + hbm(len(pieces)),
+        out_specs=hbm(len(widths)),
+        scratch_shapes=[pltpu.SemaphoreType.DMA((len(pieces) * len(widths),))],
+        compiler_params=pltpu.CompilerParams(vmem_limit_bytes=4 << 20),
+        cost_estimate=pl.CostEstimate(
+            flops=0, bytes_accessed=4 * n_doc * rows * sum(widths), transcendentals=0
+        ),
+        name="settle",
+    )(where, *pieces)
+
+
+def segment_pairs(n_doc, n_seq):
+    places = [(d, z) for d in range(n_doc) for z in range(n_seq)]
+
+    def route(target):
+        return [(d * n_seq + z, target(d, z)[0] * n_seq + target(d, z)[1]) for d, z in places]
+
+    def regroup(d, z):
+        return ((d & ~1) | (z >> 1), 2 * (d & 1) + (z & 1))
+
+    return {
+        "regroup": route(regroup),
+        "core": route(lambda d, z: (d ^ 1, z)),
+        "x": route(lambda d, z: (d ^ 2, z)),
+        "y": route(lambda d, z: (d ^ 4, z)),
+        1: route(lambda d, z: (d, z ^ 1)),
+        2: route(lambda d, z: (d ^ 1, z)),
+        3: route(lambda d, z: (d ^ 1, z ^ 1)),
+        "z1": route(lambda d, z: (d, (z + 1) % n_seq)),
+        "z2": route(lambda d, z: (d, (z + 2) % n_seq)),
+        "z3": route(lambda d, z: (d, (z + 3) % n_seq)),
+    }
+
+
+def on_pair(
+    routes,
+    tokens,
+    w_query,
+    w_key,
+    w_value,
+    w_out,
+    w_gate,
+    w_up,
+    w_down,
+    gain_attn,
+    gain_ffn,
+    cache_keys,
+    cache_values,
+    memory_flags,
+    memory_source,
+    positions,
+    out_grad,
+):
+    low, wide = jnp.bfloat16, jnp.float32
+    n_doc, n_seq = lax.axis_size("doc"), lax.axis_size("seq")
+    d, z = lax.axis_index("doc"), lax.axis_index("seq")
+    core, odd, pair = d & 1, z & 1, z >> 1
+    quarter = 2 * core + odd
+    heads_at = 2 * odd + core
+    turn = (0, 2, 1, 3)
+    tok_local, width = tokens.shape[1:]
+    ff_width = w_gate.shape[1]
+    share = width // n_seq
+    where = d.astype(jnp.int32).reshape(1)
+
+    def move(array, name):
+        return lax.ppermute(array, LINE, routes[name])
+
+    def pick(array, index, axis=0):
+        return lax.dynamic_index_in_dim(array, index, axis, keepdims=False)
+
+    def gather(shard):
+        block = lax.all_gather(shard, "seq", axis=0, tiled=True)
+        rows = block.shape[0]
+        cut = rows // 2
+        by_x, by_y = move(block, "x"), move(block, "y")
+        far_a, far_b = move(by_x[:cut], "y"), move(by_y[cut:], "x")
+        mine = (block, by_x, by_y, far_a, far_b)
+        plan = ((0, 0, rows), (2, 0, rows), (4, 0, rows), (6, 0, cut), (6, cut, cut))
+        other = tuple(move(piece, "core") for piece in mine)
+        plan = plan + tuple((rel ^ 1, first, count) for rel, first, count in plan)
+        return plan, mine + other, rows
+
+    cols = []
+    for index in range(n_seq):
+        for weight in (w_query, w_key, w_value):
+            cols.append(weight[:, index * share : (index + 1) * share])
+    gains = jnp.concatenate([gain_attn[:, None], gain_ffn[:, None]], 1)
+    cols.append(jnp.pad(gains, ((0, 0), (0, HEAD_DIM - 2))))
+    shard_qkv = jnp.concatenate(cols, 1)
+    shard_ffn = jnp.concatenate([w_out, w_gate, w_up], 1)
+
+    plan, pieces, rows = gather(shard_qkv)
+    w_qkv, gain_cols = settle(where, plan, pieces, (3 * width, HEAD_DIM), rows, n_doc)
+    plan, pieces, rows = gather(shard_ffn)
+    w_out_f, w_gate_f, w_up_f = settle(
+        where, plan, pieces, (width, ff_width, ff_width), rows, n_doc
+    )
+    plan, pieces, rows_down = gather(w_down)
+    (w_down_f,) = settle(where, plan, pieces, (width,), rows_down, n_doc)
+    gain_a = gain_cols[:, 0].astype(wide)
+    gain_f = gain_cols[:, 1].astype(wide)
+
+    tok = move(tokens[0], "regroup")
+    grad_y = move(out_grad[0], "regroup")
+
+    notes = jnp.concatenate([memory_flags, memory_source])
+    notes = jnp.where(pair == core, notes, move(notes, "core"))
+    notes_y = move(notes, "y")
+    flag, source, source_y = notes[0], notes[1], notes_y[1]
+    pos = lax.all_gather(positions[0], "seq", axis=0, tiled=True)
+    pos = jnp.where(pair == core, pos, move(pos, "core"))
+    cos_h, sin_h = rotary_tables(pos)
+    cos_t = jnp.concatenate([cos_h, cos_h], -1)
+    sin_t = jnp.concatenate([-sin_h, sin_h], -1)
+    place = jnp.stack([quarter, flag]).astype(jnp.int32)
+
+    def half_of(which):
+        at = which * (width // 2)
+        return jnp.concatenate(
+            [
+                lax.dynamic_slice_in_dim(cache[0], at, width // 2, 1)
+                for cache in (cache_keys, cache_values)
+            ],
+            1,
+        )
+
+    same, cross = half_of(odd), half_of(1 - odd)
+    column = jnp.concatenate(
+        [same, move(cross, "z1"), move(same, "z2"), move(cross, "z3")], 0
+    )
+    parts = column.reshape(column.shape[0], 2, 2, share)
+    kept = pick(parts, core, 2).reshape(-1, 2 * share)
+    sent = move(pick(parts, 1 - core, 2).reshape(-1, 2 * share), "core")
+    here = jnp.stack([kept, sent])
+    four = jnp.concatenate([here, move(here, "x")], 0)
+
+    def rel_of(src):
+        return 2 * (((src ^ d) >> 1) & 1) + ((src ^ d) & 1)
+
+    from_y = move(pick(four, rel_of(source_y)), "y")
+    mem_src = jnp.where(((source ^ d) >> 2) == 0, pick(four, rel_of(source)), from_y)
+    mem_own = pick(here, pair ^ core)
+
+    inputs = tok.astype(wide)
+    factor_one = rms_factor(inputs)
+    normed_one = inputs * factor_one
+    attn_in = (normed_one * gain_a).astype(low)
+    qkv = dot_nn(attn_in, w_qkv).astype(low)
+
+    def part_for(array, rel, size):
+        return lax.dynamic_slice_in_dim(array, (heads_at ^ turn[rel]) * size, size, 1)
+
+    def spread(blocks):
+        size = blocks[0].shape[1]
+        out = jnp.zeros((blocks[0].shape[0], n_seq * size), low)
+        for rel, block in enumerate(blocks):
+            out = lax.dynamic_update_slice_in_dim(out, block, (heads_at ^ turn[rel]) * size, 1)
+        return out
+
+    def exchange(blocks):
+        return [blocks[0]] + [move(blocks[rel], rel) for rel in (1, 2, 3)]
+
+    blocks = exchange([part_for(qkv, rel, 3 * share) for rel in range(4)])
+    *saved, o0, o1, o2, o3 = attend(place, blocks, mem_own, mem_src, cos_t, sin_t)
+    attn_low = spread(exchange([o0, o1, o2, o3]))
+    resid_mid = inputs + dot_nn(attn_low, w_out_f)
+    factor_two = rms_factor(resid_mid)
+    normed_two = resid_mid * factor_two
+    ffn_in = (normed_two * gain_f).astype(low)
+    gate_act = dot_nn(ffn_in, w_gate_f)
+    up_act = dot_nn(ffn_in, w_up_f)
+    sig_gate = jax.nn.sigmoid(gate_act)
+    silu_gate = gate_act * sig_gate
+    hidden = (silu_gate * up_act).astype(low)
+    layer_out = move((resid_mid + dot_nn(hidden, w_down_f)).astype(low), "regroup")
+
+    def reduce(grads, block_rows):
+        cut = block_rows // 2
+
+        def side(which):
+            picked = [
+                pick(grad.reshape(n_doc // 2, 2, block_rows, grad.shape[1]), which, 1)
+                for grad in grads
+            ]
+            return picked[0] if len(picked) == 1 else jnp.concatenate(picked, 2)
+
+        met = move(side(1 - core), "core")
+        both = (side(core).astype(wide) + met.astype(wide)).astype(low)
+        at = d >> 1
+        far = pick(both, at ^ 3)
+        in_a, in_b = move(far[:cut], "y"), move(far[cut:], "x")
+        to_x, to_y = pick(both, at ^ 1), pick(both, at ^ 2)
+        to_x = jnp.concatenate(
+            [(to_x[:cut].astype(wide) + in_a.astype(wide)).astype(low), to_x[cut:]], 0
+        )
+        to_y = jnp.concatenate(
+            [to_y[:cut], (to_y[cut:].astype(wide) + in_b.astype(wide)).astype(low)], 0
+        )
+        in_x, in_y = move(to_x, "x"), move(to_y, "y")
+        total = (
+            pick(both, at).astype(wide) + in_x.astype(wide) + in_y.astype(wide)
+        ).astype(low)
+        return lax.psum_scatter(total, "seq", scatter_dimension=0, tiled=True).astype(wide)
+
+    def row_sums(product):
+        ones = jnp.ones((product.shape[0], HEAD_DIM), low)
+        return dot_tn(product.astype(low), ones).astype(low)
+
+    d_hidden = dot_nt(grad_y, w_down_f)
+    grad_down = dot_tn(hidden, grad_y).astype(low)
+    out_down = reduce([grad_down], rows_down)
+    d_gate = (d_hidden * up_act * (sig_gate * (1.0 + gate_act * (1.0 - sig_gate)))).astype(low)
+    d_up = (d_hidden * silu_gate).astype(low)
+    d_ffn_in = dot_nt(d_gate, w_gate_f) + dot_nt(d_up, w_up_f)
+    d_mid = grad_y.astype(wide) + norm_back(d_ffn_in * gain_f, normed_two, factor_two)
+    d_branch = d_mid.astype(low)
+    d_att = dot_nt(d_branch, w_out_f).astype(low)
+    d_blocks = exchange([part_for(d_att, rel, share) for rel in range(4)])
+    grad_gate = dot_tn(ffn_in, d_gate).astype(low)
+    grad_up = dot_tn(ffn_in, d_up).astype(low)
+    grad_out = dot_tn(attn_low, d_branch).astype(low)
+    gain_f_cols = row_sums(d_ffn_in * normed_two)
+    out_ffn = reduce([grad_gate, grad_up], rows)
+    out_mid = reduce([grad_out, gain_f_cols], rows)
+    d_parts = attend_back(place, saved, d_blocks, mem_own, mem_src, cos_t, sin_t)
+    d_qkv = spread(exchange(d_parts))
+    d_attn_in = dot_nt(d_qkv, w_qkv)
+    grad_qkv = dot_tn(attn_in, d_qkv).astype(low)
+    gain_a_cols = row_sums(d_attn_in * normed_one)
+    out_qkv = reduce([grad_qkv, gain_a_cols], rows)
+    grad_in = d_mid + norm_back(d_attn_in * gain_a, normed_one, factor_one)
+    grad_tokens = move(grad_in.astype(low), "regroup").astype(wide)
+
+    split = out_qkv[:, : 3 * width].reshape(-1, n_seq, 3, share)
+    out_q, out_k, out_v = (split[:, :, which].reshape(-1, width) for which in range(3))
+    return (
+        layer_out[None],
+        grad_tokens[None],
+        out_q,
+        out_k,
+        out_v,
+        out_mid[:, :width],
+        out_ffn[:, :ff_width],
+        out_ffn[:, ff_width:],
+        out_down,
+        out_qkv[:, 3 * width],
+        out_mid[:, width],
+    )
+
+
 def solution(mesh):
     in_specs = (
         P("doc", "seq", None),
@@ -401,6 +931,10 @@
         P(("doc", "seq")),
         P(("doc", "seq")),
     )
+    n_doc, n_seq = mesh.shape["doc"], mesh.shape["seq"]
+    step = on_device
+    if (n_doc, n_seq) == (8, 4):
+        step = functools.partial(on_pair, segment_pairs(n_doc, n_seq))
     return jax.shard_map(
-        on_device, mesh=mesh, in_specs=in_specs, out_specs=out_specs, check_vma=False
-    )
+        step, mesh=mesh, in_specs=in_specs, out_specs=out_specs, check_vma=False
+    )

time: 2190 us -> 687 us (0.31)
  the two profiles are of different devices: /device:TPU:0 before, /device:TPU:1 now
where the time goes in v1:
time: 687 us; the launch traced here: 681 us
  waiting for transfers between devices  220 us (32%)
  starting transfers between devices  87.9 us (13%)
  matrix products  76.1 us (11%)
  blocking collectives  73.5 us (11%)
  other arithmetic  69.3 us (10%)
  Pallas kernels  68.2 us (10%)
  local copies, waits for them, and re-layouts  67.5 us (10%)
  between operations  18.1 us (3%)
    ppermute x72, waiting for transfers between devices, move(): return lax.ppermute(array, LINE, routes[name])  220 us
    ppermute x72, starting transfers between devices, move(): return lax.ppermute(array, LINE, routes[name])  87.5 us
    all_gather x2, blocking collectives, gather(): block = lax.all_gather(shard, 'seq', axis=0, tiled=True)  59.4 us
    pallas_call x1, Pallas kernels, attend_back(): pl.pallas_call(attend_back_kernel, out_shape=[jax.ShapeDtypeStruct((rows_...  35.1 us
    dot_general x5, matrix products, dot_nn(): return jnp.dot(left, right, **MXU)  30.9 us
    unnamed x140, local copies, waits for them, and re-layouts  25.2 us
    pallas_call x1, Pallas kernels, attend(): pl.pallas_call(attend_kernel, out_shape=[full] * 5 + [jax.ShapeDtypeStruc...  24.1 us
    dot_general x5, matrix products, dot_nt(): return lax.dot_general(left, right, (((1,), (1,)), ((), ())), **MXU)  23.2 us
  transfers between devices with their start and end apart: 77, of which 27 were waited for; matrix products, arithmetic and copies ran while one was open for 21% of the time, Pallas kernels for 9%

profile of v1, /device:TPU:1, one launch (start us, length us, event | category | flops | bytes accessed | tf_op | source)
XLA Modules:
  0.0 680.9 jit_solution(13135532865652746756)
XLA Ops:
  16.0 14.0 %all-gather = s32[1,2048]{1,0:T(1,128)S(1)} all-gather(s32[1,512]{1,0:T(1,128)} %param.30), channel_id=2, replica_groups=mesh['doc'=8,'seq'=4] {'seq'}, dimensions={1}, use_global_device_ids=true | all-gather | bytes 10240 | tf_op jit(solution)/shard_map/all_gather | solution.py:761
  34.7 20.5 %all_gather.15.refs_1_ = bf16[352,1024]{1,0:T(8,128)(2,1)S(1)} all-gather(bf16[88,1024]{1,0:T(8,128)(2,1)S(1)} %copy-done.48), channel_id=1, replica_groups=mesh['doc'=8,'seq'=4] {'seq'}, dimensions={0}, use_global_device_ids=true | all-gather | bytes 901120 | tf_op jit(solution)/shard_map/all_gather | solution.py:723
  62.0 39.0 %all_gather.12.refs_1_ = bf16[128,3200]{1,0:T(8,128)(2,1)S(1)} all-gather(bf16[32,3200]{1,0:T(8,128)(2,1)S(1)} %constant_dynamic-update-slice_fusion), channel_id=1, replica_groups=mesh['doc'=8,'seq'=4] {'seq'}, dimensions={0}, use_global_device_ids=true | all-gather | bytes 1024000 | tf_op jit(solution)/shard_map/all_gather | solution.py:723
  110.8 7.2 %collective-permute-start.6 = (bf16[128,3200]{1,0:T(8,128)(2,1)S(1)}, bf16[128,3200]{1,0:T(8,128)(2,1)}, u32[]{:S(2)}, u32[]{:S(2)}) collective-permute-start(bf16[128,3200]{1,0:T(8,128)(2,1)S(1)} %all_gather.12.refs_1_), channel_id=1, source_target_pairs={{0,4},{1,5},{2,6},{3,7},{4,0},{5,1},{6,2},{7,3},{8,12},{9,13},{10,... | collective-permute-start | bytes 2457608 | tf_op jit(solution)/shard_map/ppermute | solution.py:717
  141.0 6.6 collective-permute-start.10
  168.6 6.6 convolution_convert_fusion.4
  178.9 24.5 %collective-permute-done.37.refs_5_ = bf16[176,1024]{1,0:T(8,128)(2,1)} collective-permute-done((bf16[176,1024]{1,0:T(8,128)(2,1)}, bf16[176,1024]{1,0:T(8,128)(2,1)}, u32[]{:S(2)}, u32[]{:S(2)}) %collective-permute-start.37) | collective-permute-done | bytes 360480 | tf_op jit(solution)/shard_map/ppermute | solution.py:717
  227.1 13.0 %collective-permute-done.13.b3 = bf16[512,768]{1,0:T(8,128)(2,1)} collective-permute-done((bf16[512,768]{1,0:T(8,128)(2,1)}, bf16[512,768]{1,0:T(8,128)(2,1)}, u32[]{:S(2)}, u32[]{:S(2)}) %collective-permute-start.13) | collective-permute-done | bytes 786464 | tf_op jit(solution)/shard_map/ppermute | solution.py:717
  241.0 24.1 %attend.1 = (bf16[2048,256]{1,0:T(8,128)(2,1)S(1)}, bf16[2048,256]{1,0:T(8,128)(2,1)S(1)}, bf16[2048,256]{1,0:T(8,128)(2,1)S(1)}, bf16[2048,256]{1,0:T(8,128)(2,...) custom-call(s32[2]{0:T(128)S(1)} %pad_add_fusion.1.place, ...), custom_call_target="tpu_custom_call" | custom-call | flops 4294967296 | bytes 14680064 | tf_op jit(solution)/shard_map/attend/pallas_call | solution.py:496
  291.6 8.2 %fusion.50 = f32[2816,512]{0,1:T(8,128)} fusion(bf16[2816,1024]{1,0:T(8,128)(2,1)S(1)} %settle.5, bf16[512,1024]{1,0:T(8,128)(2,1)} %collective-permute-done.44), kind=kOutput, calls=%fused_computation.199 | convolution fusion | flops 2952790016 | bytes 12582912 | tf_op jit(solution)/shard_map/dot_general | solution.py:381
  311.7 10.0 %fusion.2 = (bf16[512,2816]{1,0:T(8,128)(2,1)S(1)}, bf16[512,2816]{1,0:T(8,128)(2,1)}, bf16[512,2816]{1,0:T(8,128)(2,1)}) fusion(f32[2816,512]{0,1:T(8,128)} %fusion.50, f32[512,2816]{1,0:T(8,128)} %fusion.49, bf16[512,1024]{1,0:T(8,128)(2,1)S(1)} %multiply_convert_fusion.2, bf16[1024,2816]{1,0:T(8,128)(2,1)S(1)} %get-tuple-element.38), kind=kOutput, calls=%fused_computation.8 | convolution fusion | flops 2974416896 | bytes 27000832 | tf_op jit(solution)/shard_map/dot_general | solution.py:389
  357.7 35.1 %attend_back.1 = (bf16[512,768]{1,0:T(8,128)(2,1)S(1)}, bf16[512,768]{1,0:T(8,128)(2,1)S(1)}, bf16[512,768]{1,0:T(8,128)(2,1)S(1)}, bf16[512,768]{1,0:T(8,128)(2,1)S(1)}) custom-call(s32[2]{0:T(128)S(1)} %pad_add_fusion.1.place, bf16[2048,256]{1,0:T(8,128)(2,1)} %copy-done.21, bf16[2048,256]{1,0:T(8,128)(2,1)} %copy-done.22, bf16[2048,256]{1,0:T(8,128)(2,1)} %copy-done.23, ...), custom_call_target="tpu_custom_call" | custom-call | flops 10737418240 | bytes 14680064 | tf_op jit(solution)/shard_map/attend_back/pallas_call | solution.py:603
  404.5 7.2 %collective-permute-done.48 = bf16[512,768]{1,0:T(8,128)(2,1)S(1)} collective-permute-done((bf16[512,768]{1,0:T(8,128)(2,1)S(1)}, bf16[512,768]{1,0:T(8,128)(2,1)S(1)}, u32[]{:S(2)}, u32[]{:S(2)}) %collective-permute-start.48) | collective-permute-done | bytes 786464 | tf_op jit(solution)/shard_map/ppermute | solution.py:717
  413.8 15.2 %collective-permute-done.50 = bf16[512,768]{1,0:T(8,128)(2,1)S(1)} collective-permute-done((bf16[512,768]{1,0:T(8,128)(2,1)S(1)}, bf16[512,768]{1,0:T(8,128)(2,1)S(1)}, u32[]{:S(2)}, u32[]{:S(2)}) %collective-permute-start.50) | collective-permute-done | bytes 786464 | tf_op jit(solution)/shard_map/ppermute | solution.py:717
  434.6 5.9 convolution_convert_fusion.3
  494.7 5.9 collective-permute-done.53
  502.6 8.2 %add_convert_fusion = bf16[4,128,5632]{2,1,0:T(8,128)(2,1)} fusion(bf16[4,128,5632]{2,1,0:T(8,128)(2,1)} %collective-permute-done.62, bf16[4,128,2816]{2,1,0:T(8,128)(2,1)} %get-tuple-element.64, bf16[4,128,2816]{2,1,0:T(8,128)(2,1)} %get-tuple-element.62), kind=kLoop, calls=%fused_computation | loop fusion | flops 20185088 | bytes 17301504 | tf_op jit(solution)/shard_map/convert_element_type | solution.py:839
  516.0 9.8 %collective-permute-done.63 = bf16[64,5632]{1,0:T(8,128)(2,1)S(1)} collective-permute-done((bf16[64,5632]{1,0:T(8,128)(2,1)S(1)}, bf16[64,5632]{1,0:T(8,128)(2,1)S(1)}, u32[]{:S(2)}, u32[]{:S(2)}) %collective-permute-start.63) | collective-permute-done | bytes 720928 | tf_op jit(solution)/shard_map/ppermute | solution.py:717
  530.5 12.8 %collective-permute-done.56 = bf16[128,3200]{1,0:T(8,128)(2,1)S(1)} collective-permute-done((bf16[128,3200]{1,0:T(8,128)(2,1)S(1)}, bf16[128,3200]{1,0:T(8,128)(2,1)S(1)}, u32[]{:S(2)}, u32[]{:S(2)}) %collective-permute-start.56) | collective-permute-done | bytes 819232 | tf_op jit(solution)/shard_map/ppermute | solution.py:717
  546.6 27.8 %collective-permute-done.66 = bf16[128,5632]{1,0:T(8,128)(2,1)} collective-permute-done((bf16[128,5632]{1,0:T(8,128)(2,1)S(1)}, bf16[128,5632]{1,0:T(8,128)(2,1)}, u32[]{:S(2)}, u32[]{:S(2)}) %collective-permute-start.66) | collective-permute-done | bytes 1441824 | tf_op jit(solution)/shard_map/ppermute | solution.py:717
  579.1 6.8 add_convert_fusion.3
  585.9 7.7 %collective-permute-start.43 = (bf16[512,1024]{1,0:T(8,128)(2,1)S(1)}, bf16[512,1024]{1,0:T(8,128)(2,1)S(1)}, u32[]{:S(2)}, u32[]{:S(2)}) collective-permute-start(bf16[512,1024]{1,0:T(8,128)(2,1)S(1)} %add_convert_fusion.3), channel_id=1, source_target_pairs={{0,0},{1,1},{2,4},{3,5},{4,2},{5,3},{6,6},{7,7},{8,8},{9,9},{10,12... | collective-permute-start | bytes 3145736 | tf_op jit(solution)/shard_map/ppermute | solution.py:717
  597.4 50.2 %collective-permute-done.43 = bf16[512,1024]{1,0:T(8,128)(2,1)S(1)} collective-permute-done((bf16[512,1024]{1,0:T(8,128)(2,1)S(1)}, bf16[512,1024]{1,0:T(8,128)(2,1)S(1)}, u32[]{:S(2)}, u32[]{:S(2)}) %collective-permute-start.43) | collective-permute-done | bytes 1048608 | tf_op jit(solution)/shard_map/ppermute | solution.py:717
  647.6 11.2 %collective-permute-done.51 = bf16[512,1024]{1,0:T(8,128)(2,1)S(1)} collective-permute-done((bf16[512,1024]{1,0:T(8,128)(2,1)S(1)}, bf16[512,1024]{1,0:T(8,128)(2,1)S(1)}, u32[]{:S(2)}, u32[]{:S(2)}) %collective-permute-start.51) | collective-permute-done | bytes 1048608 | tf_op jit(solution)/shard_map/ppermute | solution.py:717
  (405 shorter events, 285.5 us)
Async XLA Ops:
  7.2 143.9 %all-gather.3.cloned.1.call-start = ((), (), s32[]{:S(2)}) async-start(), calls=%async_computation.4 | async-start | bytes 2129920 | tf_op jit(solution)/shard_map/all_gather | solution.py:723
  9.5 91.5 %collective-permute-start.16 = (bf16[128,1024]{0,1:T(8,128)(2,1)}, bf16[128,1024]{0,1:T(8,128)(2,1)}, u32[]{:S(2)}, u32[]{:S(2)}) collective-permute-start(bf16[128,1024]{0,1:T(8,128)(2,1)} %pad_maximum_fusion.18), channel_id=1, source_target_pairs={{0,3},{1,0},{2,1},{3,2},{4,7},{5,4},{6,5},{7,6},{8,11},{9,8},{10,9... | collective-permute-start | bytes 786440 | tf_op jit(solution)/shard_map/ppermute | solution.py:717
  13.7 90.1 %collective-permute-start.14 = (bf16[128,1024]{0,1:T(8,128)(2,1)}, bf16[128,1024]{0,1:T(8,128)(2,1)}, u32[]{:S(2)}, u32[]{:S(2)}) collective-permute-start(bf16[128,1024]{0,1:T(8,128)(2,1)} %pad_maximum_fusion.18), channel_id=1, source_target_pairs={{0,1},{1,2},{2,3},{3,0},{4,5},{5,6},{6,7},{7,4},{8,9},{9,10},{10,1... | collective-permute-start | bytes 786440 | tf_op jit(solution)/shard_map/ppermute | solution.py:717
  34.7 625.7 %reduce-scatter.7.cloned.1.call-start = ((), (), s32[]{:S(2)}) async-start(), calls=%async_computation.5 | async-start | bytes 368640 | tf_op jit(solution)/shard_map/reduce_scatter | solution.py:854
  55.2 55.6 %collective-permute-start.34 = (bf16[352,1024]{1,0:T(8,128)(2,1)S(1)}, bf16[352,1024]{1,0:T(8,128)(2,1)}, u32[]{:S(2)}, u32[]{:S(2)}) collective-permute-start(bf16[352,1024]{1,0:T(8,128)(2,1)S(1)} %all_gather.15.refs_1_), channel_id=1, source_target_pairs={{0,8},{1,9},{2,10},{3,11},{4,12},{5,13},{6,14},{7,15},{8,0},{9,1},... | collective-permute-start | bytes 2162696 | tf_op jit(solution)/shard_map/ppermute | solution.py:717
  59.7 59.2 %collective-permute-start.35 = (bf16[352,1024]{1,0:T(8,128)(2,1)S(1)}, bf16[352,1024]{1,0:T(8,128)(2,1)}, u32[]{:S(2)}, u32[]{:S(2)}) collective-permute-start(bf16[352,1024]{1,0:T(8,128)(2,1)S(1)} %all_gather.15.refs_1_), channel_id=1, source_target_pairs={{0,16},{1,17},{2,18},{3,19},{4,20},{5,21},{6,22},{7,23},{8,24},{9,... | collective-permute-start | bytes 2162696 | tf_op jit(solution)/shard_map/ppermute | solution.py:717
  151.1 54.0 %collective-permute-start.25 = (bf16[128,6656]{1,0:T(8,128)(2,1)}, bf16[128,6656]{1,0:T(8,128)(2,1)S(1)}, u32[]{:S(2)}, u32[]{:S(2)}) collective-permute-start(bf16[128,6656]{1,0:T(8,128)(2,1)} %all-gather.3.cloned.1.call-done.refs_1_), channel_id=1, source_target_pairs={{0,8},{1,9},{2,10},{3,11},{4,12},{5,13},{6,14},{7,15},{8,0},{9,1},... | collective-permute-start | bytes 5111816 | tf_op jit(solution)/shard_map/ppermute | solution.py:717
  167.1 48.9 %collective-permute-start.26 = (bf16[128,6656]{1,0:T(8,128)(2,1)}, bf16[128,6656]{1,0:T(8,128)(2,1)S(1)}, u32[]{:S(2)}, u32[]{:S(2)}) collective-permute-start(bf16[128,6656]{1,0:T(8,128)(2,1)} %all-gather.3.cloned.1.call-done.refs_1_), channel_id=1, source_target_pairs={{0,16},{1,17},{2,18},{3,19},{4,20},{5,21},{6,22},{7,23},{8,24},{9,... | collective-permute-start | bytes 5111816 | tf_op jit(solution)/shard_map/ppermute | solution.py:717
  177.0 49.6 %collective-permute-start.39 = (bf16[352,1024]{1,0:T(8,128)(2,1)}, bf16[352,1024]{1,0:T(8,128)(2,1)}, u32[]{:S(2)}, u32[]{:S(2)}) collective-permute-start(bf16[352,1024]{1,0:T(8,128)(2,1)} %collective-permute-done.34.refs_2_), channel_id=1, source_target_pairs={{0,4},{1,5},{2,6},{3,7},{4,0},{5,1},{6,2},{7,3},{8,12},{9,13},{10,... | collective-permute-start | bytes 2162696 | tf_op jit(solution)/shard_map/ppermute | solution.py:717
  216.0 54.7 %collective-permute-start.40 = (bf16[352,1024]{1,0:T(8,128)(2,1)}, bf16[352,1024]{1,0:T(8,128)(2,1)}, u32[]{:S(2)}, u32[]{:S(2)}) collective-permute-start(bf16[352,1024]{1,0:T(8,128)(2,1)} %collective-permute-done.35.refs_3_), channel_id=1, source_target_pairs={{0,4},{1,5},{2,6},{3,7},{4,0},{5,1},{6,2},{7,3},{8,12},{9,13},{10,... | collective-permute-start | bytes 2162696 | tf_op jit(solution)/shard_map/ppermute | solution.py:717
  226.6 44.8 %collective-permute-start.41 = (bf16[176,1024]{1,0:T(8,128)(2,1)}, bf16[176,1024]{1,0:T(8,128)(2,1)S(1)}, u32[]{:S(2)}, u32[]{:S(2)}) collective-permute-start(bf16[176,1024]{1,0:T(8,128)(2,1)} %collective-permute-done.36.refs_4_), channel_id=1, source_target_pairs={{0,4},{1,5},{2,6},{3,7},{4,0},{5,1},{6,2},{7,3},{8,12},{9,13},{10,... | collective-permute-start | bytes 1081352 | tf_op jit(solution)/shard_map/ppermute | solution.py:717
  226.6 45.5 %collective-permute-start.42 = (bf16[176,1024]{1,0:T(8,128)(2,1)}, bf16[176,1024]{1,0:T(8,128)(2,1)S(1)}, u32[]{:S(2)}, u32[]{:S(2)}) collective-permute-start(bf16[176,1024]{1,0:T(8,128)(2,1)} %collective-permute-done.37.refs_5_), channel_id=1, source_target_pairs={{0,4},{1,5},{2,6},{3,7},{4,0},{5,1},{6,2},{7,3},{8,12},{9,13},{10,... | collective-permute-start | bytes 1081352 | tf_op jit(solution)/shard_map/ppermute | solution.py:717
  227.1 63.9 %collective-permute-start.27 = (bf16[64,6656]{1,0:T(8,128)(2,1)}, bf16[64,6656]{1,0:T(8,128)(2,1)}, u32[]{:S(2)}, u32[]{:S(2)}) collective-permute-start(bf16[64,6656]{1,0:T(8,128)(2,1)} %slice.298), channel_id=1, source_target_pairs={{0,16},{1,17},{2,18},{3,19},{4,20},{5,21},{6,22},{7,23},{8,24},{9,... | collective-permute-start | bytes 2555912 | tf_op jit(solution)/shard_map/ppermute | solution.py:717
  240.1 51.1 %collective-permute-start.28 = (bf16[64,6656]{1,0:T(8,128)(2,1)}, bf16[64,6656]{1,0:T(8,128)(2,1)}, u32[]{:S(2)}, u32[]{:S(2)}) collective-permute-start(bf16[64,6656]{1,0:T(8,128)(2,1)} %slice.299), channel_id=1, source_target_pairs={{0,8},{1,9},{2,10},{3,11},{4,12},{5,13},{6,14},{7,15},{8,0},{9,1},... | collective-permute-start | bytes 2555912 | tf_op jit(solution)/shard_map/ppermute | solution.py:717
  347.2 99.6 %collective-permute-start.57 = (bf16[4,128,1152]{2,1,0:T(8,128)(2,1)}, bf16[4,128,1152]{2,1,0:T(8,128)(2,1)S(1)}, u32[]{:S(2)}, u32[]{:S(2)}) collective-permute-start(bf16[4,128,1152]{2,1,0:T(8,128)(2,1)} %pad_maximum_fusion.6), channel_id=1, source_target_pairs={{0,4},{1,5},{2,6},{3,7},{4,0},{5,1},{6,2},{7,3},{8,12},{9,13},{10,... | collective-permute-start | bytes 3538952 | tf_op jit(solution)/shard_map/ppermute | solution.py:717
  354.3 148.3 %collective-permute-start.62 = (bf16[4,128,5632]{2,1,0:T(8,128)(2,1)}, bf16[4,128,5632]{2,1,0:T(8,128)(2,1)}, u32[]{:S(2)}, u32[]{:S(2)}) collective-permute-start(bf16[4,128,5632]{2,1,0:T(8,128)(2,1)} %pad_maximum_fusion), channel_id=1, source_target_pairs={{0,4},{1,5},{2,6},{3,7},{4,0},{5,1},{6,2},{7,3},{8,12},{9,13},{10,... | collective-permute-start | bytes 17301512 | tf_op jit(solution)/shard_map/ppermute | solution.py:717
  411.8 47.7 %collective-permute-start.67 = (bf16[4,352,1024]{2,1,0:T(8,128)(2,1)}, bf16[4,352,1024]{2,1,0:T(8,128)(2,1)}, u32[]{:S(2)}, u32[]{:S(2)}) collective-permute-start(bf16[4,352,1024]{2,1,0:T(8,128)(2,1)} %dynamic-slice_bitcast_fusion.2), channel_id=1, source_target_pairs={{0,4},{1,5},{2,6},{3,7},{4,0},{5,1},{6,2},{7,3},{8,12},{9,13},{10,... | collective-permute-start | bytes 8650760 | tf_op jit(solution)/shard_map/ppermute | solution.py:717
  468.5 194.9 %reduce-scatter.11.cloned.1.call-start = ((), (), s32[]{:S(2)}) async-start(), calls=%async_computation.7 | async-start | bytes 901120 | tf_op jit(solution)/shard_map/reduce_scatter | solution.py:854
  494.6 170.5 %reduce-scatter.13.cloned.1.call-start = ((), (), s32[]{:S(2)}) async-start(), calls=%async_computation.8 | async-start | bytes 1024000
  528.3 46.0 %collective-permute-start.66 = (bf16[128,5632]{1,0:T(8,128)(2,1)S(1)}, bf16[128,5632]{1,0:T(8,128)(2,1)}, u32[]{:S(2)}, u32[]{:S(2)}) collective-permute-start(bf16[128,5632]{1,0:T(8,128)(2,1)S(1)} %pad_maximum_fusion.4), channel_id=1, source_target_pairs={{0,16},{1,17},{2,18},{3,19},{4,20},{5,21},{6,22},{7,23},{8,24},{9,... | collective-permute-start | bytes 4325384 | tf_op jit(solution)/shard_map/ppermute | solution.py:717
  530.1 45.1 %collective-permute-start.64 = (bf16[128,5632]{1,0:T(8,128)(2,1)}, bf16[128,5632]{1,0:T(8,128)(2,1)}, u32[]{:S(2)}, u32[]{:S(2)}) collective-permute-start(bf16[128,5632]{1,0:T(8,128)(2,1)} %pad_maximum_fusion.3), channel_id=1, source_target_pairs={{0,8},{1,9},{2,10},{3,11},{4,12},{5,13},{6,14},{7,15},{8,0},{9,1},... | collective-permute-start | bytes 4325384 | tf_op jit(solution)/shard_map/ppermute | solution.py:717
  546.5 123.3 %reduce-scatter.9.cloned.1.call-start = ((), (), s32[]{:S(2)}) async-start(), calls=%async_computation.6 | async-start | bytes 1802240 | tf_op jit(solution)/shard_map/reduce_scatter | solution.py:854
  585.9 61.7 %collective-permute-start.43 = (bf16[512,1024]{1,0:T(8,128)(2,1)S(1)}, bf16[512,1024]{1,0:T(8,128)(2,1)S(1)}, u32[]{:S(2)}, u32[]{:S(2)}) collective-permute-start(bf16[512,1024]{1,0:T(8,128)(2,1)S(1)} %add_convert_fusion.3), channel_id=1, source_target_pairs={{0,0},{1,1},{2,4},{3,5},{4,2},{5,3},{6,6},{7,7},{8,8},{9,9},{10,12... | collective-permute-start | bytes 3145736 | tf_op jit(solution)/shard_map/ppermute | solution.py:717
  595.5 63.4 %collective-permute-start.51 = (bf16[512,1024]{1,0:T(8,128)(2,1)S(1)}, bf16[512,1024]{1,0:T(8,128)(2,1)S(1)}, u32[]{:S(2)}, u32[]{:S(2)}) collective-permute-start(bf16[512,1024]{1,0:T(8,128)(2,1)S(1)} %fusion.16), channel_id=1, source_target_pairs={{0,0},{1,1},{2,4},{3,5},{4,2},{5,3},{6,6},{7,7},{8,8},{9,9},{10,12... | collective-permute-start | bytes 3145736 | tf_op jit(solution)/shard_map/ppermute | solution.py:717
  (116 other events, 2421.9 us)
Sparse Core Ops, SparseCore 0:
  34.8 60.0 all-gather.2
  468.7 18.1 reduce-scatter.6
  494.7 26.6 reduce-scatter.10
  546.6 31.1 reduce-scatter.12
  580.0 44.0 reduce-scatter.8

commit v2 on v0

--- a/solution.py
+++ b/solution.py
@@ -1,8 +1,11 @@
+import functools
 import math
 
 import jax
 import jax.numpy as jnp
 from jax import lax
+from jax.experimental import pallas as pl
+from jax.experimental.pallas import tpu as pltpu
 from jax.sharding import PartitionSpec as P
 
 HEADS = 8
@@ -369,6 +372,717 @@
     )
 
 
+LINE = ("doc", "seq")
+MXU = dict(preferred_element_type=jnp.float32)
+LOG2E = 1.4426950408889634
+
+
+def dot_nt(left, right):
+    return lax.dot_general(left, right, (((1,), (1,)), ((), ())), **MXU)
+
+
+def dot_tn(left, right):
+    return lax.dot_general(left, right, (((0,), (0,)), ((), ())), **MXU)
+
+
+def dot_nn(left, right):
+    return jnp.dot(left, right, **MXU)
+
+
+def whole(count):
+    return [pl.BlockSpec(memory_space=pltpu.VMEM)] * count
+
+
+def hbm(count):
+    return [pl.BlockSpec(memory_space=pl.ANY)] * count
+
+
+def smem():
+    return pl.BlockSpec(memory_space=pltpu.SMEM)
+
+
+def place_rows(quarter, rel, rows_q):
+    return pl.ds(pl.multiple_of((quarter ^ rel) * rows_q, rows_q), rows_q)
+
+
+def stack_memory(pieces, head, keys_ref, vals_ref):
+    count = keys_ref.shape[0] // (2 * len(pieces))
+    span = pieces[0].shape[1] // 4
+    at = 0
+    for piece in pieces:
+        for part in (0, 2):
+            left = part * span + head * HEAD_DIM
+            keys_ref[at : at + count, :] = piece[:count, left : left + HEAD_DIM]
+            vals_ref[at : at + count, :] = piece[:count, left + span : left + span + HEAD_DIM]
+            at += count
+
+
+def fetch(sources, targets, sems):
+    copies = [
+        pltpu.make_async_copy(source, target, sems.at[index])
+        for index, (source, target) in enumerate(zip(sources, targets))
+    ]
+    for copy in copies:
+        copy.start()
+    return copies
+
+
+def attend_kernel(head, n_in, *refs):
+    place = refs[0]
+    given, refs = refs[1 : 1 + n_in], refs[1 + n_in :]
+    n_kept = n_in - 10
+    saved, outs, refs = refs[:6], refs[6 : 6 + 4 * n_kept], refs[6 + 4 * n_kept :]
+    held, refs = refs[:n_in], refs[n_in:]
+    b0, b1, b2, b3, m0, m1, m2, m3, cos_ref, sin_ref = held[:10]
+    kept = held[10:]
+    qr_ref, qm_ref, kr_ref, v_ref, att_ref, lse_ref = refs[:6]
+    max_s, sum_s, acc_s, mkey, mval, in_sems, out_sems = refs[6:]
+    quarter, flag = place[0], place[1]
+    rows_q = b0.shape[0]
+    tiles = qr_ref.shape[0] // rows_q
+    scale2 = LOG2E / math.sqrt(HEAD_DIM)
+    half = HEAD_DIM // 2
+    low = jnp.bfloat16
+
+    for copy in fetch(given, held, in_sems):
+        copy.wait()
+    stack_memory((m0, m1, m2, m3), head, mkey, mval)
+    for rel, block in enumerate((b0, b1, b2, b3)):
+        rows = place_rows(quarter, rel, rows_q)
+        turned = pl.ds(rel * rows_q, rows_q)
+        cos_t, sin_t = cos_ref[turned, :], sin_ref[turned, :]
+        query = block[:, :HEAD_DIM]
+        qm_ref[rows, :] = query
+        wide = query.astype(jnp.float32)
+        qr_ref[rows, :] = (wide * cos_t + pltpu.roll(wide, half, 1) * sin_t).astype(low)
+        wide = block[:, HEAD_DIM : 2 * HEAD_DIM].astype(jnp.float32)
+        kr_ref[rows, :] = (wide * cos_t + pltpu.roll(wide, half, 1) * sin_t).astype(low)
+        v_ref[rows, :] = block[:, 2 * HEAD_DIM :]
+    leaving = fetch((qr_ref, qm_ref, kr_ref, v_ref), saved[:4], out_sems)
+
+    def fold(scores, values):
+        old_max = max_s[...]
+        new_max = jnp.maximum(old_max, jnp.max(scores, 1, keepdims=True))
+        spread = jnp.concatenate([new_max] * (scores.shape[1] // HEAD_DIM), 1)
+        weights = jnp.exp2((scores - spread) * scale2)
+        shrink = jnp.exp2((old_max - new_max) * scale2)
+        sum_s[...] = sum_s[...] * shrink + jnp.sum(weights, 1, keepdims=True)
+        acc_s[...] = acc_s[...] * shrink + dot_nn(weights.astype(low), values)
+        max_s[...] = new_max
+
+    def tile(index, carry):
+        rows = pl.ds(pl.multiple_of(index * rows_q, rows_q), rows_q)
+        query = qr_ref[rows, :]
+        max_s[...] = jnp.full_like(max_s, NEG_FILL)
+        sum_s[...] = jnp.zeros_like(sum_s)
+        acc_s[...] = jnp.zeros_like(acc_s)
+
+        def earlier(block, inner):
+            keys = pl.ds(pl.multiple_of(block * rows_q, rows_q), rows_q)
+            fold(dot_nt(query, kr_ref[keys, :]), v_ref[keys, :])
+            return inner
+
+        lax.fori_loop(0, index, earlier, 0)
+        scores = dot_nt(query, kr_ref[rows, :])
+        row_i = lax.broadcasted_iota(jnp.int32, scores.shape, 0)
+        col_i = lax.broadcasted_iota(jnp.int32, scores.shape, 1)
+        fold(jnp.where(col_i <= row_i, scores, NEG_FILL), v_ref[rows, :])
+
+        @pl.when(flag > 0)
+        def _():
+            plain = qm_ref[rows, :]
+            for at in range(0, mkey.shape[0], rows_q):
+                fold(dot_nt(plain, mkey[at : at + rows_q, :]), mval[at : at + rows_q, :])
+
+        total = sum_s[...]
+        att_ref[rows, :] = (acc_s[...] / total).astype(low)
+        lse = max_s[...] * scale2 + jnp.log(total) * LOG2E
+        lse_ref[:, rows] = jnp.transpose(lse)[:8]
+        return carry
+
+    lax.fori_loop(0, tiles, tile, 0)
+
+    for rel in range(4 * n_kept // max(n_kept, 1)):
+        rows = place_rows(quarter, rel, rows_q)
+        for at, source in enumerate((*kept, att_ref)):
+            if n_kept:
+                outs[rel][:, at * HEAD_DIM : (at + 1) * HEAD_DIM] = source[rows, :]
+    for at, (source, target) in enumerate(((att_ref, saved[4]), (lse_ref, saved[5]))):
+        copy = pltpu.make_async_copy(source, target, out_sems.at[4 + at])
+        copy.start()
+        leaving.append(copy)
+    for copy in leaving:
+        copy.wait()
+
+
+def attend(head, place, blocks, memory, mem_rows, cos_t, sin_t, kept=()):
+    rows_q = blocks[0].shape[0]
+    length = cos_t.shape[0]
+    low = jnp.bfloat16
+    given = (*blocks, *memory, cos_t, sin_t, *kept)
+    saved = [((length, HEAD_DIM), low)] * 5 + [((8, length), jnp.float32)]
+    part = jax.ShapeDtypeStruct((rows_q, (len(kept) + 1) * HEAD_DIM), low)
+    n_out = 4 if kept else 0
+    return pl.pallas_call(
+        functools.partial(attend_kernel, head, len(given)),
+        out_shape=[jax.ShapeDtypeStruct(*kind) for kind in saved] + [part] * n_out,
+        in_specs=[smem()] + hbm(len(given)),
+        out_specs=hbm(6) + whole(n_out),
+        scratch_shapes=[pltpu.VMEM(array.shape, array.dtype) for array in given]
+        + [pltpu.VMEM(*kind) for kind in saved]
+        + [pltpu.VMEM((rows_q, HEAD_DIM), jnp.float32)] * 3
+        + [pltpu.VMEM((mem_rows, HEAD_DIM), low)] * 2
+        + [pltpu.SemaphoreType.DMA((len(given),)), pltpu.SemaphoreType.DMA((6,))],
+        compiler_params=pltpu.CompilerParams(vmem_limit_bytes=24 << 20),
+        cost_estimate=pl.CostEstimate(flops=1, bytes_accessed=1, transcendentals=0),
+        name="attend",
+    )(place, *given)
+
+
+def attend_back_kernel(head, n_in, *refs):
+    place = refs[0]
+    given, refs = refs[1 : 1 + n_in], refs[1 + n_in :]
+    g0, g1, g2, g3 = refs[:4]
+    held, refs = refs[4 : 4 + n_in], refs[4 + n_in :]
+    qr_ref, qm_ref, kr_ref, v_ref, att_ref, lse_ref = held[:6]
+    d0, d1, d2, d3, m0, m1, m2, m3, cos_ref, sin_ref = held[6:]
+    datt, dkey, dval, dqr, dqm, grads, mkey, mval, in_sems = refs
+    coming = fetch(given, held, in_sems)
+    quarter, flag = place[0], place[1]
+    rows_q = d0.shape[0]
+    tiles = qr_ref.shape[0] // rows_q
+    scale = 1.0 / math.sqrt(HEAD_DIM)
+    scale2 = LOG2E * scale
+    half = HEAD_DIM // 2
+    low = jnp.bfloat16
+
+    def unrotate(grad, index):
+        turned = place_rows(quarter, index, rows_q)
+        return grad * cos_ref[turned, :] - pltpu.roll(grad, half, 1) * sin_ref[turned, :]
+
+    for copy in coming:
+        copy.wait()
+    stack_memory((m0, m1, m2, m3), head, mkey, mval)
+    cols = slice(head * HEAD_DIM, (head + 1) * HEAD_DIM)
+    for rel, block in enumerate((d0, d1, d2, d3)):
+        datt[place_rows(quarter, rel, rows_q), :] = block[:, cols]
+    dkey[...] = jnp.zeros_like(dkey)
+    dval[...] = jnp.zeros_like(dval)
+
+    def tile(index, carry):
+        rows = pl.ds(pl.multiple_of(index * rows_q, rows_q), rows_q)
+        query = qr_ref[rows, :]
+        d_out = datt[rows, :]
+        delta = jnp.sum(
+            jnp.transpose(d_out.astype(jnp.float32) * att_ref[rows, :].astype(jnp.float32)),
+            0,
+            keepdims=True,
+        )
+        lse = lse_ref[0:1, rows]
+        dqr[...] = jnp.zeros_like(dqr)
+        dqm[...] = jnp.zeros_like(dqm)
+
+        def block_grads(keys, values, queries, masked):
+            power = dot_nt(keys, queries) * scale2 - lse
+            if masked:
+                key_i = lax.broadcasted_iota(jnp.int32, power.shape, 0)
+                query_i = lax.broadcasted_iota(jnp.int32, power.shape, 1)
+                power = jnp.where(key_i <= query_i, power, NEG_FILL)
+            probs = jnp.exp2(power)
+            d_scores = probs * (dot_nt(values, d_out) - delta)
+            return probs.astype(low), d_scores.astype(low)
+
+        def local(keys_at, masked):
+            keys = kr_ref[keys_at, :]
+            probs, d_scores = block_grads(keys, v_ref[keys_at, :], query, masked)
+            dval[keys_at, :] += dot_nn(probs, d_out)
+            dkey[keys_at, :] += dot_nn(d_scores, query)
+            dqr[...] += dot_tn(d_scores, keys)
+
+        def earlier(block, inner):
+            local(pl.ds(pl.multiple_of(block * rows_q, rows_q), rows_q), False)
+            return inner
+
+        lax.fori_loop(0, index, earlier, 0)
+        local(rows, True)
+
+        @pl.when(flag > 0)
+        def _():
+            plain = qm_ref[rows, :]
+            for at in range(0, mkey.shape[0], rows_q):
+                keys = mkey[at : at + rows_q, :]
+                _, d_scores = block_grads(keys, mval[at : at + rows_q, :], plain, False)
+                dqm[...] += dot_tn(d_scores, keys)
+
+        grads[rows, :HEAD_DIM] = ((unrotate(dqr[...], index) + dqm[...]) * scale).astype(low)
+        return carry
+
+    lax.fori_loop(0, tiles, tile, 0)
+    for index in range(tiles):
+        rows = pl.ds(index * rows_q, rows_q)
+        grads[rows, HEAD_DIM : 2 * HEAD_DIM] = (unrotate(dkey[rows, :], index) * scale).astype(low)
+        grads[rows, 2 * HEAD_DIM :] = dval[rows, :].astype(low)
+
+    for rel, out in enumerate((g0, g1, g2, g3)):
+        out[...] = grads[place_rows(quarter, rel, rows_q), :]
+
+
+def attend_back(head, place, saved, d_blocks, memory, mem_rows, cos_t, sin_t):
+    rows_q = d_blocks[0].shape[0]
+    length = cos_t.shape[0]
+    low, wide = jnp.bfloat16, jnp.float32
+    given = (*saved, *d_blocks, *memory, cos_t, sin_t)
+    return pl.pallas_call(
+        functools.partial(attend_back_kernel, head, len(given)),
+        out_shape=[jax.ShapeDtypeStruct((rows_q, 3 * HEAD_DIM), low)] * 4,
+        in_specs=[smem()] + hbm(len(given)),
+        out_specs=whole(4),
+        scratch_shapes=[pltpu.VMEM(array.shape, array.dtype) for array in given]
+        + [
+            pltpu.VMEM((length, HEAD_DIM), low),
+            pltpu.VMEM((length, HEAD_DIM), wide),
+            pltpu.VMEM((length, HEAD_DIM), wide),
+            pltpu.VMEM((rows_q, HEAD_DIM), wide),
+            pltpu.VMEM((rows_q, HEAD_DIM), wide),
+            pltpu.VMEM((length, 3 * HEAD_DIM), low),
+            pltpu.VMEM((mem_rows, HEAD_DIM), low),
+            pltpu.VMEM((mem_rows, HEAD_DIM), low),
+            pltpu.SemaphoreType.DMA((len(given),)),
+        ],
+        compiler_params=pltpu.CompilerParams(vmem_limit_bytes=28 << 20),
+        cost_estimate=pl.CostEstimate(flops=1, bytes_accessed=1, transcendentals=0),
+        name="attend_back",
+    )(place, *given)
+
+
+def deal_kernel(n_heads, n_owners, wq, wk, wv, gains, out):
+    at = 0
+    for head in range(n_heads):
+        for owner in range(n_owners):
+            left = (owner * n_heads + head) * HEAD_DIM
+            for weight in (wq, wk, wv):
+                out[:, at : at + HEAD_DIM] = weight[:, left : left + HEAD_DIM]
+                at += HEAD_DIM
+    out[:, at:] = gains[...]
+
+
+def deal(n_heads, n_owners, wq, wk, wv, gains):
+    rows, width = wq.shape
+    return pl.pallas_call(
+        functools.partial(deal_kernel, n_heads, n_owners),
+        out_shape=jax.ShapeDtypeStruct((rows, 3 * width + gains.shape[1]), wq.dtype),
+        in_specs=whole(4),
+        out_specs=whole(1)[0],
+        compiler_params=pltpu.CompilerParams(vmem_limit_bytes=4 << 20),
+        cost_estimate=pl.CostEstimate(flops=1, bytes_accessed=1, transcendentals=0),
+        name="deal",
+    )(wq, wk, wv, gains)
+
+
+def join_kernel(turn, *refs):
+    where, blocks, out, sems = refs[0], refs[1:-2], refs[-2], refs[-1]
+    size = blocks[0].shape[1]
+    targets = [
+        out.at[:, pl.ds(pl.multiple_of((where[0] ^ flip) * size, HEAD_DIM), size)] for flip in turn
+    ]
+    for copy in fetch(blocks, targets, sems):
+        copy.wait()
+
+
+def join(where, turn, blocks):
+    rows, size = blocks[0].shape
+    return pl.pallas_call(
+        functools.partial(join_kernel, turn),
+        out_shape=jax.ShapeDtypeStruct((rows, len(blocks) * size), blocks[0].dtype),
+        in_specs=[smem()] + hbm(len(blocks)),
+        out_specs=hbm(1)[0],
+        scratch_shapes=[pltpu.SemaphoreType.DMA((len(blocks),))],
+        compiler_params=pltpu.CompilerParams(vmem_limit_bytes=4 << 20),
+        cost_estimate=pl.CostEstimate(flops=1, bytes_accessed=1, transcendentals=0),
+        name="join",
+    )(where, *blocks)
+
+
+def settle_kernel(rels, widths, chunks, *refs):
+    where = refs[0]
+    pieces = refs[1 : 1 + len(rels)]
+    outs = refs[1 + len(rels) : 1 + len(rels) + len(widths)]
+    sems = refs[-1]
+    rows = pieces[0].shape[0]
+    count = rows // chunks
+    copies = []
+    for piece, rel in zip(pieces, rels):
+        rel, half = rel if isinstance(rel, tuple) else (rel, 0)
+        hops = piece.shape[0] // count
+        for hop in range(hops):
+            chunk = (where[1] + chunks - half * hops - hop) % chunks
+            start = pl.multiple_of((where[0] ^ rel) * rows + chunk * count, 16)
+            left = 0
+            for out, width in zip(outs, widths):
+                copy = pltpu.make_async_copy(
+                    piece.at[pl.ds(hop * count, count), pl.ds(left, width)],
+                    out.at[pl.ds(start, count), :],
+                    sems.at[len(copies)],
+                )
+                copy.start()
+                copies.append(copy)
+                left += width
+    for copy in copies:
+        copy.wait()
+
+
+def settle(where, rels, pieces, widths, chunks):
+    low = jnp.bfloat16
+    total = sum(piece.shape[0] for piece in pieces)
+    return pl.pallas_call(
+        functools.partial(settle_kernel, rels, widths, chunks),
+        out_shape=[jax.ShapeDtypeStruct((total, width), low) for width in widths],
+        in_specs=[smem()] + hbm(len(pieces)),
+        out_specs=hbm(len(widths)),
+        scratch_shapes=[pltpu.SemaphoreType.DMA((len(pieces) * chunks * len(widths),))],
+        compiler_params=pltpu.CompilerParams(vmem_limit_bytes=4 << 20),
+        cost_estimate=pl.CostEstimate(flops=1, bytes_accessed=1, transcendentals=0),
+        name="settle",
+    )(where, *pieces)
+
+
+def segment_pairs(n_doc, n_seq):
+    places = [(d, z) for d in range(n_doc) for z in range(n_seq)]
+
+    def route(target):
+        pairs = [(d * n_seq + z, target(d, z)[0] * n_seq + target(d, z)[1]) for d, z in places]
+        return [(source, goal) for source, goal in pairs if source != goal]
+
+    def regroup(rel):
+        def target(d, z):
+            spot = z ^ rel
+            return ((d & ~1) | (spot >> 1), 2 * (d & 1) + (spot & 1))
+
+        return target
+
+    routes = {
+        "core": route(lambda d, z: (d ^ 1, z)),
+        "x": route(lambda d, z: (d ^ 2, z)),
+        "y": route(lambda d, z: (d ^ 4, z)),
+        "xy": route(lambda d, z: (d ^ 6, z)),
+        "z1": route(lambda d, z: (d, (z + 1) % n_seq)),
+        "z2": route(lambda d, z: (d, (z + 2) % n_seq)),
+        "z3": route(lambda d, z: (d, (z + 3) % n_seq)),
+    }
+    for rel in range(n_seq):
+        routes["group", rel] = route(regroup(rel))
+        routes["part", rel] = route(
+            lambda d, z, rel=rel: (d ^ (rel >> 1), z ^ (rel & 1))
+        )
+    return routes
+
+
+def later(values, *others):
+    return lax.optimization_barrier((values, others))[0]
+
+
+def on_pair(
+    routes,
+    tokens,
+    w_query,
+    w_key,
+    w_value,
+    w_out,
+    w_gate,
+    w_up,
+    w_down,
+    gain_attn,
+    gain_ffn,
+    cache_keys,
+    cache_values,
+    memory_flags,
+    memory_source,
+    positions,
+    out_grad,
+):
+    low, wide = jnp.bfloat16, jnp.float32
+    n_doc, n_seq = lax.axis_size("doc"), lax.axis_size("seq")
+    d, z = lax.axis_index("doc"), lax.axis_index("seq")
+    core, odd, pair, plane = d & 1, z & 1, z >> 1, d >> 1
+    quarter = 2 * core + odd
+    heads_at = 2 * odd + core
+    turn = (0, 2, 1, 3)
+    width = tokens.shape[2]
+    ff_width = w_gate.shape[1]
+    share = width // n_seq
+    n_heads = share // HEAD_DIM
+    where = jnp.stack([d, z]).astype(jnp.int32)
+    mem_rows = 2 * n_seq * cache_keys.shape[1]
+
+    def move(array, name):
+        return lax.ppermute(array, LINE, routes[name])
+
+    def to_group(array, rel=0):
+        moved = move(array, ("group", rel))
+        return moved if rel else jnp.where(pair == core, array, moved)
+
+    def pick(array, index, axis=0):
+        return lax.dynamic_index_in_dim(array, index, axis, keepdims=False)
+
+    def plus(*terms):
+        total = terms[0].astype(wide)
+        for term in terms[1:]:
+            total = total + term.astype(wide)
+        return total.astype(low)
+
+    def along_z(shard):
+        return [shard] + [move(shard, f"z{hop}") for hop in range(1, n_seq)]
+
+    def in_plane(block):
+        return [block, move(block, "x"), move(block, "y"), move(block, "xy")]
+
+    def swap_halves(pieces):
+        cut = pieces[1].shape[0] // 2
+        return [move(pieces[1][:cut], "y"), move(pieces[2][cut:], "x")]
+
+    def other_core(pieces):
+        return pieces + [move(piece, "core") for piece in pieces]
+
+    rels = (0, 2, 4, 6, 1, 3, 5, 7)
+
+    def part_for(array, rel, size):
+        return lax.dynamic_slice_in_dim(array, (heads_at ^ turn[rel]) * size, size, 1)
+
+    heads_where = heads_at.astype(jnp.int32).reshape(1)
+
+    def spread(blocks):
+        return join(heads_where, turn, blocks)
+
+    def exchange(blocks):
+        return [blocks[0]] + [move(blocks[rel], ("part", rel)) for rel in range(1, n_seq)]
+
+    gains = jnp.concatenate([gain_attn[:, None], gain_ffn[:, None]], 1)
+    gains = jnp.pad(gains, ((0, 0), (0, HEAD_DIM - 2)))
+    lines = along_z(deal(n_heads, n_seq, w_query, w_key, w_value, gains))
+
+    own_kv = jnp.concatenate([cache_keys[0], cache_values[0]], 1)
+    two = jnp.stack([own_kv, move(own_kv, "x")])
+    notes = jnp.concatenate([memory_flags, memory_source])
+    notes_core, notes_y = later((move(notes, "core"), move(notes, "y")), two)
+    flag = jnp.where(pair == core, notes[0], notes_core[0])
+    source, source_y = notes[1], notes_y[1]
+    place = jnp.stack([quarter, flag]).astype(jnp.int32)
+    pos = [to_group(later(positions[0], two), rel) for rel in range(n_seq)]
+
+    four = jnp.concatenate([two, move(two, "core")])
+
+    def spot(src):
+        return 2 * ((src ^ d) & 1) + (((src ^ d) >> 1) & 1)
+
+    for_y = pick(four, spot(source_y))
+    from_y = move(for_y, "y")
+    block = jnp.concatenate(later(lines, for_y))
+    rows = block.shape[0]
+    projections = in_plane(block)
+    lines_ab = along_z(later(jnp.concatenate([w_out, w_gate, w_up], 1), block))
+    from_y = later(from_y, block)
+    src_kv = jnp.where(((source ^ d) >> 2) == 0, pick(four, spot(source)), from_y)
+
+    def heads_for(rel):
+        to = z ^ rel
+        at = (2 * (to & 1) + (to >> 1)) * share
+        picked = [
+            lax.dynamic_slice_in_dim(kv, side * width + at, share, 1)
+            for kv in (own_kv, src_kv)
+            for side in (0, 1)
+        ]
+        return jnp.concatenate(picked, 1)
+
+    parts = [heads_for(rel) for rel in range(n_seq)]
+    cos_h, sin_h = rotary_tables(jnp.concatenate(later(pos, parts)))
+    cos_t = jnp.concatenate([cos_h, cos_h], -1)
+    sin_t = jnp.concatenate([-sin_h, sin_h], -1)
+    block_ab = jnp.concatenate(later(lines_ab, cos_t, sin_t))
+    tok = to_group(later(tokens[0], block_ab))
+    projections = later(projections, block_ab)
+    pieces_ab = in_plane(later(block_ab, projections))[:3]
+    *w_heads, gain_cols = settle(
+        where,
+        rels,
+        other_core(projections),
+        (3 * n_seq * HEAD_DIM,) * n_heads + (HEAD_DIM,),
+        n_seq,
+    )
+    gain_a = gain_cols[:, 0].astype(wide)
+    gain_f = gain_cols[:, 1].astype(wide)
+
+    inputs = later(tok, w_heads).astype(wide)
+    factor_one = rms_factor(inputs)
+    normed_one = inputs * factor_one
+    attn_in = (normed_one * gain_a).astype(low)
+
+    def projected(head, *others):
+        weight = later(w_heads[head], *others) if others else w_heads[head]
+        qkv = dot_nn(attn_in, weight).astype(low)
+        return [part_for(qkv, rel, 3 * HEAD_DIM) for rel in range(n_seq)]
+
+    first = projected(0)
+    first_own = first[0]
+    first = exchange(first)
+    parts = later(parts, first_own)
+    memory = [to_group(part, rel) for rel, part in enumerate(parts)]
+    second = projected(1, parts)
+    second_own = second[0]
+    second = exchange(second)
+    pieces_ab = later(pieces_ab, second_own)
+    far_ab = swap_halves(pieces_ab)
+    first, memory = later((first, memory), pieces_ab)
+    saved_0 = attend(0, place, first, memory, mem_rows, cos_t, sin_t)
+    att_0 = saved_0[4]
+    lines_c = along_z(later(w_down, att_0))
+    *saved_1, o0, o1, o2, o3 = attend(
+        1, place, later(second, att_0), memory, mem_rows, cos_t, sin_t, (att_0,)
+    )
+    block_c = jnp.stack(later(lines_c, o0))
+    block_c = jnp.concatenate([pick(block_c, (z - at) % n_seq) for at in range(n_seq)])
+    rows_c = block_c.shape[0]
+    att = exchange(later([o0, o1, o2, o3], block_c))
+    far_ab = later(far_ab, block_c)
+    pieces_c = in_plane(later(block_c, far_ab))
+    w_out_f, w_gate_f, w_up_f = settle(
+        where,
+        (0, 2, 4, 1, 3, 5, (6, 0), (6, 1), (7, 0), (7, 1)),
+        other_core(later(pieces_ab, block_c)) + other_core(far_ab),
+        (width, ff_width, ff_width),
+        n_seq,
+    )
+    attn_low = spread(later(att, w_out_f))
+    grad_y = to_group(later(out_grad[0], attn_low))
+    resid_mid = inputs + dot_nn(attn_low, w_out_f)
+    factor_two = rms_factor(resid_mid)
+    normed_two = resid_mid * factor_two
+    ffn_in = (normed_two * gain_f).astype(low)
+    gate_act = dot_nn(ffn_in, w_gate_f)
+    up_act = dot_nn(ffn_in, w_up_f)
+    sig_gate = jax.nn.sigmoid(gate_act)
+    silu_gate = gate_act * sig_gate
+    hidden = (silu_gate * up_act).astype(low)
+    grad_y, pieces_c = later((grad_y, pieces_c), hidden)
+
+    def side(array, which, turned=True):
+        return jnp.concatenate(
+            [
+                lax.dynamic_slice_in_dim(
+                    array, (2 * (plane ^ rel if turned else rel) + which) * rows, rows, 1
+                )
+                for rel in range(n_doc // 2)
+            ],
+            1,
+        )
+
+    def met_in_plane(both):
+        size = both.shape[0] // (n_doc // 2)
+        parts = [both[rel * size : (rel + 1) * size] for rel in range(n_doc // 2)]
+        return [parts[0]] + [move(parts[rel + 1], name) for rel, name in enumerate(("x", "y", "xy"))]
+
+    def finish_by_hops(total):
+        chunks = total.reshape(n_seq, -1, total.shape[1])
+        return sum(
+            (
+                move(pick(chunks, (z + hop) % n_seq), f"z{hop}").astype(wide)
+                for hop in range(1, n_seq)
+            ),
+            pick(chunks, z).astype(wide),
+        )
+
+    def kept(mine, array, met):
+        return (dot_tn(mine, array) + met.astype(wide)).astype(low)
+
+    pieces_c = other_core(pieces_c)
+    grad_down = dot_tn(hidden, grad_y).astype(low).reshape(n_doc // 2, 2, rows_c, width)
+    down_sent = pick(grad_down, 1 - core, 1)
+    met_down = move(down_sent, "core")
+    (w_down_f,) = settle(where, rels, later(pieces_c, down_sent), (width,), 1)
+    d_hidden = dot_nt(grad_y, w_down_f)
+    d_gate = (d_hidden * up_act * (sig_gate * (1.0 + gate_act * (1.0 - sig_gate)))).astype(low)
+    d_up = (d_hidden * silu_gate).astype(low)
+    d_ffn_in = dot_nt(d_gate, w_gate_f) + dot_nt(d_up, w_up_f)
+    d_mid = grad_y.astype(wide) + norm_back(d_ffn_in * gain_f, normed_two, factor_two)
+    d_branch = d_mid.astype(low)
+    d_att = dot_nt(d_branch, w_out_f).astype(low)
+    d_blocks = [part_for(d_att, rel, share) for rel in range(n_seq)]
+    d_sent = d_blocks[0]
+    d_blocks = exchange(d_blocks)
+    met_down = later(met_down, d_sent)
+    both_down = plus(pick(grad_down, core, 1), met_down)
+    both_down = jnp.concatenate([pick(both_down, plane ^ rel) for rel in range(n_doc // 2)])
+    total_down = met_in_plane(both_down)
+    away, home = side(ffn_in, 1 - core), side(ffn_in, core)
+    away_gate = dot_tn(later(away, both_down), d_gate).astype(low)
+    met_gate = move(away_gate, "core")
+    away_up = dot_tn(later(away, away_gate), d_up).astype(low)
+    met_up = move(away_up, "core")
+    d_blocks = later(d_blocks, away_up)
+    g_0 = attend_back(0, place, saved_0, d_blocks, memory, mem_rows, cos_t, sin_t)
+    d_set_0 = exchange(g_0)
+    both_gate = kept(home, d_gate, later(met_gate, g_0))
+    total_down = later(total_down, both_gate)
+    total_gate = met_in_plane(later(both_gate, total_down))
+    g_1 = attend_back(
+        1, place, saved_1, later(d_blocks, both_gate, total_down), memory, mem_rows, cos_t, sin_t
+    )
+    g_1 = later(g_1, d_set_0)
+    d_set_1 = exchange(g_1)
+
+    away, home_in = side(attn_in, 1 - core), side(attn_in, core)
+    d_qkv_0 = spread(later(d_set_0, g_1))
+    away_0 = dot_tn(away, d_qkv_0).astype(low)
+    met_0 = move(away_0, "core")
+    both_up = kept(home, d_up, later(met_up, away_0))
+    total_gate = later(total_gate, both_up)
+    total_up = met_in_plane(later(both_up, total_gate))
+    d_set_1 = later(d_set_1, both_up)
+    d_qkv_1 = spread(d_set_1)
+    away_1 = dot_tn(away, d_qkv_1).astype(low)
+    met_1 = move(away_1, "core")
+    out_down = finish_by_hops(plus(*later(total_down, away_1)))
+    both_0 = kept(home_in, d_qkv_0, later(met_0, away_1))
+    away_out = dot_tn(later(side(attn_low, 1 - core), both_0), d_branch).astype(low)
+    met_out = move(away_out, "core")
+    out_gate = finish_by_hops(plus(*later(total_gate, away_out)))
+    both_1 = kept(home_in, d_qkv_1, later(met_1, away_out))
+    layer_out = (resid_mid + dot_nn(later(hidden, both_1), w_down_f)).astype(low)
+    both_out = kept(side(attn_low, core), later(d_branch, layer_out), later(met_out, layer_out))
+    total_up = later(total_up, both_out)
+    last = met_in_plane(later(jnp.concatenate([both_0, both_1, both_out], 1), total_up))
+    d_attn_in = dot_nt(later(d_qkv_0, total_up), w_heads[0]) + dot_nt(
+        later(d_qkv_1, total_up), w_heads[1]
+    )
+    layer_out = to_group(later(layer_out, total_up))
+    grad_in = d_mid + norm_back(d_attn_in * gain_a, normed_one, factor_one)
+    grad_in = grad_in.astype(low)
+    grad_tokens = to_group(grad_in).astype(wide)
+    out_up = finish_by_hops(plus(*later(total_up, grad_in)))
+    both = finish_by_hops(plus(*later(last, grad_in)))
+    out_out = both[:, 3 * width :]
+    split = both[:, : 3 * width].reshape(-1, n_heads, n_seq, 3, HEAD_DIM)
+    split = jnp.swapaxes(split, 1, 2)
+    out_q, out_k, out_v = (split[:, :, :, which].reshape(-1, width) for which in range(3))
+
+    def gain_grad(gain, pairs):
+        total = sum(jnp.sum(weight.astype(wide) * grad, 1) for weight, grad in pairs)
+        return total / gain.astype(wide)
+
+    return (
+        layer_out[None],
+        grad_tokens[None],
+        out_q,
+        out_k,
+        out_v,
+        out_out,
+        out_gate,
+        out_up,
+        out_down,
+        gain_grad(gain_attn, ((w_query, out_q), (w_key, out_k), (w_value, out_v))),
+        gain_grad(gain_ffn, ((w_gate, out_gate), (w_up, out_up))),
+    )
+
+
 def solution(mesh):
     in_specs = (
         P("doc", "seq", None),
@@ -401,6 +1115,10 @@
         P(("doc", "seq")),
         P(("doc", "seq")),
     )
+    n_doc, n_seq = mesh.shape["doc"], mesh.shape["seq"]
+    step = on_device
+    if (n_doc, n_seq) == (8, 4):
+        step = functools.partial(on_pair, segment_pairs(n_doc, n_seq))
     return jax.shard_map(
-        on_device, mesh=mesh, in_specs=in_specs, out_specs=out_specs, check_vma=False
-    )
+        step, mesh=mesh, in_specs=in_specs, out_specs=out_specs, check_vma=False
+    )

time: 2190 us -> 595 us (0.27)
  waiting for transfers between devices: 1620 us -> 170 us
  matrix products: 275 us -> 68.6 us
  starting transfers between devices: 1.1 us -> 185 us
  blocking collectives: 110 us -> 0 us
  Pallas kernels: 0 us -> 59 us
  local copies, waits for them, and re-layouts: 89 us -> 54 us
    reduce_scatter x2 -> x0, waiting for transfers between devices: 743 us -> none  [the longest x1 493 us: on_device(): lax.psum_scatter(jnp.concatenate([gate_part, up_part], 1), ('doc', 'seq')...]
    all_gather x15 -> x0, waiting for transfers between devices: 600 us -> none  [the longest x1 77.7 us: on_device(): key_part = lax.all_gather(k_rot, 'seq', axis=1, tiled=True)]
    unnamed x19 -> x0, waiting for transfers between devices: 279 us -> none
    dot_general x37 -> x23, matrix products: 275 us -> 68.6 us  [the longest x6 27.6 us: dot_nt(): return lax.dot_general(left, right, (((1,), (1,)), ((), ())), **MXU)]
    ppermute x0 -> x97, starting transfers between devices: none -> 185 us  [move(): return lax.ppermute(array, LINE, routes[name])]
    ppermute x0 -> x97, waiting for transfers between devices: none -> 170 us  [move(): return lax.ppermute(array, LINE, routes[name])]
    unnamed x2 -> x0, blocking collectives: 83.2 us -> none
    pallas_call x0 -> x11, Pallas kernels: none -> 59 us  [the longest x2 24.1 us: attend_back(): pl.pallas_call(functools.partial(attend_back_kernel, head, len(given)), o...]
  transfers between devices with their start and end apart: 18 -> 97, of which waited for: 16 -> 26; matrix products, arithmetic and copies ran while one was open for 14% -> 23% of each run, Pallas kernels for 0% -> 10%
where the time goes in v2:
time: 595 us; the launch traced here: 586 us
  starting transfers between devices  185 us (31%)
  waiting for transfers between devices  170 us (29%)
  matrix products  68.6 us (12%)
  Pallas kernels  59 us (10%)
  local copies, waits for them, and re-layouts  54 us (9%)
  other arithmetic  44.4 us (7%)
    ppermute x97, starting transfers between devices, move(): return lax.ppermute(array, LINE, routes[name])  185 us
    ppermute x97, waiting for transfers between devices, move(): return lax.ppermute(array, LINE, routes[name])  170 us
    unnamed x250, local copies, waits for them, and re-layouts  34.6 us
    dot_general x6, matrix products, dot_nt(): return lax.dot_general(left, right, (((1,), (1,)), ((), ())), **MXU)  27.6 us
    dot_general x11, matrix products, dot_tn(): return lax.dot_general(left, right, (((0,), (0,)), ((), ())), **MXU)  24.1 us
    pallas_call x2, Pallas kernels, attend_back(): pl.pallas_call(functools.partial(attend_back_kernel, head, len(given)), o...  24.1 us
    pallas_call x2, Pallas kernels, attend(): pl.pallas_call(functools.partial(attend_kernel, head, len(given)), out_sh...  20.2 us
    dot_general x6, matrix products, dot_nn(): return jnp.dot(left, right, **MXU)  16.9 us
  transfers between devices with their start and end apart: 97, of which 26 were waited for; matrix products, arithmetic and copies ran while one was open for 23% of the time, Pallas kernels for 10%

profile of v2, /device:TPU:0, one launch (start us, length us, event | category | flops | bytes accessed | tf_op | source)
XLA Modules:
  0.0 586.2 jit_solution(8056417576982616122)
XLA Ops:
  48.8 8.8 %collective-permute-start.9 = (bf16[32,6656]{1,0:T(8,128)(2,1)S(1)}, bf16[32,6656]{1,0:T(8,128)(2,1)S(1)}, u32[]{:S(2)}, u32[]{:S(2)}) collective-permute-start(bf16[32,6656]{1,0:T(8,128)(2,1)S(1)} %pad_maximum_fusion.13), channel_id=1, source_target_pairs={{0,3},{1,0},{2,1},{3,2},{4,7},{5,4},{6,5},{7,6},{8,11},{9,8},{10,9... | collective-permute-start | bytes 1277960 | tf_op jit(solution)/shard_map/ppermute | solution.py:818
  65.5 8.7 %collective-permute-done.8 = bf16[32,6656]{1,0:T(8,128)(2,1)S(1)} collective-permute-done((bf16[32,6656]{1,0:T(8,128)(2,1)S(1)}, bf16[32,6656]{1,0:T(8,128)(2,1)S(1)}, u32[]{:S(2)}, u32[]{:S(2)}) %collective-permute-start.8) | collective-permute-done | bytes 426016 | tf_op jit(solution)/shard_map/ppermute | solution.py:818
  80.7 14.7 %collective-permute-done.17.refs_3_ = bf16[128,3200]{1,0:T(8,128)(2,1)} collective-permute-done((bf16[128,3200]{1,0:T(8,128)(2,1)S(1)}, bf16[128,3200]{1,0:T(8,128)(2,1)}, u32[]{:S(2)}, u32[]{:S(2)}) %collective-permute-start.17) | collective-permute-done | bytes 819232 | tf_op jit(solution)/shard_map/ppermute | solution.py:818
  112.9 18.1 %collective-permute-start.31 = (bf16[128,1024]{1,0:T(8,128)(2,1)S(1)}, bf16[128,1024]{1,0:T(8,128)(2,1)S(1)}, u32[]{:S(2)}, u32[]{:S(2)}) collective-permute-start(bf16[128,1024]{1,0:T(8,128)(2,1)S(1)} %copy-done.94), channel_id=1, source_target_pairs={{0,4},{1,5},{2,0},{3,1},{4,6},{5,7},{6,2},{7,3},{8,12},{9,13},{10,... | collective-permute-start | bytes 786440 | tf_op jit(solution)/shard_map/ppermute | solution.py:818
  131.0 9.4 %collective-permute-start.32 = (bf16[128,1024]{1,0:T(8,128)(2,1)S(1)}, bf16[128,1024]{1,0:T(8,128)(2,1)S(1)}, u32[]{:S(2)}, u32[]{:S(2)}) collective-permute-start(bf16[128,1024]{1,0:T(8,128)(2,1)S(1)} %copy-done.92), channel_id=1, source_target_pairs={{0,5},{1,4},{2,1},{3,0},{4,7},{5,6},{6,3},{7,2},{8,13},{9,12},{10,... | collective-permute-start | bytes 786440 | tf_op jit(solution)/shard_map/ppermute | solution.py:818
  152.5 12.0 %collective-permute-done.26.refs_2_ = bf16[512,384]{1,0:T(8,128)(2,1)S(1)} collective-permute-done((bf16[512,384]{1,0:T(8,128)(2,1)S(1)}, bf16[512,384]{1,0:T(8,128)(2,1)S(1)}, u32[]{:S(2)}, u32[]{:S(2)}) %collective-permute-start.26) | collective-permute-done | bytes 393248 | tf_op jit(solution)/shard_map/ppermute | solution.py:818
  169.5 9.6 %attend.2 = (bf16[2048,128]{1,0:T(8,128)(2,1)S(1)}, bf16[2048,128]{1,0:T(8,128)(2,1)S(1)}, bf16[2048,128]{1,0:T(8,128)(2,1)S(1)}, bf16[2048,128]{1,0:T(8,128)(2,...) custom-call(s32[2]{0:T(128)S(1)} %pad_add_fusion.2.refs_0_, ...), custom_call_target="tpu_custom_call" | custom-call | flops 1 | bytes 1 | tf_op jit(solution)/shard_map/attend/pallas_call | solution.py:526
  187.9 6.0 %collective-permute-start.36 = (bf16[88,1024]{1,0:T(8,128)(2,1)}, bf16[88,1024]{1,0:T(8,128)(2,1)}, u32[]{:S(2)}, u32[]{:S(2)}) collective-permute-start(bf16[88,1024]{1,0:T(8,128)(2,1)} %param.23), channel_id=1, source_target_pairs={{0,2},{1,3},{2,0},{3,1},{4,6},{5,7},{6,4},{7,5},{8,10},{9,11},{10,... | collective-permute-start | bytes 540680 | tf_op jit(solution)/shard_map/ppermute | solution.py:818
  198.5 10.6 %attend.3 = (bf16[2048,128]{1,0:T(8,128)(2,1)S(1)}, bf16[2048,128]{1,0:T(8,128)(2,1)S(1)}, bf16[2048,128]{1,0:T(8,128)(2,1)S(1)}, bf16[2048,128]{1,0:T(8,128)(2,...) custom-call(s32[2]{0:T(128)S(1)} %pad_add_fusion.2.refs_0_, ...), custom_call_target="tpu_custom_call" | custom-call | flops 1 | bytes 1 | tf_op jit(solution)/shard_map/attend/pallas_call | solution.py:526
  268.2 9.0 %collective-permute-start.52 = (bf16[352,1024]{1,0:T(8,128)(2,1)S(1)}, bf16[352,1024]{1,0:T(8,128)(2,1)S(1)}, u32[]{:S(2)}, u32[]{:S(2)}) collective-permute-start(bf16[352,1024]{1,0:T(8,128)(2,1)S(1)} %copy-done), channel_id=1, source_target_pairs={{0,4},{1,5},{2,6},{3,7},{4,0},{5,1},{6,2},{7,3},{8,12},{9,13},{10,... | collective-permute-start | bytes 2162696 | tf_op jit(solution)/shard_map/ppermute | solution.py:818
  288.1 9.9 %multiply_convert_fusion.1 = (bf16[512,2816]{1,0:T(8,128)(2,1)}, bf16[512,2816]{1,0:T(8,128)(2,1)}) fusion(f32[512,2816]{1,0:T(8,128)} %copy-done.117, f32[512,2816]{1,0:T(8,128)} %get-tuple-element.456, bf16[512,1024]{1,0:T(8,128)(2,1)} %copy-done.60, bf16[2816,1024]{1,0:T(8,128)(2,1)S(1)} %settle.5), kind=kOutput, calls=%fused_computation.5 | convolution fusion | flops 2971533312 | bytes 24117248 | tf_op jit(solution)/shard_map/dot_general | solution.py:381
  298.0 6.5 %fusion.57 = f32[512,1024]{1,0:T(8,128)} fusion(bf16[512,2816]{1,0:T(8,128)(2,1)} %get-tuple-element.360, bf16[1024,2816]{1,0:T(8,128)(2,1)S(1)} %get-tuple-element.254), kind=kOutput, calls=%fused_computation.228 | convolution fusion | flops 2952790016 | bytes 10747904 | tf_op jit(solution)/shard_map/dot_general | solution.py:381
  307.8 6.1 %multiply_reduce_fusion = (f32[512]{0:T(512)S(1)}, f32[512,1024]{1,0:T(8,128)}) fusion(f32[512,1024]{1,0:T(8,128)S(1)} %copy-done.52, f32[512]{0:T(512)S(1)} %add_rsqrt_fusion, f32[1024]{0:T(1024)S(1)} %copy-done.113, f32[512,1024]{1,0:T(8,128)} %fusion.57, bf16[512,2816]{1,0:T(8,128)(2,1)S(1)} %copy-done.58, bf16[1024,2816]{1,0:T(8,128)(2,1)S(1)} %get-tuple-element.253), kind=kOutput, calls=%fused_computation.41 | convolution fusion | flops 2955410944 | bytes 14950400 | tf_op jit(solution)/shard_map/dot_general | solution.py:381
  335.0 5.9 %collective-permute-done.58.refs_10_ = bf16[512,256]{1,0:T(8,128)(2,1)S(1)} collective-permute-done((bf16[512,256]{1,0:T(8,128)(2,1)S(1)}, bf16[512,256]{1,0:T(8,128)(2,1)S(1)}, u32[]{:S(2)}, u32[]{:S(2)}) %collective-permute-start.58) | collective-permute-done | bytes 262176 | tf_op jit(solution)/shard_map/ppermute | solution.py:818
  341.0 12.3 %attend_back.2 = (bf16[512,384]{1,0:T(8,128)(2,1)S(1)}, bf16[512,384]{1,0:T(8,128)(2,1)S(1)}, bf16[512,384]{1,0:T(8,128)(2,1)S(1)}, bf16[512,384]{1,0:T(8,128)(2,1)S(1)}) custom-call(s32[2]{0:T(128)S(1)} %pad_add_fusion.2.refs_0_, bf16[2048,128]{1,0:T(8,128)(2,1)S(1)} %copy-done.16, bf16[2048,128]{1,0:T(8,128)(2,1)S(1)} %copy-done.18, ...), custom_call_target="tpu_custom_call" | custom-call | flops 1 | bytes 1 | tf_op jit(solution)/shard_map/attend_back/pallas_call | solution.py:635
  358.7 5.6 add_convert_fusion.1
  364.3 11.4 %collective-permute-done.63 = bf16[352,1024]{1,0:T(8,128)(2,1)S(1)} collective-permute-done((bf16[352,1024]{1,0:T(8,128)(2,1)}, bf16[352,1024]{1,0:T(8,128)(2,1)S(1)}, u32[]{:S(2)}, u32[]{:S(2)}) %collective-permute-start.63) | collective-permute-done | bytes 720928 | tf_op jit(solution)/shard_map/ppermute | solution.py:818
  376.6 11.9 %attend_back.3 = (bf16[512,384]{1,0:T(8,128)(2,1)S(1)}, bf16[512,384]{1,0:T(8,128)(2,1)S(1)}, bf16[512,384]{1,0:T(8,128)(2,1)S(1)}, bf16[512,384]{1,0:T(8,128)(2,1)S(1)}) custom-call(s32[2]{0:T(128)S(1)} %pad_add_fusion.2.refs_0_, bf16[2048,128]{1,0:T(8,128)(2,1)S(1)} %copy-done.24, bf16[2048,128]{1,0:T(8,128)(2,1)S(1)} %copy-done.26, ...), custom_call_target="tpu_custom_call" | custom-call | flops 1 | bytes 1 | tf_op jit(solution)/shard_map/attend_back/pallas_call | solution.py:635
  394.6 12.0 %collective-permute-start.73 = (bf16[128,2816]{1,0:T(8,128)(2,1)}, bf16[128,2816]{1,0:T(8,128)(2,1)S(1)}, u32[]{:S(2)}, u32[]{:S(2)}) collective-permute-start(bf16[128,2816]{1,0:T(8,128)(2,1)} %get-tuple-element.371), channel_id=1, source_target_pairs={{0,8},{1,9},{2,10},{3,11},{4,12},{5,13},{6,14},{7,15},{8,0},{9,1},... | collective-permute-start | bytes 2162696 | tf_op jit(solution)/shard_map/ppermute | solution.py:818
  416.7 7.1 %collective-permute-done.73 = bf16[128,2816]{1,0:T(8,128)(2,1)S(1)} collective-permute-done((bf16[128,2816]{1,0:T(8,128)(2,1)}, bf16[128,2816]{1,0:T(8,128)(2,1)S(1)}, u32[]{:S(2)}, u32[]{:S(2)}) %collective-permute-start.73) | collective-permute-done | bytes 720928 | tf_op jit(solution)/shard_map/ppermute | solution.py:818
  428.2 15.0 %collective-permute-done.74 = bf16[128,2816]{1,0:T(8,128)(2,1)S(1)} collective-permute-done((bf16[128,2816]{1,0:T(8,128)(2,1)}, bf16[128,2816]{1,0:T(8,128)(2,1)S(1)}, u32[]{:S(2)}, u32[]{:S(2)}) %collective-permute-start.74) | collective-permute-done | bytes 720928 | tf_op jit(solution)/shard_map/ppermute | solution.py:818
  463.6 16.6 %collective-permute-start.90 = (bf16[32,2816]{1,0:T(8,128)(2,1)S(1)}, bf16[32,2816]{1,0:T(8,128)(2,1)S(1)}, u32[]{:S(2)}, u32[]{:S(2)}) collective-permute-start(bf16[32,2816]{1,0:T(8,128)(2,1)S(1)} %get-tuple-element.423), channel_id=1, source_target_pairs={{0,3},{1,0},{2,1},{3,2},{4,7},{5,4},{6,5},{7,6},{8,11},{9,8},{10,9... | collective-permute-start | bytes 540680 | tf_op jit(solution)/shard_map/ppermute | solution.py:818
  516.9 17.6 %collective-permute-done.83 = bf16[128,4096]{1,0:T(8,128)(2,1)S(1)} collective-permute-done((bf16[128,4096]{1,0:T(8,128)(2,1)S(1)}, bf16[128,4096]{1,0:T(8,128)(2,1)S(1)}, u32[]{:S(2)}, u32[]{:S(2)}) %collective-permute-start.83) | collective-permute-done | bytes 1048608 | tf_op jit(solution)/shard_map/ppermute | solution.py:818
  543.4 39.6 %collective-permute-done.86 = bf16[32,4096]{1,0:T(8,128)(2,1)S(1)} collective-permute-done((bf16[32,4096]{1,0:T(8,128)(2,1)S(1)}, bf16[32,4096]{1,0:T(8,128)(2,1)S(1)}, u32[]{:S(2)}, u32[]{:S(2)}) %collective-permute-start.86) | collective-permute-done | bytes 262176 | tf_op jit(solution)/shard_map/ppermute | solution.py:818
  (546 shorter events, 297.2 us)
Async XLA Ops:
  59.0 36.3 %collective-permute-start.17 = (bf16[128,3200]{1,0:T(8,128)(2,1)S(1)}, bf16[128,3200]{1,0:T(8,128)(2,1)}, u32[]{:S(2)}, u32[]{:S(2)}) collective-permute-start(bf16[128,3200]{1,0:T(8,128)(2,1)S(1)} %constant_dynamic-update-slice_fusion.refs_1_), channel_id=1, source_target_pairs={{0,16},{1,17},{2,18},{3,19},{4,20},{5,21},{6,22},{7,23},{8,24},{9,... | collective-permute-start | bytes 2457608 | tf_op jit(solution)/shard_map/ppermute | solution.py:818
  96.5 68.9 %collective-permute-start.33 = (bf16[128,6656]{1,0:T(8,128)(2,1)}, bf16[128,6656]{1,0:T(8,128)(2,1)}, u32[]{:S(2)}, u32[]{:S(2)}) collective-permute-start(bf16[128,6656]{1,0:T(8,128)(2,1)} %constant_dynamic-update-slice_fusion.4.refs_1_), channel_id=1, source_target_pairs={{0,8},{1,9},{2,10},{3,11},{4,12},{5,13},{6,14},{7,15},{8,0},{9,1},... | collective-permute-start | bytes 5111816 | tf_op jit(solution)/shard_map/ppermute | solution.py:818
  99.1 66.3 %collective-permute-start.34 = (bf16[128,6656]{1,0:T(8,128)(2,1)}, bf16[128,6656]{1,0:T(8,128)(2,1)}, u32[]{:S(2)}, u32[]{:S(2)}) collective-permute-start(bf16[128,6656]{1,0:T(8,128)(2,1)} %constant_dynamic-update-slice_fusion.4.refs_1_), channel_id=1, source_target_pairs={{0,16},{1,17},{2,18},{3,19},{4,20},{5,21},{6,22},{7,23},{8,24},{9,... | collective-permute-start | bytes 5111816 | tf_op jit(solution)/shard_map/ppermute | solution.py:818
  112.9 37.6 %collective-permute-start.31 = (bf16[128,1024]{1,0:T(8,128)(2,1)S(1)}, bf16[128,1024]{1,0:T(8,128)(2,1)S(1)}, u32[]{:S(2)}, u32[]{:S(2)}) collective-permute-start(bf16[128,1024]{1,0:T(8,128)(2,1)S(1)} %copy-done.94), channel_id=1, source_target_pairs={{0,4},{1,5},{2,0},{3,1},{4,6},{5,7},{6,2},{7,3},{8,12},{9,13},{10,... | collective-permute-start | bytes 786440 | tf_op jit(solution)/shard_map/ppermute | solution.py:818
  165.4 31.0 %collective-permute-start.24 = (bf16[512,384]{1,0:T(8,128)(2,1)}, bf16[512,384]{1,0:T(8,128)(2,1)}, u32[]{:S(2)}, u32[]{:S(2)}) collective-permute-start(bf16[512,384]{1,0:T(8,128)(2,1)} %get-tuple-element.382), channel_id=1, source_target_pairs={{0,4},{1,5},{2,6},{3,7},{4,0},{5,1},{6,2},{7,3},{8,12},{9,13},{10,... | collective-permute-start | bytes 1179656 | tf_op jit(solution)/shard_map/ppermute | solution.py:818
  229.7 35.9 %collective-permute-start.49 = (bf16[352,1024]{1,0:T(8,128)(2,1)S(1)}, bf16[352,1024]{1,0:T(8,128)(2,1)S(1)}, u32[]{:S(2)}, u32[]{:S(2)}) collective-permute-start(bf16[352,1024]{1,0:T(8,128)(2,1)S(1)} %copy-done), channel_id=1, source_target_pairs={{0,8},{1,9},{2,10},{3,11},{4,12},{5,13},{6,14},{7,15},{8,0},{9,1},... | collective-permute-start | bytes 2162696 | tf_op jit(solution)/shard_map/ppermute | solution.py:818
  234.8 33.4 %collective-permute-start.50 = (bf16[352,1024]{1,0:T(8,128)(2,1)S(1)}, bf16[352,1024]{1,0:T(8,128)(2,1)S(1)}, u32[]{:S(2)}, u32[]{:S(2)}) collective-permute-start(bf16[352,1024]{1,0:T(8,128)(2,1)S(1)} %copy-done), channel_id=1, source_target_pairs={{0,16},{1,17},{2,18},{3,19},{4,20},{5,21},{6,22},{7,23},{8,24},{9,... | collective-permute-start | bytes 2162696 | tf_op jit(solution)/shard_map/ppermute | solution.py:818
  284.6 35.3 %collective-permute-start.60 = (bf16[4,352,1024]{2,1,0:T(8,128)(2,1)}, bf16[4,352,1024]{2,1,0:T(8,128)(2,1)}, u32[]{:S(2)}, u32[]{:S(2)}) collective-permute-start(bf16[4,352,1024]{2,1,0:T(8,128)(2,1)} %dynamic-slice_bitcast_fusion), channel_id=1, source_target_pairs={{0,4},{1,5},{2,6},{3,7},{4,0},{5,1},{6,2},{7,3},{8,12},{9,13},{10,... | collective-permute-start | bytes 8650760 | tf_op jit(solution)/shard_map/ppermute | solution.py:818
  307.7 46.5 %collective-permute-start.59 = (bf16[512,2816]{1,0:T(8,128)(2,1)}, bf16[512,2816]{1,0:T(8,128)(2,1)}, u32[]{:S(2)}, u32[]{:S(2)}) collective-permute-start(bf16[512,2816]{1,0:T(8,128)(2,1)} %convolution_convert_fusion.2), channel_id=1, source_target_pairs={{0,4},{1,5},{2,6},{3,7},{4,0},{5,1},{6,2},{7,3},{8,12},{9,13},{10,... | collective-permute-start | bytes 8650760 | tf_op jit(solution)/shard_map/ppermute | solution.py:818
  317.2 76.0 %collective-permute-start.70 = (bf16[512,2816]{1,0:T(8,128)(2,1)}, bf16[512,2816]{1,0:T(8,128)(2,1)}, u32[]{:S(2)}, u32[]{:S(2)}) collective-permute-start(bf16[512,2816]{1,0:T(8,128)(2,1)} %convolution_convert_fusion.1), channel_id=1, source_target_pairs={{0,4},{1,5},{2,6},{3,7},{4,0},{5,1},{6,2},{7,3},{8,12},{9,13},{10,... | collective-permute-start | bytes 8650760 | tf_op jit(solution)/shard_map/ppermute | solution.py:818
  353.2 35.3 %collective-permute-start.64 = (bf16[512,384]{1,0:T(8,128)(2,1)S(1)}, bf16[512,384]{1,0:T(8,128)(2,1)S(1)}, u32[]{:S(2)}, u32[]{:S(2)}) collective-permute-start(bf16[512,384]{1,0:T(8,128)(2,1)S(1)} %get-tuple-element.287), channel_id=1, source_target_pairs={{0,1},{1,0},{2,3},{3,2},{4,5},{5,4},{6,7},{7,6},{8,9},{9,8},{10,11... | collective-permute-start | bytes 1179656 | tf_op jit(solution)/shard_map/ppermute | solution.py:818
  354.2 34.3 %collective-permute-start.65 = (bf16[512,384]{1,0:T(8,128)(2,1)S(1)}, bf16[512,384]{1,0:T(8,128)(2,1)S(1)}, u32[]{:S(2)}, u32[]{:S(2)}) collective-permute-start(bf16[512,384]{1,0:T(8,128)(2,1)S(1)} %get-tuple-element.288), channel_id=1, source_target_pairs={{0,4},{1,5},{2,6},{3,7},{4,0},{5,1},{6,2},{7,3},{8,12},{9,13},{10,... | collective-permute-start | bytes 1179656 | tf_op jit(solution)/shard_map/ppermute | solution.py:818
  354.4 34.2 %collective-permute-start.66 = (bf16[512,384]{1,0:T(8,128)(2,1)S(1)}, bf16[512,384]{1,0:T(8,128)(2,1)S(1)}, u32[]{:S(2)}, u32[]{:S(2)}) collective-permute-start(bf16[512,384]{1,0:T(8,128)(2,1)S(1)} %get-tuple-element.289), channel_id=1, source_target_pairs={{0,5},{1,4},{2,7},{3,6},{4,1},{5,0},{6,3},{7,2},{8,13},{9,12},{10,... | collective-permute-start | bytes 1179656 | tf_op jit(solution)/shard_map/ppermute | solution.py:818
  393.2 50.8 %collective-permute-start.72 = (bf16[512,1536]{1,0:T(8,128)(2,1)}, bf16[512,1536]{1,0:T(8,128)(2,1)}, u32[]{:S(2)}, u32[]{:S(2)}) collective-permute-start(bf16[512,1536]{1,0:T(8,128)(2,1)} %convolution_convert_fusion.4), channel_id=1, source_target_pairs={{0,4},{1,5},{2,6},{3,7},{4,0},{5,1},{6,2},{7,3},{8,12},{9,13},{10,... | collective-permute-start | bytes 4718600 | tf_op jit(solution)/shard_map/ppermute | solution.py:818
  409.2 34.0 %collective-permute-start.74 = (bf16[128,2816]{1,0:T(8,128)(2,1)}, bf16[128,2816]{1,0:T(8,128)(2,1)S(1)}, u32[]{:S(2)}, u32[]{:S(2)}) collective-permute-start(bf16[128,2816]{1,0:T(8,128)(2,1)} %get-tuple-element.370), channel_id=1, source_target_pairs={{0,16},{1,17},{2,18},{3,19},{4,20},{5,21},{6,22},{7,23},{8,24},{9,... | collective-permute-start | bytes 2162696 | tf_op jit(solution)/shard_map/ppermute | solution.py:818
  409.3 33.9 %collective-permute-start.75 = (bf16[128,2816]{1,0:T(8,128)(2,1)S(1)}, bf16[128,2816]{1,0:T(8,128)(2,1)S(1)}, u32[]{:S(2)}, u32[]{:S(2)}) collective-permute-start(bf16[128,2816]{1,0:T(8,128)(2,1)S(1)} %get-tuple-element.369), channel_id=1, source_target_pairs={{0,24},{1,25},{2,26},{3,27},{4,28},{5,29},{6,30},{7,31},{8,16},{9,... | collective-permute-start | bytes 2162696 | tf_op jit(solution)/shard_map/ppermute | solution.py:818
  415.6 35.1 %collective-permute-start.71 = (bf16[512,1536]{1,0:T(8,128)(2,1)S(1)}, bf16[512,1536]{1,0:T(8,128)(2,1)S(1)}, u32[]{:S(2)}, u32[]{:S(2)}) collective-permute-start(bf16[512,1536]{1,0:T(8,128)(2,1)S(1)} %convolution_convert_fusion.3), channel_id=1, source_target_pairs={{0,4},{1,5},{2,6},{3,7},{4,0},{5,1},{6,2},{7,3},{8,12},{9,13},{10,... | collective-permute-start | bytes 4718600 | tf_op jit(solution)/shard_map/ppermute | solution.py:818
  423.8 65.5 %collective-permute-start.96 = (bf16[88,1024]{1,0:T(8,128)(2,1)S(1)}, bf16[88,1024]{1,0:T(8,128)(2,1)S(1)}, u32[]{:S(2)}, u32[]{:S(2)}) collective-permute-start(bf16[88,1024]{1,0:T(8,128)(2,1)S(1)} %get-tuple-element.417), channel_id=1, source_target_pairs={{0,3},{1,0},{2,1},{3,2},{4,7},{5,4},{6,5},{7,6},{8,11},{9,8},{10,9... | collective-permute-start | bytes 540680 | tf_op jit(solution)/shard_map/ppermute | solution.py:818
  444.0 36.2 %collective-permute-start.78 = (bf16[128,2816]{1,0:T(8,128)(2,1)S(1)}, bf16[128,2816]{1,0:T(8,128)(2,1)S(1)}, u32[]{:S(2)}, u32[]{:S(2)}) collective-permute-start(bf16[128,2816]{1,0:T(8,128)(2,1)S(1)} %get-tuple-element.365), channel_id=1, source_target_pairs={{0,24},{1,25},{2,26},{3,27},{4,28},{5,29},{6,30},{7,31},{8,16},{9,... | collective-permute-start | bytes 2162696 | tf_op jit(solution)/shard_map/ppermute | solution.py:818
  456.5 33.2 %collective-permute-start.95 = (bf16[88,1024]{1,0:T(8,128)(2,1)S(1)}, bf16[88,1024]{1,0:T(8,128)(2,1)S(1)}, u32[]{:S(2)}, u32[]{:S(2)}) collective-permute-start(bf16[88,1024]{1,0:T(8,128)(2,1)S(1)} %get-tuple-element.418), channel_id=1, source_target_pairs={{0,2},{1,3},{2,0},{3,1},{4,6},{5,7},{6,4},{7,5},{8,10},{9,11},{10,... | collective-permute-start | bytes 540680 | tf_op jit(solution)/shard_map/ppermute | solution.py:818
  489.8 44.8 %collective-permute-start.83 = (bf16[128,4096]{1,0:T(8,128)(2,1)S(1)}, bf16[128,4096]{1,0:T(8,128)(2,1)S(1)}, u32[]{:S(2)}, u32[]{:S(2)}) collective-permute-start(bf16[128,4096]{1,0:T(8,128)(2,1)S(1)} %get-tuple-element.362), channel_id=1, source_target_pairs={{0,16},{1,17},{2,18},{3,19},{4,20},{5,21},{6,22},{7,23},{8,24},{9,... | collective-permute-start | bytes 3145736 | tf_op jit(solution)/shard_map/ppermute | solution.py:818
  490.8 43.8 %collective-permute-start.84 = (bf16[128,4096]{1,0:T(8,128)(2,1)S(1)}, bf16[128,4096]{1,0:T(8,128)(2,1)S(1)}, u32[]{:S(2)}, u32[]{:S(2)}) collective-permute-start(bf16[128,4096]{1,0:T(8,128)(2,1)S(1)} %get-tuple-element.361), channel_id=1, source_target_pairs={{0,24},{1,25},{2,26},{3,27},{4,28},{5,29},{6,30},{7,31},{8,16},{9,... | collective-permute-start | bytes 3145736 | tf_op jit(solution)/shard_map/ppermute | solution.py:818
  536.6 46.4 %collective-permute-start.86 = (bf16[32,4096]{1,0:T(8,128)(2,1)S(1)}, bf16[32,4096]{1,0:T(8,128)(2,1)S(1)}, u32[]{:S(2)}, u32[]{:S(2)}) collective-permute-start(bf16[32,4096]{1,0:T(8,128)(2,1)S(1)} %get-tuple-element.387), channel_id=1, source_target_pairs={{0,2},{1,3},{2,0},{3,1},{4,6},{5,7},{6,4},{7,5},{8,10},{9,11},{10,... | collective-permute-start | bytes 786440 | tf_op jit(solution)/shard_map/ppermute | solution.py:818
  538.3 44.7 %collective-permute-start.85 = (bf16[32,4096]{1,0:T(8,128)(2,1)S(1)}, bf16[32,4096]{1,0:T(8,128)(2,1)S(1)}, u32[]{:S(2)}, u32[]{:S(2)}) collective-permute-start(bf16[32,4096]{1,0:T(8,128)(2,1)S(1)} %get-tuple-element.385), channel_id=1, source_target_pairs={{0,1},{1,2},{2,3},{3,0},{4,5},{5,6},{6,7},{7,4},{8,9},{9,10},{10,1... | collective-permute-start | bytes 786440 | tf_op jit(solution)/shard_map/ppermute | solution.py:818
  (195 other events, 2049.8 us)

commit v3 on v2

--- a/solution.py
+++ b/solution.py
@@ -427,9 +427,9 @@
     return copies
 
 
-def attend_kernel(head, n_in, *refs):
+def attend_kernel(head, n_in, n_first, *refs):
     place = refs[0]
-    given, refs = refs[1 : 1 + n_in], refs[1 + n_in :]
+    given, refs = refs[1 : 1 + n_in], refs[1 + n_in + n_first :]
     n_kept = n_in - 10
     saved, outs, refs = refs[:6], refs[6 : 6 + 4 * n_kept], refs[6 + 4 * n_kept :]
     held, refs = refs[:n_in], refs[n_in:]
@@ -515,7 +515,7 @@
         copy.wait()
 
 
-def attend(head, place, blocks, memory, mem_rows, cos_t, sin_t, kept=()):
+def attend(head, place, blocks, memory, mem_rows, cos_t, sin_t, kept=(), first=()):
     rows_q = blocks[0].shape[0]
     length = cos_t.shape[0]
     low = jnp.bfloat16
@@ -524,9 +524,9 @@
     part = jax.ShapeDtypeStruct((rows_q, (len(kept) + 1) * HEAD_DIM), low)
     n_out = 4 if kept else 0
     return pl.pallas_call(
-        functools.partial(attend_kernel, head, len(given)),
+        functools.partial(attend_kernel, head, len(given), len(first)),
         out_shape=[jax.ShapeDtypeStruct(*kind) for kind in saved] + [part] * n_out,
-        in_specs=[smem()] + hbm(len(given)),
+        in_specs=[smem()] + hbm(len(given) + len(first)),
         out_specs=hbm(6) + whole(n_out),
         scratch_shapes=[pltpu.VMEM(array.shape, array.dtype) for array in given]
         + [pltpu.VMEM(*kind) for kind in saved]
@@ -536,12 +536,12 @@
         compiler_params=pltpu.CompilerParams(vmem_limit_bytes=24 << 20),
         cost_estimate=pl.CostEstimate(flops=1, bytes_accessed=1, transcendentals=0),
         name="attend",
-    )(place, *given)
-
-
-def attend_back_kernel(head, n_in, *refs):
+    )(place, *given, *first)
+
+
+def attend_back_kernel(head, n_in, n_first, *refs):
     place = refs[0]
-    given, refs = refs[1 : 1 + n_in], refs[1 + n_in :]
+    given, refs = refs[1 : 1 + n_in], refs[1 + n_in + n_first :]
     g0, g1, g2, g3 = refs[:4]
     held, refs = refs[4 : 4 + n_in], refs[4 + n_in :]
     qr_ref, qm_ref, kr_ref, v_ref, att_ref, lse_ref = held[:6]
@@ -627,15 +627,15 @@
         out[...] = grads[place_rows(quarter, rel, rows_q), :]
 
 
-def attend_back(head, place, saved, d_blocks, memory, mem_rows, cos_t, sin_t):
+def attend_back(head, place, saved, d_blocks, memory, mem_rows, cos_t, sin_t, first=()):
     rows_q = d_blocks[0].shape[0]
     length = cos_t.shape[0]
     low, wide = jnp.bfloat16, jnp.float32
     given = (*saved, *d_blocks, *memory, cos_t, sin_t)
     return pl.pallas_call(
-        functools.partial(attend_back_kernel, head, len(given)),
+        functools.partial(attend_back_kernel, head, len(given), len(first)),
         out_shape=[jax.ShapeDtypeStruct((rows_q, 3 * HEAD_DIM), low)] * 4,
-        in_specs=[smem()] + hbm(len(given)),
+        in_specs=[smem()] + hbm(len(given) + len(first)),
         out_specs=whole(4),
         scratch_shapes=[pltpu.VMEM(array.shape, array.dtype) for array in given]
         + [
@@ -652,7 +652,7 @@
         compiler_params=pltpu.CompilerParams(vmem_limit_bytes=28 << 20),
         cost_estimate=pl.CostEstimate(flops=1, bytes_accessed=1, transcendentals=0),
         name="attend_back",
-    )(place, *given)
+    )(place, *given, *first)
 
 
 def deal_kernel(n_heads, n_owners, wq, wk, wv, gains, out):
@@ -975,10 +975,17 @@
             1,
         )
 
+    def plane_parts(both):
+        size = both.shape[0] // (n_doc // 2)
+        return [both[rel * size : (rel + 1) * size] for rel in range(n_doc // 2)]
+
+    def over_plane(parts):
+        return [parts[0]] + [
+            move(part, name) for part, name in zip(parts[1:], ("x", "y", "xy"))
+        ]
+
     def met_in_plane(both):
-        size = both.shape[0] // (n_doc // 2)
-        parts = [both[rel * size : (rel + 1) * size] for rel in range(n_doc // 2)]
-        return [parts[0]] + [move(parts[rel + 1], name) for rel, name in enumerate(("x", "y", "xy"))]
+        return over_plane(plane_parts(both))
 
     def finish_by_hops(total):
         chunks = total.reshape(n_seq, -1, total.shape[1])
@@ -998,33 +1005,41 @@
     down_sent = pick(grad_down, 1 - core, 1)
     met_down = move(down_sent, "core")
     (w_down_f,) = settle(where, rels, later(pieces_c, down_sent), (width,), 1)
-    d_hidden = dot_nt(grad_y, w_down_f)
+    layer_out = (resid_mid + dot_nn(hidden, w_down_f)).astype(low)
+    layer_moved = to_group(layer_out)
+    d_hidden = dot_nt(later(grad_y, layer_out), w_down_f)
     d_gate = (d_hidden * up_act * (sig_gate * (1.0 + gate_act * (1.0 - sig_gate)))).astype(low)
     d_up = (d_hidden * silu_gate).astype(low)
     d_ffn_in = dot_nt(d_gate, w_gate_f) + dot_nt(d_up, w_up_f)
     d_mid = grad_y.astype(wide) + norm_back(d_ffn_in * gain_f, normed_two, factor_two)
-    d_branch = d_mid.astype(low)
+    layer_out = later(layer_moved, d_ffn_in)
+    d_branch = later(d_mid, layer_out).astype(low)
     d_att = dot_nt(d_branch, w_out_f).astype(low)
     d_blocks = [part_for(d_att, rel, share) for rel in range(n_seq)]
     d_sent = d_blocks[0]
     d_blocks = exchange(d_blocks)
     met_down = later(met_down, d_sent)
     both_down = plus(pick(grad_down, core, 1), met_down)
-    both_down = jnp.concatenate([pick(both_down, plane ^ rel) for rel in range(n_doc // 2)])
-    total_down = met_in_plane(both_down)
+    down_parts = [pick(both_down, plane ^ rel) for rel in range(n_doc // 2)]
+    total_down = over_plane(down_parts)
     away, home = side(ffn_in, 1 - core), side(ffn_in, core)
-    away_gate = dot_tn(later(away, both_down), d_gate).astype(low)
+    away_gate = dot_tn(away, d_gate).astype(low)
     met_gate = move(away_gate, "core")
     away_up = dot_tn(later(away, away_gate), d_up).astype(low)
     met_up = move(away_up, "core")
     d_blocks = later(d_blocks, away_up)
-    g_0 = attend_back(0, place, saved_0, d_blocks, memory, mem_rows, cos_t, sin_t)
+    g_0 = attend_back(
+        0, place, saved_0, d_blocks, memory, mem_rows, cos_t, sin_t, down_parts[1:]
+    )
     d_set_0 = exchange(g_0)
     both_gate = kept(home, d_gate, later(met_gate, g_0))
-    total_down = later(total_down, both_gate)
-    total_gate = met_in_plane(later(both_gate, total_down))
+    both_up = kept(home, d_up, later(met_up, both_gate))
+    total_down = later(total_down, both_up)
+    gate_parts = plane_parts(later(both_gate, total_down))
+    total_gate = over_plane(gate_parts)
     g_1 = attend_back(
-        1, place, saved_1, later(d_blocks, both_gate, total_down), memory, mem_rows, cos_t, sin_t
+        1, place, saved_1, later(d_blocks, both_up), memory, mem_rows, cos_t, sin_t,
+        (both_up, *total_down[1:], *gate_parts[1:]),
     )
     g_1 = later(g_1, d_set_0)
     d_set_1 = exchange(g_1)
@@ -1033,10 +1048,9 @@
     d_qkv_0 = spread(later(d_set_0, g_1))
     away_0 = dot_tn(away, d_qkv_0).astype(low)
     met_0 = move(away_0, "core")
-    both_up = kept(home, d_up, later(met_up, away_0))
-    total_gate = later(total_gate, both_up)
+    total_gate = later(total_gate, away_0)
     total_up = met_in_plane(later(both_up, total_gate))
-    d_set_1 = later(d_set_1, both_up)
+    d_set_1 = later(d_set_1, total_gate)
     d_qkv_1 = spread(d_set_1)
     away_1 = dot_tn(away, d_qkv_1).astype(low)
     met_1 = move(away_1, "core")
@@ -1044,16 +1058,16 @@
     both_0 = kept(home_in, d_qkv_0, later(met_0, away_1))
     away_out = dot_tn(later(side(attn_low, 1 - core), both_0), d_branch).astype(low)
     met_out = move(away_out, "core")
-    out_gate = finish_by_hops(plus(*later(total_gate, away_out)))
     both_1 = kept(home_in, d_qkv_1, later(met_1, away_out))
-    layer_out = (resid_mid + dot_nn(later(hidden, both_1), w_down_f)).astype(low)
-    both_out = kept(side(attn_low, core), later(d_branch, layer_out), later(met_out, layer_out))
-    total_up = later(total_up, both_out)
-    last = met_in_plane(later(jnp.concatenate([both_0, both_1, both_out], 1), total_up))
+    both_out = kept(side(attn_low, core), later(d_branch, both_1), later(met_out, both_1))
+    both = jnp.concatenate([both_0, both_1, both_out], 1)
+    total_gate = plus(*later(total_gate, both))
+    out_gate = finish_by_hops(total_gate)
+    total_up = later(total_up, total_gate)
+    last = met_in_plane(later(both, total_up))
     d_attn_in = dot_nt(later(d_qkv_0, total_up), w_heads[0]) + dot_nt(
         later(d_qkv_1, total_up), w_heads[1]
     )
-    layer_out = to_group(later(layer_out, total_up))
     grad_in = d_mid + norm_back(d_attn_in * gain_a, normed_one, factor_one)
     grad_in = grad_in.astype(low)
     grad_tokens = to_group(grad_in).astype(wide)

time: 595 us -> 560 us (0.941)
  starting transfers between devices: 185 us -> 162 us
  local copies, waits for them, and re-layouts: 54 us -> 46.2 us
    ppermute x97, starting transfers between devices: 185 us -> 162 us  [move(): return lax.ppermute(array, LINE, routes[name])]
    unnamed x250 -> x290, local copies, waits for them, and re-layouts: 34.6 us -> 29.4 us
  transfers between devices with their start and end apart: 97 -> 97, of which waited for: 26 -> 31; matrix products, arithmetic and copies ran while one was open for 23% -> 22% of each run, Pallas kernels for 10% -> 11%
where the time goes in v3:
time: 560 us; the launch traced here: 549 us
  waiting for transfers between devices  170 us (30%)
  starting transfers between devices  162 us (29%)
  matrix products  63.6 us (11%)
  Pallas kernels  60.3 us (11%)
  local copies, waits for them, and re-layouts  46.2 us (8%)
  other arithmetic  42.3 us (8%)
    ppermute x97, waiting for transfers between devices, move(): return lax.ppermute(array, LINE, routes[name])  170 us
    ppermute x97, starting transfers between devices, move(): return lax.ppermute(array, LINE, routes[name])  162 us
    unnamed x290, local copies, waits for them, and re-layouts  29.4 us
    pallas_call x2, Pallas kernels, attend_back(): pl.pallas_call(functools.partial(attend_back_kernel, head, len(given), le...  24.9 us
    dot_general x6, matrix products, dot_nt(): return lax.dot_general(left, right, (((1,), (1,)), ((), ())), **MXU)  23.4 us
    dot_general x11, matrix products, dot_tn(): return lax.dot_general(left, right, (((0,), (0,)), ((), ())), **MXU)  22 us
    pallas_call x2, Pallas kernels, attend(): pl.pallas_call(functools.partial(attend_kernel, head, len(given), len(fir...  20.2 us
    dot_general x6, matrix products, dot_nn(): return jnp.dot(left, right, **MXU)  18.2 us
  transfers between devices with their start and end apart: 97, of which 31 were waited for; matrix products, arithmetic and copies ran while one was open for 22% of the time, Pallas kernels for 11%

profile of v3, /device:TPU:0, one launch (start us, length us, event | category | flops | bytes accessed | tf_op | source)
XLA Modules:
  0.0 549.3 jit_solution(929576473363784691)
XLA Ops:
  36.1 5.6 %collective-permute-start.7 = (bf16[32,6656]{1,0:T(8,128)(2,1)S(1)}, bf16[32,6656]{1,0:T(8,128)(2,1)S(1)}, u32[]{:S(2)}, u32[]{:S(2)}) collective-permute-start(bf16[32,6656]{1,0:T(8,128)(2,1)S(1)} %pad_maximum_fusion.13), channel_id=1, source_target_pairs={{0,1},{1,2},{2,3},{3,0},{4,5},{5,6},{6,7},{7,4},{8,9},{9,10},{10,1... | collective-permute-start | bytes 1277960 | tf_op jit(solution)/shard_map/ppermute | solution.py:818
  47.1 9.5 %collective-permute-start.9 = (bf16[32,6656]{1,0:T(8,128)(2,1)S(1)}, bf16[32,6656]{1,0:T(8,128)(2,1)S(1)}, u32[]{:S(2)}, u32[]{:S(2)}) collective-permute-start(bf16[32,6656]{1,0:T(8,128)(2,1)S(1)} %pad_maximum_fusion.13), channel_id=1, source_target_pairs={{0,3},{1,0},{2,1},{3,2},{4,7},{5,4},{6,5},{7,6},{8,11},{9,8},{10,9... | collective-permute-start | bytes 1277960 | tf_op jit(solution)/shard_map/ppermute | solution.py:818
  64.7 7.8 %collective-permute-done.8 = bf16[32,6656]{1,0:T(8,128)(2,1)S(1)} collective-permute-done((bf16[32,6656]{1,0:T(8,128)(2,1)S(1)}, bf16[32,6656]{1,0:T(8,128)(2,1)S(1)}, u32[]{:S(2)}, u32[]{:S(2)}) %collective-permute-start.8) | collective-permute-done | bytes 426016 | tf_op jit(solution)/shard_map/ppermute | solution.py:818
  79.5 15.0 %collective-permute-done.17.refs_3_ = bf16[128,3200]{1,0:T(8,128)(2,1)} collective-permute-done((bf16[128,3200]{1,0:T(8,128)(2,1)S(1)}, bf16[128,3200]{1,0:T(8,128)(2,1)}, u32[]{:S(2)}, u32[]{:S(2)}) %collective-permute-start.17) | collective-permute-done | bytes 819232 | tf_op jit(solution)/shard_map/ppermute | solution.py:818
  111.6 16.6 %collective-permute-start.31 = (bf16[128,1024]{1,0:T(8,128)(2,1)S(1)}, bf16[128,1024]{1,0:T(8,128)(2,1)S(1)}, u32[]{:S(2)}, u32[]{:S(2)}) collective-permute-start(bf16[128,1024]{1,0:T(8,128)(2,1)S(1)} %copy-done.116), channel_id=1, source_target_pairs={{0,4},{1,5},{2,0},{3,1},{4,6},{5,7},{6,2},{7,3},{8,12},{9,13},{10,... | collective-permute-start | bytes 786440 | tf_op jit(solution)/shard_map/ppermute | solution.py:818
  128.2 9.4 %collective-permute-start.32 = (bf16[128,1024]{1,0:T(8,128)(2,1)S(1)}, bf16[128,1024]{1,0:T(8,128)(2,1)S(1)}, u32[]{:S(2)}, u32[]{:S(2)}) collective-permute-start(bf16[128,1024]{1,0:T(8,128)(2,1)S(1)} %copy-done.115), channel_id=1, source_target_pairs={{0,5},{1,4},{2,1},{3,0},{4,7},{5,6},{6,3},{7,2},{8,13},{9,12},{10,... | collective-permute-start | bytes 786440 | tf_op jit(solution)/shard_map/ppermute | solution.py:818
  149.8 12.0 %collective-permute-done.26.refs_2_ = bf16[512,384]{1,0:T(8,128)(2,1)S(1)} collective-permute-done((bf16[512,384]{1,0:T(8,128)(2,1)S(1)}, bf16[512,384]{1,0:T(8,128)(2,1)S(1)}, u32[]{:S(2)}, u32[]{:S(2)}) %collective-permute-start.26) | collective-permute-done | bytes 393248 | tf_op jit(solution)/shard_map/ppermute | solution.py:818
  166.8 9.6 %attend.2 = (bf16[2048,128]{1,0:T(8,128)(2,1)S(1)}, bf16[2048,128]{1,0:T(8,128)(2,1)S(1)}, bf16[2048,128]{1,0:T(8,128)(2,1)S(1)}, bf16[2048,128]{1,0:T(8,128)(2,...) custom-call(s32[2]{0:T(128)S(1)} %pad_add_fusion.2.refs_0_, ...), custom_call_target="tpu_custom_call" | custom-call | flops 1 | bytes 1 | tf_op jit(solution)/shard_map/attend/pallas_call | solution.py:526
  190.0 5.2 collective-permute-start.44
  195.7 10.6 %attend.3 = (bf16[2048,128]{1,0:T(8,128)(2,1)S(1)}, bf16[2048,128]{1,0:T(8,128)(2,1)S(1)}, bf16[2048,128]{1,0:T(8,128)(2,1)S(1)}, bf16[2048,128]{1,0:T(8,128)(2,...) custom-call(s32[2]{0:T(128)S(1)} %pad_add_fusion.2.refs_0_, ...), custom_call_target="tpu_custom_call" | custom-call | flops 1 | bytes 1 | tf_op jit(solution)/shard_map/attend/pallas_call | solution.py:526
  234.4 5.4 settle.4
  249.9 5.9 %multiply_convert_fusion.2 = (bf16[512,2816]{1,0:T(8,128)(2,1)}, f32[512,2816]{1,0:T(8,128)}) fusion(f32[512,2816]{1,0:T(8,128)S(1)} %fusion.55, bf16[512,1024]{1,0:T(8,128)(2,1)S(1)} %multiply_convert_fusion.3, bf16[1024,2816]{1,0:T(8,128)(2,1)S(1)} %get-tuple-element.255), kind=kOutput, calls=%fused_computation.6 | convolution fusion | flops 2961440768 | bytes 21233664 | tf_op jit(solution)/shard_map/dot_general | solution.py:389
  257.8 5.3 collective-permute-done.50.refs_3_
  263.1 10.3 %collective-permute-start.52 = (bf16[352,1024]{1,0:T(8,128)(2,1)}, bf16[352,1024]{1,0:T(8,128)(2,1)S(1)}, u32[]{:S(2)}, u32[]{:S(2)}) collective-permute-start(bf16[352,1024]{1,0:T(8,128)(2,1)} %pad_maximum_fusion.7.refs_1_), channel_id=1, source_target_pairs={{0,4},{1,5},{2,6},{3,7},{4,0},{5,1},{6,2},{7,3},{8,12},{9,13},{10,... | collective-permute-start | bytes 2162696 | tf_op jit(solution)/shard_map/ppermute | solution.py:818
  289.8 9.8 %multiply_convert_fusion.1 = (bf16[512,2816]{1,0:T(8,128)(2,1)}, bf16[512,2816]{1,0:T(8,128)(2,1)}) fusion(f32[512,2816]{1,0:T(8,128)} %copy-done.137, f32[512,2816]{1,0:T(8,128)} %get-tuple-element.458, bf16[512,1024]{1,0:T(8,128)(2,1)S(1)} %broadcast_select_fusion.1, bf16[2816,1024]{1,0:T(8,128)(2,1)S(1)} %settle.5), kind=kOutput, calls=%fused_computation.5 | convolution fusion | flops 2971533312 | bytes 24117248 | tf_op jit(solution)/shard_map/dot_general | solution.py:381
  346.2 11.9 %attend_back.2 = (bf16[512,384]{1,0:T(8,128)(2,1)S(1)}, bf16[512,384]{1,0:T(8,128)(2,1)S(1)}, bf16[512,384]{1,0:T(8,128)(2,1)S(1)}, bf16[512,384]{1,0:T(8,128)(2,1)S(1)}) custom-call(s32[2]{0:T(128)S(1)} %pad_add_fusion.2.refs_0_, bf16[2048,128]{1,0:T(8,128)(2,1)S(1)} %copy-done.27, bf16[2048,128]{1,0:T(8,128)(2,1)S(1)} %copy-done.29, ...), custom_call_target="tpu_custom_call" | custom-call | flops 1 | bytes 1 | tf_op jit(solution)/shard_map/attend_back/pallas_call | solution.py:635
  365.5 12.4 %collective-permute-done.67.refs_19_ = bf16[352,1024]{1,0:T(8,128)(2,1)S(1)} collective-permute-done((bf16[352,1024]{1,0:T(8,128)(2,1)S(1)}, bf16[352,1024]{1,0:T(8,128)(2,1)S(1)}, u32[]{:S(2)}, u32[]{:S(2)}) %collective-permute-start.67) | collective-permute-done | bytes 720928 | tf_op jit(solution)/shard_map/ppermute | solution.py:818
  382.4 13.0 %attend_back.3 = (bf16[512,384]{1,0:T(8,128)(2,1)S(1)}, bf16[512,384]{1,0:T(8,128)(2,1)}, bf16[512,384]{1,0:T(8,128)(2,1)}, bf16[512,384]{1,0:T(8,128)(2,1)}) custom-call(s32[2]{0:T(128)S(1)} %pad_add_fusion.2.refs_0_, bf16[2048,128]{1,0:T(8,128)(2,1)S(1)} %copy-done.35, bf16[2048,128]{1,0:T(8,128)(2,1)S(1)} %copy-done.37, bf16[2048,128]{1,0:T(8,128)(2,1)S(1)} %copy-done.39, ...), custom_call_target="tpu_custom_call" | custom-call | flops 1 | bytes 1 | tf_op jit(solution)/shard_map/attend_back/pallas_call | solution.py:635
  403.6 9.7 %collective-permute-done.71 = bf16[128,2816]{1,0:T(8,128)(2,1)} collective-permute-done((bf16[128,2816]{1,0:T(8,128)(2,1)}, bf16[128,2816]{1,0:T(8,128)(2,1)}, u32[]{:S(2)}, u32[]{:S(2)}) %collective-permute-start.71) | collective-permute-done | bytes 720928 | tf_op jit(solution)/shard_map/ppermute | solution.py:818
  413.3 6.2 %collective-permute-done.78.refs_4_ = bf16[512,384]{1,0:T(8,128)(2,1)} collective-permute-done((bf16[512,384]{1,0:T(8,128)(2,1)}, bf16[512,384]{1,0:T(8,128)(2,1)}, u32[]{:S(2)}, u32[]{:S(2)}) %collective-permute-start.78) | collective-permute-done | bytes 393248 | tf_op jit(solution)/shard_map/ppermute | solution.py:818
  448.7 11.2 %collective-permute-done.73 = bf16[128,2816]{1,0:T(8,128)(2,1)S(1)} collective-permute-done((bf16[128,2816]{1,0:T(8,128)(2,1)S(1)}, bf16[128,2816]{1,0:T(8,128)(2,1)S(1)}, u32[]{:S(2)}, u32[]{:S(2)}) %collective-permute-start.73) | collective-permute-done | bytes 720928 | tf_op jit(solution)/shard_map/ppermute | solution.py:818
  476.2 6.1 %collective-permute-done.92 = bf16[32,2816]{1,0:T(8,128)(2,1)S(1)} collective-permute-done((bf16[32,2816]{1,0:T(8,128)(2,1)S(1)}, bf16[32,2816]{1,0:T(8,128)(2,1)S(1)}, u32[]{:S(2)}, u32[]{:S(2)}) %collective-permute-start.92) | collective-permute-done | bytes 180256 | tf_op jit(solution)/shard_map/ppermute | solution.py:818
  501.5 15.6 %collective-permute-done.83 = bf16[128,4096]{1,0:T(8,128)(2,1)S(1)} collective-permute-done((bf16[128,4096]{1,0:T(8,128)(2,1)S(1)}, bf16[128,4096]{1,0:T(8,128)(2,1)S(1)}, u32[]{:S(2)}, u32[]{:S(2)}) %collective-permute-start.83) | collective-permute-done | bytes 1048608 | tf_op jit(solution)/shard_map/ppermute | solution.py:818
  528.9 17.1 %collective-permute-done.86 = bf16[32,4096]{1,0:T(8,128)(2,1)S(1)} collective-permute-done((bf16[32,4096]{1,0:T(8,128)(2,1)S(1)}, bf16[32,4096]{1,0:T(8,128)(2,1)S(1)}, u32[]{:S(2)}, u32[]{:S(2)}) %collective-permute-start.86) | collective-permute-done | bytes 262176 | tf_op jit(solution)/shard_map/ppermute | solution.py:818
  (587 shorter events, 303.0 us)
Async XLA Ops:
  26.4 30.3 %collective-permute-start.12 = (s32[512]{0:T(512)S(1)}, s32[512]{0:T(512)S(1)}, u32[]{:S(2)}, u32[]{:S(2)}) collective-permute-start(s32[512]{0:T(512)S(1)} %bitcast.172), channel_id=1, source_target_pairs={{0,4},{1,5},{2,0},{3,1},{4,6},{5,7},{6,2},{7,3},{8,12},{9,13},{10,... | collective-permute-start | bytes 6152 | tf_op jit(solution)/shard_map/ppermute | solution.py:818
  58.2 36.4 %collective-permute-start.17 = (bf16[128,3200]{1,0:T(8,128)(2,1)S(1)}, bf16[128,3200]{1,0:T(8,128)(2,1)}, u32[]{:S(2)}, u32[]{:S(2)}) collective-permute-start(bf16[128,3200]{1,0:T(8,128)(2,1)S(1)} %constant_dynamic-update-slice_fusion.refs_1_), channel_id=1, source_target_pairs={{0,16},{1,17},{2,18},{3,19},{4,20},{5,21},{6,22},{7,23},{8,24},{9,... | collective-permute-start | bytes 2457608 | tf_op jit(solution)/shard_map/ppermute | solution.py:818
  64.1 30.4 %collective-permute-start.18 = (bf16[128,3200]{1,0:T(8,128)(2,1)S(1)}, bf16[128,3200]{1,0:T(8,128)(2,1)}, u32[]{:S(2)}, u32[]{:S(2)}) collective-permute-start(bf16[128,3200]{1,0:T(8,128)(2,1)S(1)} %constant_dynamic-update-slice_fusion.refs_1_), channel_id=1, source_target_pairs={{0,24},{1,25},{2,26},{3,27},{4,28},{5,29},{6,30},{7,31},{8,16},{9,... | collective-permute-start | bytes 2457608 | tf_op jit(solution)/shard_map/ppermute | solution.py:818
  95.6 67.0 %collective-permute-start.33 = (bf16[128,6656]{1,0:T(8,128)(2,1)}, bf16[128,6656]{1,0:T(8,128)(2,1)}, u32[]{:S(2)}, u32[]{:S(2)}) collective-permute-start(bf16[128,6656]{1,0:T(8,128)(2,1)} %constant_dynamic-update-slice_fusion.4.refs_1_), channel_id=1, source_target_pairs={{0,8},{1,9},{2,10},{3,11},{4,12},{5,13},{6,14},{7,15},{8,0},{9,1},... | collective-permute-start | bytes 5111816 | tf_op jit(solution)/shard_map/ppermute | solution.py:818
  98.2 64.5 %collective-permute-start.34 = (bf16[128,6656]{1,0:T(8,128)(2,1)}, bf16[128,6656]{1,0:T(8,128)(2,1)}, u32[]{:S(2)}, u32[]{:S(2)}) collective-permute-start(bf16[128,6656]{1,0:T(8,128)(2,1)} %constant_dynamic-update-slice_fusion.4.refs_1_), channel_id=1, source_target_pairs={{0,16},{1,17},{2,18},{3,19},{4,20},{5,21},{6,22},{7,23},{8,24},{9,... | collective-permute-start | bytes 5111816 | tf_op jit(solution)/shard_map/ppermute | solution.py:818
  111.6 36.0 %collective-permute-start.31 = (bf16[128,1024]{1,0:T(8,128)(2,1)S(1)}, bf16[128,1024]{1,0:T(8,128)(2,1)S(1)}, u32[]{:S(2)}, u32[]{:S(2)}) collective-permute-start(bf16[128,1024]{1,0:T(8,128)(2,1)S(1)} %copy-done.116), channel_id=1, source_target_pairs={{0,4},{1,5},{2,0},{3,1},{4,6},{5,7},{6,2},{7,3},{8,12},{9,13},{10,... | collective-permute-start | bytes 786440 | tf_op jit(solution)/shard_map/ppermute | solution.py:818
  224.3 33.5 %collective-permute-start.49 = (bf16[352,1024]{1,0:T(8,128)(2,1)}, bf16[352,1024]{1,0:T(8,128)(2,1)S(1)}, u32[]{:S(2)}, u32[]{:S(2)}) collective-permute-start(bf16[352,1024]{1,0:T(8,128)(2,1)} %pad_maximum_fusion.7.refs_1_), channel_id=1, source_target_pairs={{0,8},{1,9},{2,10},{3,11},{4,12},{5,13},{6,14},{7,15},{8,0},{9,1},... | collective-permute-start | bytes 2162696 | tf_op jit(solution)/shard_map/ppermute | solution.py:818
  229.5 33.6 %collective-permute-start.50 = (bf16[352,1024]{1,0:T(8,128)(2,1)}, bf16[352,1024]{1,0:T(8,128)(2,1)S(1)}, u32[]{:S(2)}, u32[]{:S(2)}) collective-permute-start(bf16[352,1024]{1,0:T(8,128)(2,1)} %pad_maximum_fusion.7.refs_1_), channel_id=1, source_target_pairs={{0,16},{1,17},{2,18},{3,19},{4,20},{5,21},{6,22},{7,23},{8,24},{9,... | collective-permute-start | bytes 2162696 | tf_op jit(solution)/shard_map/ppermute | solution.py:818
  280.8 57.4 %collective-permute-start.60 = (bf16[4,352,1024]{2,1,0:T(8,128)(2,1)}, bf16[4,352,1024]{2,1,0:T(8,128)(2,1)}, u32[]{:S(2)}, u32[]{:S(2)}) collective-permute-start(bf16[4,352,1024]{2,1,0:T(8,128)(2,1)} %dynamic-slice_bitcast_fusion), channel_id=1, source_target_pairs={{0,4},{1,5},{2,6},{3,7},{4,0},{5,1},{6,2},{7,3},{8,12},{9,13},{10,... | collective-permute-start | bytes 8650760 | tf_op jit(solution)/shard_map/ppermute | solution.py:818
  311.6 46.5 %collective-permute-start.65 = (bf16[512,2816]{1,0:T(8,128)(2,1)}, bf16[512,2816]{1,0:T(8,128)(2,1)}, u32[]{:S(2)}, u32[]{:S(2)}) collective-permute-start(bf16[512,2816]{1,0:T(8,128)(2,1)} %convolution_convert_fusion.2), channel_id=1, source_target_pairs={{0,4},{1,5},{2,6},{3,7},{4,0},{5,1},{6,2},{7,3},{8,12},{9,13},{10,... | collective-permute-start | bytes 8650760 | tf_op jit(solution)/shard_map/ppermute | solution.py:818
  315.2 47.5 %collective-permute-start.64 = (bf16[512,2816]{1,0:T(8,128)(2,1)}, bf16[512,2816]{1,0:T(8,128)(2,1)}, u32[]{:S(2)}, u32[]{:S(2)}) collective-permute-start(bf16[512,2816]{1,0:T(8,128)(2,1)} %convolution_convert_fusion.1), channel_id=1, source_target_pairs={{0,4},{1,5},{2,6},{3,7},{4,0},{5,1},{6,2},{7,3},{8,12},{9,13},{10,... | collective-permute-start | bytes 8650760 | tf_op jit(solution)/shard_map/ppermute | solution.py:818
  344.6 33.3 %collective-permute-start.67 = (bf16[352,1024]{1,0:T(8,128)(2,1)S(1)}, bf16[352,1024]{1,0:T(8,128)(2,1)S(1)}, u32[]{:S(2)}, u32[]{:S(2)}) collective-permute-start(bf16[352,1024]{1,0:T(8,128)(2,1)S(1)} %get-tuple-element.377.refs_18_), channel_id=1, source_target_pairs={{0,16},{1,17},{2,18},{3,19},{4,20},{5,21},{6,22},{7,23},{8,24},{9,... | collective-permute-start | bytes 2162696 | tf_op jit(solution)/shard_map/ppermute | solution.py:818
  344.7 33.3 %collective-permute-start.68 = (bf16[352,1024]{1,0:T(8,128)(2,1)S(1)}, bf16[352,1024]{1,0:T(8,128)(2,1)S(1)}, u32[]{:S(2)}, u32[]{:S(2)}) collective-permute-start(bf16[352,1024]{1,0:T(8,128)(2,1)S(1)} %get-tuple-element.376.refs_19_), channel_id=1, source_target_pairs={{0,24},{1,25},{2,26},{3,27},{4,28},{5,29},{6,30},{7,31},{8,16},{9,... | collective-permute-start | bytes 2162696 | tf_op jit(solution)/shard_map/ppermute | solution.py:818
  358.1 37.3 %collective-permute-start.61 = (bf16[512,384]{1,0:T(8,128)(2,1)S(1)}, bf16[512,384]{1,0:T(8,128)(2,1)S(1)}, u32[]{:S(2)}, u32[]{:S(2)}) collective-permute-start(bf16[512,384]{1,0:T(8,128)(2,1)S(1)} %get-tuple-element.286), channel_id=1, source_target_pairs={{0,1},{1,0},{2,3},{3,2},{4,5},{5,4},{6,7},{7,6},{8,9},{9,8},{10,11... | collective-permute-start | bytes 1179656 | tf_op jit(solution)/shard_map/ppermute | solution.py:818
  362.7 34.4 %collective-permute-start.62 = (bf16[512,384]{1,0:T(8,128)(2,1)S(1)}, bf16[512,384]{1,0:T(8,128)(2,1)S(1)}, u32[]{:S(2)}, u32[]{:S(2)}) collective-permute-start(bf16[512,384]{1,0:T(8,128)(2,1)S(1)} %get-tuple-element.287), channel_id=1, source_target_pairs={{0,4},{1,5},{2,6},{3,7},{4,0},{5,1},{6,2},{7,3},{8,12},{9,13},{10,... | collective-permute-start | bytes 1179656 | tf_op jit(solution)/shard_map/ppermute | solution.py:818
  365.3 31.8 %collective-permute-start.63 = (bf16[512,384]{1,0:T(8,128)(2,1)S(1)}, bf16[512,384]{1,0:T(8,128)(2,1)S(1)}, u32[]{:S(2)}, u32[]{:S(2)}) collective-permute-start(bf16[512,384]{1,0:T(8,128)(2,1)S(1)} %get-tuple-element.288), channel_id=1, source_target_pairs={{0,5},{1,4},{2,7},{3,6},{4,1},{5,0},{6,3},{7,2},{8,13},{9,12},{10,... | collective-permute-start | bytes 1179656 | tf_op jit(solution)/shard_map/ppermute | solution.py:818
  399.5 30.6 %collective-permute-start.75 = (bf16[512,1536]{1,0:T(8,128)(2,1)}, bf16[512,1536]{1,0:T(8,128)(2,1)}, u32[]{:S(2)}, u32[]{:S(2)}) collective-permute-start(bf16[512,1536]{1,0:T(8,128)(2,1)} %convolution_convert_fusion.4), channel_id=1, source_target_pairs={{0,4},{1,5},{2,6},{3,7},{4,0},{5,1},{6,2},{7,3},{8,12},{9,13},{10,... | collective-permute-start | bytes 4718600 | tf_op jit(solution)/shard_map/ppermute | solution.py:818
  427.2 32.7 %collective-permute-start.73 = (bf16[128,2816]{1,0:T(8,128)(2,1)S(1)}, bf16[128,2816]{1,0:T(8,128)(2,1)S(1)}, u32[]{:S(2)}, u32[]{:S(2)}) collective-permute-start(bf16[128,2816]{1,0:T(8,128)(2,1)S(1)} %get-tuple-element.368), channel_id=1, source_target_pairs={{0,16},{1,17},{2,18},{3,19},{4,20},{5,21},{6,22},{7,23},{8,24},{9,... | collective-permute-start | bytes 2162696 | tf_op jit(solution)/shard_map/ppermute | solution.py:818
  428.7 33.0 %collective-permute-start.74 = (bf16[128,2816]{1,0:T(8,128)(2,1)S(1)}, bf16[128,2816]{1,0:T(8,128)(2,1)S(1)}, u32[]{:S(2)}, u32[]{:S(2)}) collective-permute-start(bf16[128,2816]{1,0:T(8,128)(2,1)S(1)} %get-tuple-element.367), channel_id=1, source_target_pairs={{0,24},{1,25},{2,26},{3,27},{4,28},{5,29},{6,30},{7,31},{8,16},{9,... | collective-permute-start | bytes 2162696 | tf_op jit(solution)/shard_map/ppermute | solution.py:818
  435.0 34.5 %collective-permute-start.94 = (bf16[88,1024]{1,0:T(8,128)(2,1)S(1)}, bf16[88,1024]{1,0:T(8,128)(2,1)S(1)}, u32[]{:S(2)}, u32[]{:S(2)}) collective-permute-start(bf16[88,1024]{1,0:T(8,128)(2,1)S(1)} %get-tuple-element.418), channel_id=1, source_target_pairs={{0,1},{1,2},{2,3},{3,0},{4,5},{5,6},{6,7},{7,4},{8,9},{9,10},{10,1... | collective-permute-start | bytes 540680 | tf_op jit(solution)/shard_map/ppermute | solution.py:818
  438.5 32.7 %collective-permute-start.95 = (bf16[88,1024]{1,0:T(8,128)(2,1)S(1)}, bf16[88,1024]{1,0:T(8,128)(2,1)S(1)}, u32[]{:S(2)}, u32[]{:S(2)}) collective-permute-start(bf16[88,1024]{1,0:T(8,128)(2,1)S(1)} %get-tuple-element.420), channel_id=1, source_target_pairs={{0,2},{1,3},{2,0},{3,1},{4,6},{5,7},{6,4},{7,5},{8,10},{9,11},{10,... | collective-permute-start | bytes 540680 | tf_op jit(solution)/shard_map/ppermute | solution.py:818
  469.5 32.0 %collective-permute-start.82 = (bf16[128,4096]{1,0:T(8,128)(2,1)S(1)}, bf16[128,4096]{1,0:T(8,128)(2,1)S(1)}, u32[]{:S(2)}, u32[]{:S(2)}) collective-permute-start(bf16[128,4096]{1,0:T(8,128)(2,1)S(1)} %get-tuple-element.365), channel_id=1, source_target_pairs={{0,8},{1,9},{2,10},{3,11},{4,12},{5,13},{6,14},{7,15},{8,0},{9,1},... | collective-permute-start | bytes 3145736 | tf_op jit(solution)/shard_map/ppermute | solution.py:818
  471.2 45.8 %collective-permute-start.83 = (bf16[128,4096]{1,0:T(8,128)(2,1)S(1)}, bf16[128,4096]{1,0:T(8,128)(2,1)S(1)}, u32[]{:S(2)}, u32[]{:S(2)}) collective-permute-start(bf16[128,4096]{1,0:T(8,128)(2,1)S(1)} %get-tuple-element.364), channel_id=1, source_target_pairs={{0,16},{1,17},{2,18},{3,19},{4,20},{5,21},{6,22},{7,23},{8,24},{9,... | collective-permute-start | bytes 3145736 | tf_op jit(solution)/shard_map/ppermute | solution.py:818
  471.5 45.6 %collective-permute-start.84 = (bf16[128,4096]{1,0:T(8,128)(2,1)S(1)}, bf16[128,4096]{1,0:T(8,128)(2,1)S(1)}, u32[]{:S(2)}, u32[]{:S(2)}) collective-permute-start(bf16[128,4096]{1,0:T(8,128)(2,1)S(1)} %get-tuple-element.363), channel_id=1, source_target_pairs={{0,24},{1,25},{2,26},{3,27},{4,28},{5,29},{6,30},{7,31},{8,16},{9,... | collective-permute-start | bytes 3145736 | tf_op jit(solution)/shard_map/ppermute | solution.py:818
  (215 other events, 2326.1 us)

commit v4 on v3

--- a/solution.py
+++ b/solution.py
@@ -570,7 +570,7 @@
     dval[...] = jnp.zeros_like(dval)
 
     def tile(index, carry):
-        rows = pl.ds(pl.multiple_of(index * rows_q, rows_q), rows_q)
+        rows = pl.ds(index * rows_q, rows_q)
         query = qr_ref[rows, :]
         d_out = datt[rows, :]
         delta = jnp.sum(
@@ -600,10 +600,11 @@
             dqr[...] += dot_tn(d_scores, keys)
 
         def earlier(block, inner):
-            local(pl.ds(pl.multiple_of(block * rows_q, rows_q), rows_q), False)
+            local(pl.ds(block * rows_q, rows_q), False)
             return inner
 
-        lax.fori_loop(0, index, earlier, 0)
+        for block in range(index):
+            earlier(block, 0)
         local(rows, True)
 
         @pl.when(flag > 0)
@@ -617,7 +618,8 @@
         grads[rows, :HEAD_DIM] = ((unrotate(dqr[...], index) + dqm[...]) * scale).astype(low)
         return carry
 
-    lax.fori_loop(0, tiles, tile, 0)
+    for index in range(tiles):
+        tile(index, 0)
     for index in range(tiles):
         rows = pl.ds(index * rows_q, rows_q)
         grads[rows, HEAD_DIM : 2 * HEAD_DIM] = (unrotate(dkey[rows, :], index) * scale).astype(low)

time: 560 us -> 559 us (level)
  Pallas kernels: 60.3 us -> 75.6 us
  starting transfers between devices: 162 us -> 149 us
    ppermute x97, starting transfers between devices: 162 us -> 149 us  [move(): return lax.ppermute(array, LINE, routes[name])]
    pallas_call x2, Pallas kernels: 20.2 us -> 28.3 us  [attend(): pl.pallas_call(functools.partial(attend_kernel, head, len(given), len(fir...]
    pallas_call x2, Pallas kernels: 24.9 us -> 32.1 us  [attend_back(): pl.pallas_call(functools.partial(attend_back_kernel, head, len(given), le...]
  transfers between devices with their start and end apart: 97 -> 97, of which waited for: 31 -> 32; matrix products, arithmetic and copies ran while one was open for 22% -> 22% of each run, Pallas kernels for 11% -> 14%
where the time goes in v4:
time: 559 us; the launch traced here: 549 us
  waiting for transfers between devices  168 us (30%)
  starting transfers between devices  149 us (27%)
  Pallas kernels  75.6 us (14%)
  matrix products  63.6 us (11%)
  local copies, waits for them, and re-layouts  46.2 us (8%)
  other arithmetic  42.3 us (8%)
    ppermute x97, waiting for transfers between devices, move(): return lax.ppermute(array, LINE, routes[name])  168 us
    ppermute x97, starting transfers between devices, move(): return lax.ppermute(array, LINE, routes[name])  149 us
    pallas_call x2, Pallas kernels, attend_back(): pl.pallas_call(functools.partial(attend_back_kernel, head, len(given), le...  32.1 us
    unnamed x290, local copies, waits for them, and re-layouts  29.4 us
    pallas_call x2, Pallas kernels, attend(): pl.pallas_call(functools.partial(attend_kernel, head, len(given), len(fir...  28.3 us
    dot_general x6, matrix products, dot_nt(): return lax.dot_general(left, right, (((1,), (1,)), ((), ())), **MXU)  23.4 us
    dot_general x11, matrix products, dot_tn(): return lax.dot_general(left, right, (((0,), (0,)), ((), ())), **MXU)  22 us
    dot_general x6, matrix products, dot_nn(): return jnp.dot(left, right, **MXU)  18.2 us
  transfers between devices with their start and end apart: 97, of which 32 were waited for; matrix products, arithmetic and copies ran while one was open for 22% of the time, Pallas kernels for 14%

profile of v4, /device:TPU:0, one launch (start us, length us, event | category | flops | bytes accessed | tf_op | source)
XLA Modules:
  0.0 549.2 jit_solution(3433602762808423232)
XLA Ops:
  36.1 5.6 %collective-permute-start.7 = (bf16[32,6656]{1,0:T(8,128)(2,1)S(1)}, bf16[32,6656]{1,0:T(8,128)(2,1)S(1)}, u32[]{:S(2)}, u32[]{:S(2)}) collective-permute-start(bf16[32,6656]{1,0:T(8,128)(2,1)S(1)} %pad_maximum_fusion.13), channel_id=1, source_target_pairs={{0,1},{1,2},{2,3},{3,0},{4,5},{5,6},{6,7},{7,4},{8,9},{9,10},{10,1... | collective-permute-start | bytes 1277960 | tf_op jit(solution)/shard_map/ppermute | solution.py:820
  47.1 9.5 %collective-permute-start.9 = (bf16[32,6656]{1,0:T(8,128)(2,1)S(1)}, bf16[32,6656]{1,0:T(8,128)(2,1)S(1)}, u32[]{:S(2)}, u32[]{:S(2)}) collective-permute-start(bf16[32,6656]{1,0:T(8,128)(2,1)S(1)} %pad_maximum_fusion.13), channel_id=1, source_target_pairs={{0,3},{1,0},{2,1},{3,2},{4,7},{5,4},{6,5},{7,6},{8,11},{9,8},{10,9... | collective-permute-start | bytes 1277960 | tf_op jit(solution)/shard_map/ppermute | solution.py:820
  64.7 7.8 %collective-permute-done.8 = bf16[32,6656]{1,0:T(8,128)(2,1)S(1)} collective-permute-done((bf16[32,6656]{1,0:T(8,128)(2,1)S(1)}, bf16[32,6656]{1,0:T(8,128)(2,1)S(1)}, u32[]{:S(2)}, u32[]{:S(2)}) %collective-permute-start.8) | collective-permute-done | bytes 426016 | tf_op jit(solution)/shard_map/ppermute | solution.py:820
  79.5 15.0 %collective-permute-done.17.refs_3_ = bf16[128,3200]{1,0:T(8,128)(2,1)} collective-permute-done((bf16[128,3200]{1,0:T(8,128)(2,1)S(1)}, bf16[128,3200]{1,0:T(8,128)(2,1)}, u32[]{:S(2)}, u32[]{:S(2)}) %collective-permute-start.17) | collective-permute-done | bytes 819232 | tf_op jit(solution)/shard_map/ppermute | solution.py:820
  111.6 16.6 %collective-permute-start.31 = (bf16[128,1024]{1,0:T(8,128)(2,1)S(1)}, bf16[128,1024]{1,0:T(8,128)(2,1)S(1)}, u32[]{:S(2)}, u32[]{:S(2)}) collective-permute-start(bf16[128,1024]{1,0:T(8,128)(2,1)S(1)} %copy-done.116), channel_id=1, source_target_pairs={{0,4},{1,5},{2,0},{3,1},{4,6},{5,7},{6,2},{7,3},{8,12},{9,13},{10,... | collective-permute-start | bytes 786440 | tf_op jit(solution)/shard_map/ppermute | solution.py:820
  128.2 9.3 %collective-permute-start.32 = (bf16[128,1024]{1,0:T(8,128)(2,1)S(1)}, bf16[128,1024]{1,0:T(8,128)(2,1)S(1)}, u32[]{:S(2)}, u32[]{:S(2)}) collective-permute-start(bf16[128,1024]{1,0:T(8,128)(2,1)S(1)} %copy-done.115), channel_id=1, source_target_pairs={{0,5},{1,4},{2,1},{3,0},{4,7},{5,6},{6,3},{7,2},{8,13},{9,12},{10,... | collective-permute-start | bytes 786440 | tf_op jit(solution)/shard_map/ppermute | solution.py:820
  149.7 12.0 %collective-permute-done.26.refs_2_ = bf16[512,384]{1,0:T(8,128)(2,1)S(1)} collective-permute-done((bf16[512,384]{1,0:T(8,128)(2,1)S(1)}, bf16[512,384]{1,0:T(8,128)(2,1)S(1)}, u32[]{:S(2)}, u32[]{:S(2)}) %collective-permute-start.26) | collective-permute-done | bytes 393248 | tf_op jit(solution)/shard_map/ppermute | solution.py:820
  166.8 13.6 %attend.2 = (bf16[2048,128]{1,0:T(8,128)(2,1)S(1)}, bf16[2048,128]{1,0:T(8,128)(2,1)S(1)}, bf16[2048,128]{1,0:T(8,128)(2,1)S(1)}, bf16[2048,128]{1,0:T(8,128)(2,...) custom-call(s32[2]{0:T(128)S(1)} %pad_add_fusion.2.refs_0_, ...), custom_call_target="tpu_custom_call" | custom-call | flops 1 | bytes 1 | tf_op jit(solution)/shard_map/attend/pallas_call | solution.py:526
  195.7 14.7 %attend.3 = (bf16[2048,128]{1,0:T(8,128)(2,1)S(1)}, bf16[2048,128]{1,0:T(8,128)(2,1)S(1)}, bf16[2048,128]{1,0:T(8,128)(2,1)S(1)}, bf16[2048,128]{1,0:T(8,128)(2,...) custom-call(s32[2]{0:T(128)S(1)} %pad_add_fusion.2.refs_0_, ...), custom_call_target="tpu_custom_call" | custom-call | flops 1 | bytes 1 | tf_op jit(solution)/shard_map/attend/pallas_call | solution.py:526
  234.4 5.4 settle.4
  250.3 5.9 %multiply_convert_fusion.2 = (bf16[512,2816]{1,0:T(8,128)(2,1)}, f32[512,2816]{1,0:T(8,128)}) fusion(f32[512,2816]{1,0:T(8,128)S(1)} %fusion.55, bf16[512,1024]{1,0:T(8,128)(2,1)S(1)} %multiply_convert_fusion.3, bf16[1024,2816]{1,0:T(8,128)(2,1)S(1)} %get-tuple-element.255), kind=kOutput, calls=%fused_computation.6 | convolution fusion | flops 2961440768 | bytes 21233664 | tf_op jit(solution)/shard_map/dot_general | solution.py:389
  263.1 10.7 %collective-permute-start.52 = (bf16[352,1024]{1,0:T(8,128)(2,1)}, bf16[352,1024]{1,0:T(8,128)(2,1)S(1)}, u32[]{:S(2)}, u32[]{:S(2)}) collective-permute-start(bf16[352,1024]{1,0:T(8,128)(2,1)} %pad_maximum_fusion.7.refs_1_), channel_id=1, source_target_pairs={{0,4},{1,5},{2,6},{3,7},{4,0},{5,1},{6,2},{7,3},{8,12},{9,13},{10,... | collective-permute-start | bytes 2162696 | tf_op jit(solution)/shard_map/ppermute | solution.py:820
  290.3 9.8 %multiply_convert_fusion.1 = (bf16[512,2816]{1,0:T(8,128)(2,1)}, bf16[512,2816]{1,0:T(8,128)(2,1)}) fusion(f32[512,2816]{1,0:T(8,128)} %copy-done.137, f32[512,2816]{1,0:T(8,128)} %get-tuple-element.458, bf16[512,1024]{1,0:T(8,128)(2,1)S(1)} %broadcast_select_fusion.1, bf16[2816,1024]{1,0:T(8,128)(2,1)S(1)} %settle.5), kind=kOutput, calls=%fused_computation.5 | convolution fusion | flops 2971533312 | bytes 24117248 | tf_op jit(solution)/shard_map/dot_general | solution.py:381
  300.1 5.1 fusion.56
  333.0 5.1 collective-permute-done.59.refs_10_
  346.2 15.4 %attend_back.2 = (bf16[512,384]{1,0:T(8,128)(2,1)S(1)}, bf16[512,384]{1,0:T(8,128)(2,1)S(1)}, bf16[512,384]{1,0:T(8,128)(2,1)S(1)}, bf16[512,384]{1,0:T(8,128)(2,1)S(1)}) custom-call(s32[2]{0:T(128)S(1)} %pad_add_fusion.2.refs_0_, bf16[2048,128]{1,0:T(8,128)(2,1)S(1)} %copy-done.27, bf16[2048,128]{1,0:T(8,128)(2,1)S(1)} %copy-done.29, ...), custom_call_target="tpu_custom_call" | custom-call | flops 1 | bytes 1 | tf_op jit(solution)/shard_map/attend_back/pallas_call | solution.py:637
  369.0 7.9 %collective-permute-done.67.refs_19_ = bf16[352,1024]{1,0:T(8,128)(2,1)S(1)} collective-permute-done((bf16[352,1024]{1,0:T(8,128)(2,1)S(1)}, bf16[352,1024]{1,0:T(8,128)(2,1)S(1)}, u32[]{:S(2)}, u32[]{:S(2)}) %collective-permute-start.67) | collective-permute-done | bytes 720928 | tf_op jit(solution)/shard_map/ppermute | solution.py:820
  382.4 16.7 %attend_back.3 = (bf16[512,384]{1,0:T(8,128)(2,1)S(1)}, bf16[512,384]{1,0:T(8,128)(2,1)}, bf16[512,384]{1,0:T(8,128)(2,1)}, bf16[512,384]{1,0:T(8,128)(2,1)}) custom-call(s32[2]{0:T(128)S(1)} %pad_add_fusion.2.refs_0_, bf16[2048,128]{1,0:T(8,128)(2,1)S(1)} %copy-done.35, bf16[2048,128]{1,0:T(8,128)(2,1)S(1)} %copy-done.37, bf16[2048,128]{1,0:T(8,128)(2,1)S(1)} %copy-done.39, ...), custom_call_target="tpu_custom_call" | custom-call | flops 1 | bytes 1 | tf_op jit(solution)/shard_map/attend_back/pallas_call | solution.py:637
  405.7 10.9 %collective-permute-done.71 = bf16[128,2816]{1,0:T(8,128)(2,1)} collective-permute-done((bf16[128,2816]{1,0:T(8,128)(2,1)}, bf16[128,2816]{1,0:T(8,128)(2,1)}, u32[]{:S(2)}, u32[]{:S(2)}) %collective-permute-start.71) | collective-permute-done | bytes 720928 | tf_op jit(solution)/shard_map/ppermute | solution.py:820
  416.7 5.0 collective-permute-done.78.refs_4_
  447.0 12.3 %collective-permute-done.73 = bf16[128,2816]{1,0:T(8,128)(2,1)S(1)} collective-permute-done((bf16[128,2816]{1,0:T(8,128)(2,1)S(1)}, bf16[128,2816]{1,0:T(8,128)(2,1)S(1)}, u32[]{:S(2)}, u32[]{:S(2)}) %collective-permute-start.73) | collective-permute-done | bytes 720928 | tf_op jit(solution)/shard_map/ppermute | solution.py:820
  475.9 6.1 %collective-permute-done.92 = bf16[32,2816]{1,0:T(8,128)(2,1)S(1)} collective-permute-done((bf16[32,2816]{1,0:T(8,128)(2,1)S(1)}, bf16[32,2816]{1,0:T(8,128)(2,1)S(1)}, u32[]{:S(2)}, u32[]{:S(2)}) %collective-permute-start.92) | collective-permute-done | bytes 180256 | tf_op jit(solution)/shard_map/ppermute | solution.py:820
  501.1 14.7 %collective-permute-done.83 = bf16[128,4096]{1,0:T(8,128)(2,1)S(1)} collective-permute-done((bf16[128,4096]{1,0:T(8,128)(2,1)S(1)}, bf16[128,4096]{1,0:T(8,128)(2,1)S(1)}, u32[]{:S(2)}, u32[]{:S(2)}) %collective-permute-start.83) | collective-permute-done | bytes 1048608 | tf_op jit(solution)/shard_map/ppermute | solution.py:820
  527.7 17.9 %collective-permute-done.86 = bf16[32,4096]{1,0:T(8,128)(2,1)S(1)} collective-permute-done((bf16[32,4096]{1,0:T(8,128)(2,1)S(1)}, bf16[32,4096]{1,0:T(8,128)(2,1)S(1)}, u32[]{:S(2)}, u32[]{:S(2)}) %collective-permute-start.86) | collective-permute-done | bytes 262176 | tf_op jit(solution)/shard_map/ppermute | solution.py:820
  (587 shorter events, 290.5 us)
Async XLA Ops:
  26.4 30.3 %collective-permute-start.12 = (s32[512]{0:T(512)S(1)}, s32[512]{0:T(512)S(1)}, u32[]{:S(2)}, u32[]{:S(2)}) collective-permute-start(s32[512]{0:T(512)S(1)} %bitcast.172), channel_id=1, source_target_pairs={{0,4},{1,5},{2,0},{3,1},{4,6},{5,7},{6,2},{7,3},{8,12},{9,13},{10,... | collective-permute-start | bytes 6152 | tf_op jit(solution)/shard_map/ppermute | solution.py:820
  58.2 36.4 %collective-permute-start.17 = (bf16[128,3200]{1,0:T(8,128)(2,1)S(1)}, bf16[128,3200]{1,0:T(8,128)(2,1)}, u32[]{:S(2)}, u32[]{:S(2)}) collective-permute-start(bf16[128,3200]{1,0:T(8,128)(2,1)S(1)} %constant_dynamic-update-slice_fusion.refs_1_), channel_id=1, source_target_pairs={{0,16},{1,17},{2,18},{3,19},{4,20},{5,21},{6,22},{7,23},{8,24},{9,... | collective-permute-start | bytes 2457608 | tf_op jit(solution)/shard_map/ppermute | solution.py:820
  64.1 30.4 %collective-permute-start.18 = (bf16[128,3200]{1,0:T(8,128)(2,1)S(1)}, bf16[128,3200]{1,0:T(8,128)(2,1)}, u32[]{:S(2)}, u32[]{:S(2)}) collective-permute-start(bf16[128,3200]{1,0:T(8,128)(2,1)S(1)} %constant_dynamic-update-slice_fusion.refs_1_), channel_id=1, source_target_pairs={{0,24},{1,25},{2,26},{3,27},{4,28},{5,29},{6,30},{7,31},{8,16},{9,... | collective-permute-start | bytes 2457608 | tf_op jit(solution)/shard_map/ppermute | solution.py:820
  95.6 67.0 %collective-permute-start.33 = (bf16[128,6656]{1,0:T(8,128)(2,1)}, bf16[128,6656]{1,0:T(8,128)(2,1)}, u32[]{:S(2)}, u32[]{:S(2)}) collective-permute-start(bf16[128,6656]{1,0:T(8,128)(2,1)} %constant_dynamic-update-slice_fusion.4.refs_1_), channel_id=1, source_target_pairs={{0,8},{1,9},{2,10},{3,11},{4,12},{5,13},{6,14},{7,15},{8,0},{9,1},... | collective-permute-start | bytes 5111816 | tf_op jit(solution)/shard_map/ppermute | solution.py:820
  98.2 64.5 %collective-permute-start.34 = (bf16[128,6656]{1,0:T(8,128)(2,1)}, bf16[128,6656]{1,0:T(8,128)(2,1)}, u32[]{:S(2)}, u32[]{:S(2)}) collective-permute-start(bf16[128,6656]{1,0:T(8,128)(2,1)} %constant_dynamic-update-slice_fusion.4.refs_1_), channel_id=1, source_target_pairs={{0,16},{1,17},{2,18},{3,19},{4,20},{5,21},{6,22},{7,23},{8,24},{9,... | collective-permute-start | bytes 5111816 | tf_op jit(solution)/shard_map/ppermute | solution.py:820
  111.6 36.2 %collective-permute-start.31 = (bf16[128,1024]{1,0:T(8,128)(2,1)S(1)}, bf16[128,1024]{1,0:T(8,128)(2,1)S(1)}, u32[]{:S(2)}, u32[]{:S(2)}) collective-permute-start(bf16[128,1024]{1,0:T(8,128)(2,1)S(1)} %copy-done.116), channel_id=1, source_target_pairs={{0,4},{1,5},{2,0},{3,1},{4,6},{5,7},{6,2},{7,3},{8,12},{9,13},{10,... | collective-permute-start | bytes 786440 | tf_op jit(solution)/shard_map/ppermute | solution.py:820
  162.6 31.3 %collective-permute-start.24 = (bf16[512,384]{1,0:T(8,128)(2,1)}, bf16[512,384]{1,0:T(8,128)(2,1)}, u32[]{:S(2)}, u32[]{:S(2)}) collective-permute-start(bf16[512,384]{1,0:T(8,128)(2,1)} %get-tuple-element.384), channel_id=1, source_target_pairs={{0,4},{1,5},{2,6},{3,7},{4,0},{5,1},{6,2},{7,3},{8,12},{9,13},{10,... | collective-permute-start | bytes 1179656 | tf_op jit(solution)/shard_map/ppermute | solution.py:820
  162.7 31.3 %collective-permute-start.25 = (bf16[512,384]{1,0:T(8,128)(2,1)}, bf16[512,384]{1,0:T(8,128)(2,1)}, u32[]{:S(2)}, u32[]{:S(2)}) collective-permute-start(bf16[512,384]{1,0:T(8,128)(2,1)} %get-tuple-element.383), channel_id=1, source_target_pairs={{0,5},{1,4},{2,7},{3,6},{4,1},{5,0},{6,3},{7,2},{8,13},{9,12},{10,... | collective-permute-start | bytes 1179656 | tf_op jit(solution)/shard_map/ppermute | solution.py:820
  229.5 33.6 %collective-permute-start.50 = (bf16[352,1024]{1,0:T(8,128)(2,1)}, bf16[352,1024]{1,0:T(8,128)(2,1)S(1)}, u32[]{:S(2)}, u32[]{:S(2)}) collective-permute-start(bf16[352,1024]{1,0:T(8,128)(2,1)} %pad_maximum_fusion.7.refs_1_), channel_id=1, source_target_pairs={{0,16},{1,17},{2,18},{3,19},{4,20},{5,21},{6,22},{7,23},{8,24},{9,... | collective-permute-start | bytes 2162696 | tf_op jit(solution)/shard_map/ppermute | solution.py:820
  281.2 56.9 %collective-permute-start.60 = (bf16[4,352,1024]{2,1,0:T(8,128)(2,1)}, bf16[4,352,1024]{2,1,0:T(8,128)(2,1)}, u32[]{:S(2)}, u32[]{:S(2)}) collective-permute-start(bf16[4,352,1024]{2,1,0:T(8,128)(2,1)} %dynamic-slice_bitcast_fusion), channel_id=1, source_target_pairs={{0,4},{1,5},{2,6},{3,7},{4,0},{5,1},{6,2},{7,3},{8,12},{9,13},{10,... | collective-permute-start | bytes 8650760 | tf_op jit(solution)/shard_map/ppermute | solution.py:820
  312.0 49.6 %collective-permute-start.65 = (bf16[512,2816]{1,0:T(8,128)(2,1)}, bf16[512,2816]{1,0:T(8,128)(2,1)}, u32[]{:S(2)}, u32[]{:S(2)}) collective-permute-start(bf16[512,2816]{1,0:T(8,128)(2,1)} %convolution_convert_fusion.2), channel_id=1, source_target_pairs={{0,4},{1,5},{2,6},{3,7},{4,0},{5,1},{6,2},{7,3},{8,12},{9,13},{10,... | collective-permute-start | bytes 8650760 | tf_op jit(solution)/shard_map/ppermute | solution.py:820
  315.6 50.5 %collective-permute-start.64 = (bf16[512,2816]{1,0:T(8,128)(2,1)}, bf16[512,2816]{1,0:T(8,128)(2,1)}, u32[]{:S(2)}, u32[]{:S(2)}) collective-permute-start(bf16[512,2816]{1,0:T(8,128)(2,1)} %convolution_convert_fusion.1), channel_id=1, source_target_pairs={{0,4},{1,5},{2,6},{3,7},{4,0},{5,1},{6,2},{7,3},{8,12},{9,13},{10,... | collective-permute-start | bytes 8650760 | tf_op jit(solution)/shard_map/ppermute | solution.py:820
  344.2 32.7 %collective-permute-start.67 = (bf16[352,1024]{1,0:T(8,128)(2,1)S(1)}, bf16[352,1024]{1,0:T(8,128)(2,1)S(1)}, u32[]{:S(2)}, u32[]{:S(2)}) collective-permute-start(bf16[352,1024]{1,0:T(8,128)(2,1)S(1)} %get-tuple-element.377.refs_18_), channel_id=1, source_target_pairs={{0,16},{1,17},{2,18},{3,19},{4,20},{5,21},{6,22},{7,23},{8,24},{9,... | collective-permute-start | bytes 2162696 | tf_op jit(solution)/shard_map/ppermute | solution.py:820
  346.1 31.6 %collective-permute-start.68 = (bf16[352,1024]{1,0:T(8,128)(2,1)S(1)}, bf16[352,1024]{1,0:T(8,128)(2,1)S(1)}, u32[]{:S(2)}, u32[]{:S(2)}) collective-permute-start(bf16[352,1024]{1,0:T(8,128)(2,1)S(1)} %get-tuple-element.376.refs_19_), channel_id=1, source_target_pairs={{0,24},{1,25},{2,26},{3,27},{4,28},{5,29},{6,30},{7,31},{8,16},{9,... | collective-permute-start | bytes 2162696 | tf_op jit(solution)/shard_map/ppermute | solution.py:820
  361.6 37.5 %collective-permute-start.61 = (bf16[512,384]{1,0:T(8,128)(2,1)S(1)}, bf16[512,384]{1,0:T(8,128)(2,1)S(1)}, u32[]{:S(2)}, u32[]{:S(2)}) collective-permute-start(bf16[512,384]{1,0:T(8,128)(2,1)S(1)} %get-tuple-element.286), channel_id=1, source_target_pairs={{0,1},{1,0},{2,3},{3,2},{4,5},{5,4},{6,7},{7,6},{8,9},{9,8},{10,11... | collective-permute-start | bytes 1179656 | tf_op jit(solution)/shard_map/ppermute | solution.py:820
  366.1 33.1 %collective-permute-start.62 = (bf16[512,384]{1,0:T(8,128)(2,1)S(1)}, bf16[512,384]{1,0:T(8,128)(2,1)S(1)}, u32[]{:S(2)}, u32[]{:S(2)}) collective-permute-start(bf16[512,384]{1,0:T(8,128)(2,1)S(1)} %get-tuple-element.287), channel_id=1, source_target_pairs={{0,4},{1,5},{2,6},{3,7},{4,0},{5,1},{6,2},{7,3},{8,12},{9,13},{10,... | collective-permute-start | bytes 1179656 | tf_op jit(solution)/shard_map/ppermute | solution.py:820
  368.7 30.4 %collective-permute-start.63 = (bf16[512,384]{1,0:T(8,128)(2,1)S(1)}, bf16[512,384]{1,0:T(8,128)(2,1)S(1)}, u32[]{:S(2)}, u32[]{:S(2)}) collective-permute-start(bf16[512,384]{1,0:T(8,128)(2,1)S(1)} %get-tuple-element.288), channel_id=1, source_target_pairs={{0,5},{1,4},{2,7},{3,6},{4,1},{5,0},{6,3},{7,2},{8,13},{9,12},{10,... | collective-permute-start | bytes 1179656 | tf_op jit(solution)/shard_map/ppermute | solution.py:820
  427.6 31.7 %collective-permute-start.73 = (bf16[128,2816]{1,0:T(8,128)(2,1)S(1)}, bf16[128,2816]{1,0:T(8,128)(2,1)S(1)}, u32[]{:S(2)}, u32[]{:S(2)}) collective-permute-start(bf16[128,2816]{1,0:T(8,128)(2,1)S(1)} %get-tuple-element.368), channel_id=1, source_target_pairs={{0,16},{1,17},{2,18},{3,19},{4,20},{5,21},{6,22},{7,23},{8,24},{9,... | collective-permute-start | bytes 2162696 | tf_op jit(solution)/shard_map/ppermute | solution.py:820
  428.5 32.6 %collective-permute-start.74 = (bf16[128,2816]{1,0:T(8,128)(2,1)S(1)}, bf16[128,2816]{1,0:T(8,128)(2,1)S(1)}, u32[]{:S(2)}, u32[]{:S(2)}) collective-permute-start(bf16[128,2816]{1,0:T(8,128)(2,1)S(1)} %get-tuple-element.367), channel_id=1, source_target_pairs={{0,24},{1,25},{2,26},{3,27},{4,28},{5,29},{6,30},{7,31},{8,16},{9,... | collective-permute-start | bytes 2162696 | tf_op jit(solution)/shard_map/ppermute | solution.py:820
  434.4 34.2 %collective-permute-start.94 = (bf16[88,1024]{1,0:T(8,128)(2,1)S(1)}, bf16[88,1024]{1,0:T(8,128)(2,1)S(1)}, u32[]{:S(2)}, u32[]{:S(2)}) collective-permute-start(bf16[88,1024]{1,0:T(8,128)(2,1)S(1)} %get-tuple-element.418), channel_id=1, source_target_pairs={{0,1},{1,2},{2,3},{3,0},{4,5},{5,6},{6,7},{7,4},{8,9},{9,10},{10,1... | collective-permute-start | bytes 540680 | tf_op jit(solution)/shard_map/ppermute | solution.py:820
  437.8 32.2 %collective-permute-start.95 = (bf16[88,1024]{1,0:T(8,128)(2,1)S(1)}, bf16[88,1024]{1,0:T(8,128)(2,1)S(1)}, u32[]{:S(2)}, u32[]{:S(2)}) collective-permute-start(bf16[88,1024]{1,0:T(8,128)(2,1)S(1)} %get-tuple-element.420), channel_id=1, source_target_pairs={{0,2},{1,3},{2,0},{3,1},{4,6},{5,7},{6,4},{7,5},{8,10},{9,11},{10,... | collective-permute-start | bytes 540680 | tf_op jit(solution)/shard_map/ppermute | solution.py:820
  468.6 32.5 %collective-permute-start.82 = (bf16[128,4096]{1,0:T(8,128)(2,1)S(1)}, bf16[128,4096]{1,0:T(8,128)(2,1)S(1)}, u32[]{:S(2)}, u32[]{:S(2)}) collective-permute-start(bf16[128,4096]{1,0:T(8,128)(2,1)S(1)} %get-tuple-element.365), channel_id=1, source_target_pairs={{0,8},{1,9},{2,10},{3,11},{4,12},{5,13},{6,14},{7,15},{8,0},{9,1},... | collective-permute-start | bytes 3145736 | tf_op jit(solution)/shard_map/ppermute | solution.py:820
  470.0 45.8 %collective-permute-start.83 = (bf16[128,4096]{1,0:T(8,128)(2,1)S(1)}, bf16[128,4096]{1,0:T(8,128)(2,1)S(1)}, u32[]{:S(2)}, u32[]{:S(2)}) collective-permute-start(bf16[128,4096]{1,0:T(8,128)(2,1)S(1)} %get-tuple-element.364), channel_id=1, source_target_pairs={{0,16},{1,17},{2,18},{3,19},{4,20},{5,21},{6,22},{7,23},{8,24},{9,... | collective-permute-start | bytes 3145736 | tf_op jit(solution)/shard_map/ppermute | solution.py:820
  471.0 44.9 %collective-permute-start.84 = (bf16[128,4096]{1,0:T(8,128)(2,1)S(1)}, bf16[128,4096]{1,0:T(8,128)(2,1)S(1)}, u32[]{:S(2)}, u32[]{:S(2)}) collective-permute-start(bf16[128,4096]{1,0:T(8,128)(2,1)S(1)} %get-tuple-element.363), channel_id=1, source_target_pairs={{0,24},{1,25},{2,26},{3,27},{4,28},{5,29},{6,30},{7,31},{8,16},{9,... | collective-permute-start | bytes 3145736 | tf_op jit(solution)/shard_map/ppermute | solution.py:820
  (215 other events, 2314.2 us)
